TPU v7x, 32 devices: a whole 2x2x4 slice. The times are simulated.
32 devices in a mesh: gx: 8 (over z, x), gy: 4 (over y, core).
Axes of the slice: x: 2, y: 2, z: 4, core: 2. Of those that a mesh axis runs over, the one named last changes fastest.
Arguments:
- activations: bfloat16 [64, 65536], P('gx', 'gy'), may hold values from -6 to 6
- live_blocks: int32 [4, 8, 512], P(None, 'gx', 'gy'), may hold values 0 or 1
- tile_index: int32 [4, 512, 8], replicated, may hold values from 0 to 511, as said below
- tile_count: int32 [4, 4, 128], P(None, 'gy', 'gx'), may hold values from 1 to 8, as said below
- weight_tiles: bfloat16 [4, 4, 128, 8, 128, 128], P(None, 'gy', 'gx'), may hold values from -0.375 to 0.375
- bias_terms: float32 [4, 4, 128, 128], P(None, 'gy', 'gx'), may hold values from -2 to 2
Outputs:
- final_layer: bfloat16 [64, 65536], P('gx', 'gy')
Inputs may be any that keep to these rules, and one draw needn't show every extreme that they name: The input block of slot t lies in group t mod 4: tile_index[l, j, t] divided by 128, rounded down, equals t mod 4. Of the 16 blocks g * 128 + r * 16 + k (k < 16) held by the device with index r of gx and g of gy, at most one has tile_count above 4 in each layer; in every layer some device has such a block with exactly 8 used slots.
All inputs are finite; a program needn't handle non-finite values. No bound on the sum of `live_blocks` on one device may be relied on, other than what follows from the above.
Results may differ from a plain program's by a relative error of at most 0.0057.
Values may be sent and summed in bfloat16 or wider, within the bound.
No kernel may reach another device: no remote copies, remote signals or barrier semaphores. Data moves between devices by JAX's collectives and lax.ppermute only.
A program may use at most 64 MiB of HBM per device.

v0:
```python
import jax
import jax.numpy as jnp
from jax import lax
from jax.sharding import PartitionSpec as P

LAYERS = 4


def local(activations, live_blocks, tile_index, tile_count, weight_tiles, bias_terms):
    across = lax.axis_size("gx")
    groups = lax.axis_size("gy")
    my_group = lax.axis_index("gy")
    row_count = activations.shape[0]
    tile_side = weight_tiles.shape[-1]
    group_blocks = activations.shape[1] // tile_side
    owned_blocks = weight_tiles.shape[2]
    tile_depth = weight_tiles.shape[3]
    slab_count = tile_depth // groups
    device_count = across * groups
    count_table = lax.all_gather(tile_count, ("gx", "gy"), axis=1, tiled=True)
    current = activations
    for layer_index in range(LAYERS):
        kept_mask = live_blocks[layer_index, 0].astype(jnp.bfloat16)
        blocks = current.reshape(row_count, group_blocks, tile_side) * kept_mask[None, :, None]
        tile_table = tile_index[layer_index].reshape(
            groups, across, owned_blocks, slab_count, groups
        )
        picked = lax.dynamic_index_in_dim(tile_table, my_group, 4, keepdims=False)
        picked_all = jnp.transpose(picked, (1, 0, 2, 3)) - my_group * group_blocks
        chosen = picked_all[:, :, :, 0]
        outgoing = jnp.take(blocks, chosen.reshape(-1), axis=1)
        outgoing = outgoing.reshape(row_count, device_count, owned_blocks, tile_side)
        incoming = lax.all_to_all(outgoing, ("gx", "gy"), split_axis=1, concat_axis=1, tiled=True)
        incoming = incoming.reshape(row_count, across, groups, owned_blocks, tile_side)
        counts = tile_count[layer_index, 0]
        usable = (jnp.arange(tile_depth, dtype=jnp.int32)[None, :] < counts[:, None]).astype(
            jnp.bfloat16
        )
        weights = weight_tiles[layer_index, 0] * usable[:, :, None, None]
        weights = weights.reshape(owned_blocks, slab_count, groups, tile_side, tile_side)
        summed = jnp.einsum(
            "rapki,kpij->rakj", incoming, weights[:, 0], preferred_element_type=jnp.float32
        )
        heavy_all = jnp.argmax(count_table[layer_index], axis=1)
        rest_ids = jnp.take_along_axis(
            picked_all.reshape(device_count, owned_blocks, slab_count),
            heavy_all[:, None, None],
            axis=1,
        )[:, 0, 1:]
        rest_out = jnp.take(blocks, rest_ids.reshape(-1), axis=1).reshape(
            row_count, device_count, slab_count - 1, tile_side
        )
        rest_in = lax.all_to_all(rest_out, ("gx", "gy"), split_axis=1, concat_axis=1, tiled=True)
        rest_in = rest_in.reshape(row_count, across, groups, slab_count - 1, tile_side)
        heavy_here = jnp.argmax(counts)
        rest_weights = lax.dynamic_index_in_dim(weights, heavy_here, 0, keepdims=False)[1:]
        extra = jnp.einsum(
            "rapsi,spij->raj", rest_in, rest_weights, preferred_element_type=jnp.float32
        )
        selector = (jnp.arange(owned_blocks, dtype=jnp.int32) == heavy_here).astype(jnp.float32)
        summed = summed + selector[None, None, :, None] * extra[:, :, None, :]
        shifted = summed + bias_terms[layer_index, 0][None, None]
        result = (
            jax.nn.relu(shifted)
            .astype(jnp.bfloat16)
            .reshape(row_count, across, owned_blocks * tile_side)
        )
        returned = lax.all_to_all(result, "gx", split_axis=1, concat_axis=1, tiled=True)
        current = returned.reshape(row_count, group_blocks * tile_side)
    return current


def solution(mesh):
    placed = (
        P("gx", "gy"),
        P(None, "gx", "gy"),
        P(),
        P(None, "gy", "gx"),
        P(None, "gy", "gx", None, None, None),
        P(None, "gy", "gx", None),
    )
    return jax.shard_map(
        local, mesh=mesh, in_specs=placed, out_specs=P("gx", "gy"), check_vma=False
    )
```

profile of v0, /device:TPU:0, one launch (start us, length us, event | category | flops | bytes accessed | tf_op | source)
XLA Modules:
  0.0 289.5 jit_solution(15461610320700656826)
XLA Ops:
  0.0 43.6 %all_gather.3 = s32[4,32,16]{2,0,1:T(4,128)S(1)} all-gather(s32[4,1,16]{2,0,1:T(4,128)} %bitcast.395), channel_id=1, replica_groups=mesh['gx'=8,'gy'=4] {'gx','gy'}, dimensions={1}, use_global_device_ids=true | all-gather | bytes 8448 | tf_op jit(solution)/shard_map/all_gather | solution.py:20
  45.7 0.8 fusion.42
  48.1 0.7 gather_fusion.1
  49.0 1.1 bitcast_multiply_fusion
  50.7 0.7 select_bitcast_fusion.3
  51.4 2.6 all-to-all-start.1
  54.0 0.7 slice_bitcast_fusion.56
  54.7 1.4 iota_reduce_fusion.7
  56.2 1.8 gather_fusion
  58.3 1.8 broadcast_select_fusion.3
  60.1 1.2 copy.89
  61.4 5.7 %all-to-all-start = ((bf16[8,32,16,128]{3,2,0,1:T(8,128)(2,1)}), bf16[8,32,16,128]{3,2,0,1:T(8,128)(2,1)S(1)}, u32[]{:S(2)}, u32[]{:S(2)}) async-start(bf16[8,32,16,128]{3,2,0,1:T(8,128)(2,1)} %copy.89), calls=%async_computation | async-start | bytes 2097152 | tf_op jit(solution)/shard_map/all_to_all | solution.py:33
  69.5 0.7 gather_fusion.4
  71.1 11.1 %fusion.40 = (bf16[1,1,16,8,128,128]{5,4,3,2,1,0:T(8,128)(2,1)S(1)}, bf16[1,1,16,8,128,128]{5,4,3,2,1,0:T(8,128)(2,1)}, bf16[1,1,16,8,128,128]{5,4,3,2,1,0:T(8,128)(2,1)}, bf16[1,1,16,8,128,128]{5,4,3,2,1,0:T(8,128)(2,1)}) fusion(bf16[4,1,16,8,128,128]{5,4,3,2,1,0:T(8,128)(2,1)} %param.16), kind=kLoop, calls=%fused_computation.161 | loop fusion | bytes 33554432 | tf_op jit(solution)/shard_map/slice | solution.py:39
  82.5 1.9 copy-done.1
  84.7 8.7 %all-to-all-done = bf16[8,32,16,128]{3,2,0,1:T(8,128)(2,1)S(1)} async-done(((bf16[8,32,16,128]{3,2,0,1:T(8,128)(2,1)}), bf16[8,32,16,128]{3,2,0,1:T(8,128)(2,1)S(1)}, u32[]{:S(2)}, u32[]{:S(2)}) %all-to-all-start) | async-done | bytes 1048608 | tf_op jit(solution)/shard_map/all_to_all | solution.py:33
  93.3 3.0 %fusion.23 = bf16[8,8,16,128]{3,1,0,2:T(8,128)(2,1)S(1)} fusion(bf16[16,2,4,128,128]{4,3,2,0,1:T(8,128)(2,1)} %copy-done.1, bf16[8,8,4,16,128]{4,3,0,2,1:T(8,128)(2,1)S(1)} %bitcast.371, f32[16,128]{1,0:T(8,128)S(1)} %get-tuple-element.46, f32[8,8,128]{2,1,0:T(8,128)S(1)} %convolution_bitcast_fusion.3, f32[16]{0:T(128)S(1)} %compare_convert_fusion.7), kind=kOutput, calls=%fused_computation.43 | convolution fusion | flops 134873088 | bytes 3448896 | tf_op jit(solution)/shard_map/rapki,kpij->rakj/dot_general | solution.py:41
  96.5 0.8 reshape.513
  97.3 3.6 %all-to-all-start.2 = ((bf16[8,8,2048]{2,0,1:T(8,128)(2,1)}), bf16[8,8,2048]{2,0,1:T(8,128)(2,1)S(1)}, u32[]{:S(2)}, u32[]{:S(2)}) async-start(bf16[8,8,2048]{2,0,1:T(8,128)(2,1)} %reshape.513), calls=%async_computation.2 | async-start | bytes 524288 | tf_op jit(solution)/shard_map/all_to_all | solution.py:68
  101.0 9.1 %all-to-all-done.2 = bf16[8,8,2048]{2,0,1:T(8,128)(2,1)S(1)} async-done(((bf16[8,8,2048]{2,0,1:T(8,128)(2,1)}), bf16[8,8,2048]{2,0,1:T(8,128)(2,1)S(1)}, u32[]{:S(2)}, u32[]{:S(2)}) %all-to-all-start.2) | async-done | bytes 262176 | tf_op jit(solution)/shard_map/all_to_all | solution.py:68
  110.3 1.8 gather_fusion.3
  112.7 0.7 select_bitcast_fusion.2
  113.5 3.6 %all-to-all-start.4 = ((bf16[8,32,1,128]{3,0,2,1:T(8,128)(2,1)}), bf16[8,32,1,128]{3,0,2,1:T(8,128)(2,1)S(1)}, u32[]{:S(2)}, u32[]{:S(2)}) async-start(bf16[8,32,1,128]{3,0,2,1:T(8,128)(2,1)} %select_bitcast_fusion.2), calls=%async_computation.4 | async-start | bytes 131072 | tf_op jit(solution)/shard_map/all_to_all | solution.py:53
  117.1 1.8 broadcast_select_fusion.2
  118.8 1.3 copy.101
  120.1 4.4 %all-to-all-done.4 = bf16[8,32,1,128]{3,0,2,1:T(8,128)(2,1)S(1)} async-done(((bf16[8,32,1,128]{3,0,2,1:T(8,128)(2,1)}), bf16[8,32,1,128]{3,0,2,1:T(8,128)(2,1)S(1)}, u32[]{:S(2)}, u32[]{:S(2)}) %all-to-all-start.4) | async-done | bytes 65568 | tf_op jit(solution)/shard_map/all_to_all | solution.py:53
  124.5 2.8 all-to-all-start.3
  129.7 0.7 gather_fusion.7
  131.7 2.5 copy_multiply_fusion.1
  134.3 2.0 copy-done.2
  136.4 16.9 %all-to-all-done.3 = bf16[8,32,16,128]{3,2,0,1:T(8,128)(2,1)S(1)} async-done(((bf16[8,32,16,128]{3,2,0,1:T(8,128)(2,1)}), bf16[8,32,16,128]{3,2,0,1:T(8,128)(2,1)S(1)}, u32[]{:S(2)}, u32[]{:S(2)}) %all-to-all-start.3) | async-done | bytes 1048608 | tf_op jit(solution)/shard_map/all_to_all | solution.py:33
  153.3 3.0 %fusion.22 = bf16[8,8,16,128]{3,1,0,2:T(8,128)(2,1)S(1)} fusion(bf16[16,2,4,128,128]{4,3,2,0,1:T(8,128)(2,1)} %copy-done.2, bf16[8,8,4,16,128]{4,3,0,2,1:T(8,128)(2,1)S(1)} %bitcast.370, f32[16,128]{1,0:T(8,128)S(1)} %get-tuple-element.45, f32[8,8,128]{2,1,0:T(8,128)S(1)} %convolution_bitcast_fusion.2, f32[16]{0:T(128)S(1)} %compare_convert_fusion.6), kind=kOutput, calls=%fused_computation.42 | convolution fusion | flops 134873088 | bytes 3448896 | tf_op jit(solution)/shard_map/rapki,kpij->rakj/dot_general | solution.py:41
  156.5 0.8 reshape.514
  157.3 3.5 %all-to-all-start.5 = ((bf16[8,8,2048]{2,0,1:T(8,128)(2,1)}), bf16[8,8,2048]{2,0,1:T(8,128)(2,1)S(1)}, u32[]{:S(2)}, u32[]{:S(2)}) async-start(bf16[8,8,2048]{2,0,1:T(8,128)(2,1)} %reshape.514), calls=%async_computation.5 | async-start | bytes 524288 | tf_op jit(solution)/shard_map/all_to_all | solution.py:68
  161.0 9.0 %all-to-all-done.5 = bf16[8,8,2048]{2,0,1:T(8,128)(2,1)S(1)} async-done(((bf16[8,8,2048]{2,0,1:T(8,128)(2,1)}), bf16[8,8,2048]{2,0,1:T(8,128)(2,1)S(1)}, u32[]{:S(2)}, u32[]{:S(2)}) %all-to-all-start.5) | async-done | bytes 262176 | tf_op jit(solution)/shard_map/all_to_all | solution.py:68
  170.2 1.8 gather_fusion.6
  172.6 0.7 select_bitcast_fusion.1
  173.3 3.6 %all-to-all-start.7 = ((bf16[8,32,1,128]{3,0,2,1:T(8,128)(2,1)}), bf16[8,32,1,128]{3,0,2,1:T(8,128)(2,1)S(1)}, u32[]{:S(2)}, u32[]{:S(2)}) async-start(bf16[8,32,1,128]{3,0,2,1:T(8,128)(2,1)} %select_bitcast_fusion.1), calls=%async_computation.7 | async-start | bytes 131072 | tf_op jit(solution)/shard_map/all_to_all | solution.py:53
  176.9 1.8 broadcast_select_fusion.1
  178.7 1.3 copy.112
  180.0 4.3 %all-to-all-done.7 = bf16[8,32,1,128]{3,0,2,1:T(8,128)(2,1)S(1)} async-done(((bf16[8,32,1,128]{3,0,2,1:T(8,128)(2,1)}), bf16[8,32,1,128]{3,0,2,1:T(8,128)(2,1)S(1)}, u32[]{:S(2)}, u32[]{:S(2)}) %all-to-all-start.7) | async-done | bytes 65568 | tf_op jit(solution)/shard_map/all_to_all | solution.py:53
  184.3 2.6 all-to-all-start.6
  187.0 0.7 iota_reduce_fusion.5
  189.2 0.7 gather_fusion.10
  191.3 2.5 copy_multiply_fusion.2
  193.8 2.0 copy-done.3
  195.9 17.2 %all-to-all-done.6 = bf16[8,32,16,128]{3,2,0,1:T(8,128)(2,1)S(1)} async-done(((bf16[8,32,16,128]{3,2,0,1:T(8,128)(2,1)}), bf16[8,32,16,128]{3,2,0,1:T(8,128)(2,1)S(1)}, u32[]{:S(2)}, u32[]{:S(2)}) %all-to-all-start.6) | async-done | bytes 1048608 | tf_op jit(solution)/shard_map/all_to_all | solution.py:33
  213.2 3.0 %fusion.21 = bf16[8,8,16,128]{3,1,0,2:T(8,128)(2,1)S(1)} fusion(bf16[16,2,4,128,128]{4,3,2,0,1:T(8,128)(2,1)} %copy-done.3, bf16[8,8,4,16,128]{4,3,0,2,1:T(8,128)(2,1)S(1)} %bitcast.372, f32[16,128]{1,0:T(8,128)S(1)} %get-tuple-element.47, f32[8,8,128]{2,1,0:T(8,128)S(1)} %convolution_bitcast_fusion.1, f32[16]{0:T(128)S(1)} %compare_convert_fusion.5), kind=kOutput, calls=%fused_computation.41 | convolution fusion | flops 134873088 | bytes 3448896 | tf_op jit(solution)/shard_map/rapki,kpij->rakj/dot_general | solution.py:41
  216.4 0.8 reshape.515
  217.2 3.5 %all-to-all-start.8 = ((bf16[8,8,2048]{2,0,1:T(8,128)(2,1)}), bf16[8,8,2048]{2,0,1:T(8,128)(2,1)S(1)}, u32[]{:S(2)}, u32[]{:S(2)}) async-start(bf16[8,8,2048]{2,0,1:T(8,128)(2,1)} %reshape.515), calls=%async_computation.8 | async-start | bytes 524288 | tf_op jit(solution)/shard_map/all_to_all | solution.py:68
  220.7 9.1 %all-to-all-done.8 = bf16[8,8,2048]{2,0,1:T(8,128)(2,1)S(1)} async-done(((bf16[8,8,2048]{2,0,1:T(8,128)(2,1)}), bf16[8,8,2048]{2,0,1:T(8,128)(2,1)S(1)}, u32[]{:S(2)}, u32[]{:S(2)}) %all-to-all-start.8) | async-done | bytes 262176 | tf_op jit(solution)/shard_map/all_to_all | solution.py:68
  230.0 1.8 gather_fusion.9
  232.4 0.7 select_bitcast_fusion
  233.2 3.6 %all-to-all-start.10 = ((bf16[8,32,1,128]{3,0,2,1:T(8,128)(2,1)}), bf16[8,32,1,128]{3,0,2,1:T(8,128)(2,1)S(1)}, u32[]{:S(2)}, u32[]{:S(2)}) async-start(bf16[8,32,1,128]{3,0,2,1:T(8,128)(2,1)} %select_bitcast_fusion), calls=%async_computation.10 | async-start | bytes 131072 | tf_op jit(solution)/shard_map/all_to_all | solution.py:53
  236.8 1.8 broadcast_select_fusion
  238.6 1.2 copy.123
  239.8 4.4 %all-to-all-done.10 = bf16[8,32,1,128]{3,0,2,1:T(8,128)(2,1)S(1)} async-done(((bf16[8,32,1,128]{3,0,2,1:T(8,128)(2,1)}), bf16[8,32,1,128]{3,0,2,1:T(8,128)(2,1)S(1)}, u32[]{:S(2)}, u32[]{:S(2)}) %all-to-all-start.10) | async-done | bytes 65568 | tf_op jit(solution)/shard_map/all_to_all | solution.py:53
  244.2 2.6 all-to-all-start.9
  250.1 2.5 copy_multiply_fusion.3
  252.6 1.9 copy-done
  254.7 18.3 %all-to-all-done.9 = bf16[8,32,16,128]{3,2,0,1:T(8,128)(2,1)S(1)} async-done(((bf16[8,32,16,128]{3,2,0,1:T(8,128)(2,1)}), bf16[8,32,16,128]{3,2,0,1:T(8,128)(2,1)S(1)}, u32[]{:S(2)}, u32[]{:S(2)}) %all-to-all-start.9) | async-done | bytes 1048608 | tf_op jit(solution)/shard_map/all_to_all | solution.py:33
  273.0 3.0 %fusion.20 = bf16[8,8,16,128]{3,1,0,2:T(8,128)(2,1)S(1)} fusion(bf16[16,2,4,128,128]{4,3,2,0,1:T(8,128)(2,1)} %copy-done, bf16[8,8,4,16,128]{4,3,0,2,1:T(8,128)(2,1)S(1)} %bitcast.373, f32[16,128]{1,0:T(8,128)S(1)} %get-tuple-element.44, f32[8,8,128]{2,1,0:T(8,128)S(1)} %convolution_bitcast_fusion, f32[16]{0:T(128)S(1)} %compare_convert_fusion.4), kind=kOutput, calls=%fused_computation.40 | convolution fusion | flops 134873088 | bytes 3448896 | tf_op jit(solution)/shard_map/rapki,kpij->rakj/dot_general | solution.py:41
  276.3 12.5 %all_to_all.60 = bf16[8,8,2048]{2,0,1:T(8,128)(2,1)S(1)} all-to-all(bf16[8,8,2048]{2,0,1:T(8,128)(2,1)S(1)} %reshape.516), channel_id=1, replica_groups=mesh['gx'=8,'gy'=4] {'gx'}, dimensions={1} | all-to-all | bytes 524288 | tf_op jit(solution)/shard_map/all_to_all | solution.py:68
  288.8 0.7 copy.197
  (102 shorter events, 14.5 us)
Async XLA Ops:
  51.4 10.0 %all-to-all-start.1 = ((bf16[8,32,1,128]{3,0,2,1:T(8,128)(2,1)}), bf16[8,32,1,128]{3,0,2,1:T(8,128)(2,1)S(1)}, u32[]{:S(2)}, u32[]{:S(2)}) async-start(bf16[8,32,1,128]{3,0,2,1:T(8,128)(2,1)} %select_bitcast_fusion.3), calls=%async_computation.1 | async-start | bytes 131072 | tf_op jit(solution)/shard_map/all_to_all | solution.py:53
  56.2 14.9 %copy-start.4 = (f32[4,1,16,128]{3,2,1,0:T(8,128)S(1)}, f32[4,1,16,128]{3,2,1,0:T(8,128)}, u32[]{:S(2)}) copy-start(f32[4,1,16,128]{3,2,1,0:T(8,128)} %param.17) | copy-start | bytes 98308
  61.4 31.9 %all-to-all-start = ((bf16[8,32,16,128]{3,2,0,1:T(8,128)(2,1)}), bf16[8,32,16,128]{3,2,0,1:T(8,128)(2,1)S(1)}, u32[]{:S(2)}, u32[]{:S(2)}) async-start(bf16[8,32,16,128]{3,2,0,1:T(8,128)(2,1)} %copy.89), calls=%async_computation | async-start | bytes 2097152 | tf_op jit(solution)/shard_map/all_to_all | solution.py:33
  82.5 2.0 copy-start.1
  97.3 12.8 %all-to-all-start.2 = ((bf16[8,8,2048]{2,0,1:T(8,128)(2,1)}), bf16[8,8,2048]{2,0,1:T(8,128)(2,1)S(1)}, u32[]{:S(2)}, u32[]{:S(2)}) async-start(bf16[8,8,2048]{2,0,1:T(8,128)(2,1)} %reshape.513), calls=%async_computation.2 | async-start | bytes 524288 | tf_op jit(solution)/shard_map/all_to_all | solution.py:68
  110.3 17.0 %copy-start.5 = (s32[4,1,16]{2,1,0:T(1,128)S(1)}, s32[4,1,16]{2,1,0:T(1,128)}, u32[]{:S(2)}) copy-start(s32[4,1,16]{2,1,0:T(1,128)} %param.15) | copy-start | bytes 772
  113.5 11.0 %all-to-all-start.4 = ((bf16[8,32,1,128]{3,0,2,1:T(8,128)(2,1)}), bf16[8,32,1,128]{3,0,2,1:T(8,128)(2,1)S(1)}, u32[]{:S(2)}, u32[]{:S(2)}) async-start(bf16[8,32,1,128]{3,0,2,1:T(8,128)(2,1)} %select_bitcast_fusion.2), calls=%async_computation.4 | async-start | bytes 131072 | tf_op jit(solution)/shard_map/all_to_all | solution.py:53
  124.5 28.8 %all-to-all-start.3 = ((bf16[8,32,16,128]{3,2,0,1:T(8,128)(2,1)}), bf16[8,32,16,128]{3,2,0,1:T(8,128)(2,1)S(1)}, u32[]{:S(2)}, u32[]{:S(2)}) async-start(bf16[8,32,16,128]{3,2,0,1:T(8,128)(2,1)} %copy.101), calls=%async_computation.3 | async-start | bytes 2097152 | tf_op jit(solution)/shard_map/all_to_all | solution.py:33
  134.3 2.0 copy-start.2
  157.3 12.7 %all-to-all-start.5 = ((bf16[8,8,2048]{2,0,1:T(8,128)(2,1)}), bf16[8,8,2048]{2,0,1:T(8,128)(2,1)S(1)}, u32[]{:S(2)}, u32[]{:S(2)}) async-start(bf16[8,8,2048]{2,0,1:T(8,128)(2,1)} %reshape.514), calls=%async_computation.5 | async-start | bytes 524288 | tf_op jit(solution)/shard_map/all_to_all | solution.py:68
  173.3 11.0 %all-to-all-start.7 = ((bf16[8,32,1,128]{3,0,2,1:T(8,128)(2,1)}), bf16[8,32,1,128]{3,0,2,1:T(8,128)(2,1)S(1)}, u32[]{:S(2)}, u32[]{:S(2)}) async-start(bf16[8,32,1,128]{3,0,2,1:T(8,128)(2,1)} %select_bitcast_fusion.1), calls=%async_computation.7 | async-start | bytes 131072 | tf_op jit(solution)/shard_map/all_to_all | solution.py:53
  184.3 28.8 %all-to-all-start.6 = ((bf16[8,32,16,128]{3,2,0,1:T(8,128)(2,1)}), bf16[8,32,16,128]{3,2,0,1:T(8,128)(2,1)S(1)}, u32[]{:S(2)}, u32[]{:S(2)}) async-start(bf16[8,32,16,128]{3,2,0,1:T(8,128)(2,1)} %copy.112), calls=%async_computation.6 | async-start | bytes 2097152 | tf_op jit(solution)/shard_map/all_to_all | solution.py:33
  193.8 2.0 copy-start.3
  217.2 12.7 %all-to-all-start.8 = ((bf16[8,8,2048]{2,0,1:T(8,128)(2,1)}), bf16[8,8,2048]{2,0,1:T(8,128)(2,1)S(1)}, u32[]{:S(2)}, u32[]{:S(2)}) async-start(bf16[8,8,2048]{2,0,1:T(8,128)(2,1)} %reshape.515), calls=%async_computation.8 | async-start | bytes 524288 | tf_op jit(solution)/shard_map/all_to_all | solution.py:68
  233.2 11.0 %all-to-all-start.10 = ((bf16[8,32,1,128]{3,0,2,1:T(8,128)(2,1)}), bf16[8,32,1,128]{3,0,2,1:T(8,128)(2,1)S(1)}, u32[]{:S(2)}, u32[]{:S(2)}) async-start(bf16[8,32,1,128]{3,0,2,1:T(8,128)(2,1)} %select_bitcast_fusion), calls=%async_computation.10 | async-start | bytes 131072 | tf_op jit(solution)/shard_map/all_to_all | solution.py:53
  244.2 28.8 %all-to-all-start.9 = ((bf16[8,32,16,128]{3,2,0,1:T(8,128)(2,1)}), bf16[8,32,16,128]{3,2,0,1:T(8,128)(2,1)S(1)}, u32[]{:S(2)}, u32[]{:S(2)}) async-start(bf16[8,32,16,128]{3,2,0,1:T(8,128)(2,1)} %copy.123), calls=%async_computation.9 | async-start | bytes 2097152 | tf_op jit(solution)/shard_map/all_to_all | solution.py:33
  252.6 1.9 copy-start
where the time goes:
time: 291 us; the launch traced here: 289 us
  waiting for transfers between devices  102 us (35%)
  blocking collectives  56.1 us (19%)
  local copies, waits for them, and re-layouts  44 us (15%)
  starting transfers between devices  37.9 us (13%)
  other arithmetic  29.1 us (10%)
  matrix products  12.6 us (4%)
  between operations  8.25 us (3%)
    all_to_all x4, waiting for transfers between devices, local(): lax.all_to_all(outgoing, ('gx', 'gy'), split_axis=1, concat_axis=1, tiled...  61.2 us
    all_gather x1, blocking collectives, local(): count_table = lax.all_gather(tile_count, ('gx', 'gy'), axis=1, tiled=True)  43.6 us
    all_to_all x3, waiting for transfers between devices, local(): lax.all_to_all(result, 'gx', split_axis=1, concat_axis=1, tiled=True)  27.2 us
    all_to_all x4, starting transfers between devices, local(): lax.all_to_all(outgoing, ('gx', 'gy'), split_axis=1, concat_axis=1, tiled...  13.8 us
    all_to_all x4, starting transfers between devices, local(): lax.all_to_all(rest_out, ('gx', 'gy'), split_axis=1, concat_axis=1, tiled...  13.4 us
    all_to_all x4, waiting for transfers between devices, local(): lax.all_to_all(rest_out, ('gx', 'gy'), split_axis=1, concat_axis=1, tiled...  13.3 us
    all_to_all x1, blocking collectives, local(): lax.all_to_all(result, 'gx', split_axis=1, concat_axis=1, tiled=True)  12.5 us
    dot_general x4, matrix products, local(): jnp.einsum('rapki,kpij->rakj', incoming, weights[:, 0], preferred_element...  12 us
  transfers between devices with their start and end apart: 11, of which 11 were waited for; matrix products, arithmetic and copies ran while one was open for 15% of the time, Pallas kernels for 0%

commit v1 on v0

v1 whole, which is shorter than its diff:
```python
import functools

import jax
import jax.numpy as jnp
from jax import lax
from jax.experimental import pallas as pl
from jax.experimental.pallas import tpu as pltpu
from jax.sharding import PartitionSpec as P


def pick_kernel(layer, owned, groups, table, heavy, live, state_ref, out_ref, kept_ref):
    step = pl.program_id(0)
    blocks = state_ref.shape[0]
    dests = out_ref.shape[0]

    @pl.when(step == 0)
    def _():
        def mask(i, carry):
            kept_ref[i] = jnp.where(live[layer, i] > 0, state_ref[i], jnp.zeros_like(state_ref[i]))
            return carry

        lax.fori_loop(0, blocks, mask, 0, unroll=8)

    def one_dest(d, carry):
        dest = step * dests + d
        first = (dest % groups) * blocks + (dest // groups) * owned
        for k in range(owned):
            out_ref[d, k] = kept_ref[table[layer, 0, first + k]]
        out_ref[d, owned] = kept_ref[table[layer, 1, first + heavy[dest, layer]]]
        return carry

    lax.fori_loop(0, dests, one_dest, 0)


def pick(layer, owned, groups, table, heavy, live, state):
    blocks, rows, side = state.shape
    devices = heavy.shape[0]
    steps = 4
    return pl.pallas_call(
        functools.partial(pick_kernel, layer, owned, groups),
        out_shape=jax.ShapeDtypeStruct((devices, owned + 1, rows, side), state.dtype),
        grid_spec=pltpu.PrefetchScalarGridSpec(
            num_scalar_prefetch=3,
            grid=(steps,),
            in_specs=[pl.BlockSpec((blocks, rows, side), lambda i, *_: (0, 0, 0))],
            out_specs=pl.BlockSpec(
                (devices // steps, owned + 1, rows, side), lambda i, *_: (i, 0, 0, 0)
            ),
            scratch_shapes=[pltpu.VMEM((blocks, rows, side), state.dtype)],
        ),
        name=f"pick_{layer}",
    )(table, heavy, live, state)


def matmul_kernel(
    layer, counts, x_ref, rest_ref, w_ref, w_any, bias_ref, out_ref, acc_ref, wrest_ref, sem
):
    step = pl.program_id(0)
    across, groups, chunk, rows, side = x_ref.shape
    owned = counts.shape[1]
    total_rows = across * rows
    heavy = jnp.int32(0)
    for k in range(owned):
        heavy = jnp.where(counts[layer, k] > groups, k, heavy)
    copy = pltpu.make_async_copy(w_any.at[layer, 0, heavy, pl.ds(groups, groups)], wrest_ref, sem)

    @pl.when(step == 0)
    def _():
        copy.start()

    def gathered(ref, position, first, count):
        parts = []
        for g in range(groups):
            part = ref[:, g, position].reshape(total_rows, side)
            parts.append(jnp.where(first + g < count, part, jnp.zeros_like(part)))
        return jnp.concatenate(parts, axis=1)

    for c in range(chunk):
        k = step * chunk + c
        lhs = gathered(x_ref, c, 0, counts[layer, k])
        weight = w_ref[0, 0, c].reshape(groups * side, side)
        summed = jnp.dot(lhs, weight, preferred_element_type=jnp.float32)
        summed = summed + bias_ref[0, 0, pl.ds(k, 1), :]
        acc_ref[k] = summed
        out_ref[:, k] = (
            jnp.maximum(summed, 0.0).astype(out_ref.dtype).reshape(across, rows, side)
        )

    @pl.when(step == pl.num_programs(0) - 1)
    def _():
        copy.wait()
        lhs = gathered(rest_ref, 0, groups, counts[layer, heavy])
        weight = wrest_ref[...].reshape(groups * side, side)
        summed = acc_ref[heavy] + jnp.dot(lhs, weight, preferred_element_type=jnp.float32)
        out_ref[:, heavy] = (
            jnp.maximum(summed, 0.0).astype(out_ref.dtype).reshape(across, rows, side)
        )


def multiply(layer, counts, incoming, weight_tiles, bias_terms):
    across, groups, width, rows, side = incoming.shape
    owned = width - 1
    steps = 4 if owned % 4 == 0 else 1
    chunk = owned // steps
    return pl.pallas_call(
        functools.partial(matmul_kernel, layer),
        out_shape=jax.ShapeDtypeStruct((across, owned, rows, side), incoming.dtype),
        grid_spec=pltpu.PrefetchScalarGridSpec(
            num_scalar_prefetch=1,
            grid=(steps,),
            in_specs=[
                pl.BlockSpec((across, groups, chunk, rows, side), lambda i, *_: (0, 0, i, 0, 0)),
                pl.BlockSpec((across, groups, 1, rows, side), lambda i, *_: (0, 0, owned, 0, 0)),
                pl.BlockSpec(
                    (1, 1, chunk, groups, side, side), lambda i, *_: (layer, 0, i, 0, 0, 0)
                ),
                pl.BlockSpec(memory_space=pl.ANY),
                pl.BlockSpec((1, 1, owned, side), lambda i, *_: (layer, 0, 0, 0)),
            ],
            out_specs=pl.BlockSpec((across, owned, rows, side), lambda i, *_: (0, 0, 0, 0)),
            scratch_shapes=[
                pltpu.VMEM((owned, across * rows, side), jnp.float32),
                pltpu.VMEM((groups, side, side), weight_tiles.dtype),
                pltpu.SemaphoreType.DMA,
            ],
        ),
        name=f"multiply_{layer}",
    )(counts, incoming, incoming, weight_tiles, weight_tiles, bias_terms)


def local(activations, live_blocks, tile_index, tile_count, weight_tiles, bias_terms):
    across = lax.axis_size("gx")
    groups = lax.axis_size("gy")
    my_group = lax.axis_index("gy")
    layers = tile_index.shape[0]
    rows = activations.shape[0]
    side = weight_tiles.shape[-1]
    owned = weight_tiles.shape[2]
    blocks = activations.shape[1] // side
    devices = across * groups

    counts = tile_count[:, 0]
    spots = jnp.arange(owned, dtype=jnp.int32)
    heavy = jnp.sum(jnp.where(counts > groups, spots[None], 0), axis=1)
    heavy = jnp.pad(heavy, (0, side - layers))
    heavy_all = lax.all_to_all(
        jnp.broadcast_to(heavy, (devices, 1, side)), ("gx", "gy"), 0, 0, tiled=True
    )[:, 0, :layers]

    slots = jnp.transpose(tile_index, (0, 2, 1)).reshape(layers, -1, groups, tile_index.shape[1])
    table = lax.dynamic_index_in_dim(slots, my_group, 2, keepdims=False) - my_group * blocks
    live = live_blocks[:, 0]

    state = jnp.transpose(activations.reshape(rows, blocks, side), (1, 0, 2))
    for layer in range(layers):
        outgoing = pick(layer, owned, groups, table, heavy_all, live, state)
        incoming = lax.all_to_all(outgoing, ("gx", "gy"), 0, 0, tiled=True)
        incoming = incoming.reshape(across, groups, owned + 1, rows, side)
        result = multiply(layer, counts, incoming, weight_tiles, bias_terms)
        state = lax.all_to_all(result, "gx", 0, 0, tiled=True).reshape(blocks, rows, side)
    return jnp.transpose(state, (1, 0, 2)).reshape(rows, blocks * side)


def solution(mesh):
    placed = (
        P("gx", "gy"),
        P(None, "gx", "gy"),
        P(),
        P(None, "gy", "gx"),
        P(None, "gy", "gx", None, None, None),
        P(None, "gy", "gx", None),
    )
    return jax.shard_map(
        local, mesh=mesh, in_specs=placed, out_specs=P("gx", "gy"), check_vma=False
    )
```

time: 291 us -> 241 us (0.83)
  blocking collectives: 56.1 us -> 182 us
  waiting for transfers between devices: 102 us -> 5.58 us
  local copies, waits for them, and re-layouts: 44 us -> 3.42 us
  Pallas kernels: 0 us -> 39.9 us
  starting transfers between devices: 37.9 us -> 7.33 us
  other arithmetic: 29.1 us -> 0.81 us
  matrix products: 12.6 us -> 0 us
  between operations: 8.25 us -> 0.07 us
    all_to_all x1 -> x8, blocking collectives: 12.5 us -> 182 us  [the longest x4 131 us: local(): incoming = lax.all_to_all(outgoing, ('gx', 'gy'), 0, 0, tiled=True)]
    all_to_all x11 -> x1, waiting for transfers between devices: 102 us -> 5.58 us  [local(): lax.all_to_all(jnp.broadcast_to(heavy, (devices, 1, side)), ('gx', 'gy'),...]
    all_gather x1 -> x0, blocking collectives: 43.6 us -> none  [local(): count_table = lax.all_gather(tile_count, ('gx', 'gy'), axis=1, tiled=True)]
    pallas_call x0 -> x8, Pallas kernels: none -> 39.9 us  [the longest x4 21.3 us: pick(): pl.pallas_call(functools.partial(pick_kernel, layer, owned, groups), out_...]
    all_to_all x11 -> x1, starting transfers between devices: 37.9 us -> 7.33 us  [local(): lax.all_to_all(jnp.broadcast_to(heavy, (devices, 1, side)), ('gx', 'gy'),...]
    gather x16 -> x0, local copies, waits for them, and re-layouts: 12.7 us -> none  [the longest x4 7.2 us: local(): outgoing = jnp.take(blocks, chosen.reshape(-1), axis=1)]
    dot_general x8 -> x0, matrix products: 12.6 us -> none  [the longest x4 12 us: local(): jnp.einsum('rapki,kpij->rakj', incoming, weights[:, 0], preferred_element...]
    slice x7 -> x0, local copies, waits for them, and re-layouts: 11.9 us -> none  [the longest x1 11.1 us: local(): weights = weight_tiles[layer_index, 0] * usable[:, :, None, None]]
  transfers between devices with their start and end apart: 11 -> 1, of which waited for: 11 -> 1; matrix products, arithmetic and copies ran while one was open for 15% -> 1% of each run, Pallas kernels for 0% -> 0%
where the time goes in v1:
time: 241 us; the launch traced here: 239 us
  blocking collectives  182 us (76%)
  Pallas kernels  39.9 us (17%)
  starting transfers between devices  7.33 us (3%)
  waiting for transfers between devices  5.58 us (2%)
  local copies, waits for them, and re-layouts  3.42 us (1%)
    all_to_all x4, blocking collectives, local(): incoming = lax.all_to_all(outgoing, ('gx', 'gy'), 0, 0, tiled=True)  131 us
    all_to_all x4, blocking collectives, local(): lax.all_to_all(result, 'gx', 0, 0, tiled=True).reshape(blocks, rows, side)  51.3 us
    pallas_call x4, Pallas kernels, pick(): pl.pallas_call(functools.partial(pick_kernel, layer, owned, groups), out_...  21.3 us
    pallas_call x4, Pallas kernels, multiply(): pl.pallas_call(functools.partial(matmul_kernel, layer), out_shape=jax.Sha...  18.6 us
    all_to_all x1, starting transfers between devices, local(): lax.all_to_all(jnp.broadcast_to(heavy, (devices, 1, side)), ('gx', 'gy'),...  7.33 us
    all_to_all x1, waiting for transfers between devices, local(): lax.all_to_all(jnp.broadcast_to(heavy, (devices, 1, side)), ('gx', 'gy'),...  5.58 us
  transfers between devices with their start and end apart: 1, of which 1 were waited for; matrix products, arithmetic and copies ran while one was open for 1% of the time, Pallas kernels for 0%

profile of v1, /device:TPU:0, one launch (start us, length us, event | category | flops | bytes accessed | tf_op | source)
XLA Modules:
  0.0 239.2 jit_solution(6680246541656820276)
XLA Ops:
  0.0 0.8 select_reduce_fusion
  0.8 0.6 broadcast_in_dim.18
  1.4 7.3 %all-to-all-start = ((s32[32,1,128]{2,1,0:T(1,128)}), s32[32,1,128]{2,1,0:T(1,128)S(1)}, u32[]{:S(2)}, u32[]{:S(2)}) async-start(s32[32,1,128]{2,1,0:T(1,128)} %broadcast_in_dim.18), calls=%async_computation | async-start | bytes 32768 | tf_op jit(solution)/shard_map/all_to_all | solution.py:146
  8.8 0.9 copy.17
  9.7 0.6 copy.28
  10.3 5.6 %all-to-all-done = s32[32,1,128]{2,1,0:T(1,128)S(1)} async-done(((s32[32,1,128]{2,1,0:T(1,128)}), s32[32,1,128]{2,1,0:T(1,128)S(1)}, u32[]{:S(2)}, u32[]{:S(2)}) %all-to-all-start) | async-done | bytes 16416 | tf_op jit(solution)/shard_map/all_to_all | solution.py:146
  15.9 0.0 copy-start
  15.9 0.6 copy-done
  16.5 5.0 %pick_0.1 = bf16[32,17,8,128]{3,2,1,0:T(8,128)(2,1)} custom-call(s32[4,2,512]{2,1,0:T(2,128)} %bitcast.40, s32[32,4]{1,0:T(8,128)} %bitcast.36, s32[4,128]{1,0:T(4,128)} %bitcast.52, bf16[128,8,128]{2,1,0:T(8,128)(2,1)} %bitcast.44), custom_call_target="tpu_custom_call" | custom-call | tf_op jit(solution)/shard_map/pick_0/pallas_call | solution.py:39
  21.5 32.7 %all_to_all.45 = bf16[32,17,8,128]{3,2,1,0:T(8,128)(2,1)} all-to-all(bf16[32,17,8,128]{3,2,1,0:T(8,128)(2,1)} %pick_0.1), channel_id=1, replica_groups=mesh['gx'=8,'gy'=4] {'gx','gy'}, dimensions={0} | all-to-all | bytes 2228224 | tf_op jit(solution)/shard_map/all_to_all | solution.py:157
  54.2 4.7 %multiply_0.1 = bf16[8,16,8,128]{3,2,1,0:T(8,128)(2,1)} custom-call(s32[4,16]{1,0:T(4,128)} %bitcast.48, bf16[8,4,17,8,128]{4,3,2,1,0:T(8,128)(2,1)} %bitcast.24, bf16[8,4,17,8,128]{4,3,2,1,0:T(8,128)(2,1)} %bitcast.25, bf16[4,1,16,8,128,128]{5,4,3,2,1,0:T(8,128)(2,1)} %w_any.7, bf16[4,1,16,8,128,128]{5,4,3,2,1,0:T(8,128)(2,1)} %w_any.7, ...), custom_call_target="tpu_custom_call" | custom-call | tf_op jit(solution)/shard_map/multiply_0/pallas_call | solution.py:105
  58.9 13.0 %all_to_all.46 = bf16[8,16,8,128]{3,2,1,0:T(8,128)(2,1)} all-to-all(bf16[8,16,8,128]{3,2,1,0:T(8,128)(2,1)} %multiply_0.1), channel_id=1, replica_groups=mesh['gx'=8,'gy'=4] {'gx'}, dimensions={0} | all-to-all | bytes 524288 | tf_op jit(solution)/shard_map/all_to_all | solution.py:160
  71.9 5.4 %pick_1.1 = bf16[32,17,8,128]{3,2,1,0:T(8,128)(2,1)} custom-call(s32[4,2,512]{2,1,0:T(2,128)} %bitcast.41, s32[32,4]{1,0:T(8,128)} %bitcast.37, s32[4,128]{1,0:T(4,128)} %bitcast.53, bf16[128,8,128]{2,1,0:T(8,128)(2,1)} %bitcast.34), custom_call_target="tpu_custom_call" | custom-call | tf_op jit(solution)/shard_map/pick_1/pallas_call | solution.py:39
  77.3 32.7 %all_to_all.47 = bf16[32,17,8,128]{3,2,1,0:T(8,128)(2,1)} all-to-all(bf16[32,17,8,128]{3,2,1,0:T(8,128)(2,1)} %pick_1.1), channel_id=1, replica_groups=mesh['gx'=8,'gy'=4] {'gx','gy'}, dimensions={0} | all-to-all | bytes 2228224 | tf_op jit(solution)/shard_map/all_to_all | solution.py:157
  110.0 4.7 %multiply_1.1 = bf16[8,16,8,128]{3,2,1,0:T(8,128)(2,1)} custom-call(s32[4,16]{1,0:T(4,128)} %bitcast.49, bf16[8,4,17,8,128]{4,3,2,1,0:T(8,128)(2,1)} %bitcast.26, bf16[8,4,17,8,128]{4,3,2,1,0:T(8,128)(2,1)} %bitcast.27, bf16[4,1,16,8,128,128]{5,4,3,2,1,0:T(8,128)(2,1)} %w_any.7, bf16[4,1,16,8,128,128]{5,4,3,2,1,0:T(8,128)(2,1)} %w_any.7, ...), custom_call_target="tpu_custom_call" | custom-call | tf_op jit(solution)/shard_map/multiply_1/pallas_call | solution.py:105
  114.6 13.0 %all_to_all.48 = bf16[8,16,8,128]{3,2,1,0:T(8,128)(2,1)} all-to-all(bf16[8,16,8,128]{3,2,1,0:T(8,128)(2,1)} %multiply_1.1), channel_id=1, replica_groups=mesh['gx'=8,'gy'=4] {'gx'}, dimensions={0} | all-to-all | bytes 524288 | tf_op jit(solution)/shard_map/all_to_all | solution.py:160
  127.6 5.4 %pick_2.1 = bf16[32,17,8,128]{3,2,1,0:T(8,128)(2,1)} custom-call(s32[4,2,512]{2,1,0:T(2,128)} %bitcast.42, s32[32,4]{1,0:T(8,128)} %bitcast.38, s32[4,128]{1,0:T(4,128)} %bitcast.54, bf16[128,8,128]{2,1,0:T(8,128)(2,1)} %bitcast.35), custom_call_target="tpu_custom_call" | custom-call | tf_op jit(solution)/shard_map/pick_2/pallas_call | solution.py:39
  133.1 32.7 %all_to_all.49 = bf16[32,17,8,128]{3,2,1,0:T(8,128)(2,1)} all-to-all(bf16[32,17,8,128]{3,2,1,0:T(8,128)(2,1)} %pick_2.1), channel_id=1, replica_groups=mesh['gx'=8,'gy'=4] {'gx','gy'}, dimensions={0} | all-to-all | bytes 2228224 | tf_op jit(solution)/shard_map/all_to_all | solution.py:157
  165.8 4.7 %multiply_2.1 = bf16[8,16,8,128]{3,2,1,0:T(8,128)(2,1)} custom-call(s32[4,16]{1,0:T(4,128)} %bitcast.50, bf16[8,4,17,8,128]{4,3,2,1,0:T(8,128)(2,1)} %bitcast.28, bf16[8,4,17,8,128]{4,3,2,1,0:T(8,128)(2,1)} %bitcast.29, bf16[4,1,16,8,128,128]{5,4,3,2,1,0:T(8,128)(2,1)} %w_any.7, bf16[4,1,16,8,128,128]{5,4,3,2,1,0:T(8,128)(2,1)} %w_any.7, ...), custom_call_target="tpu_custom_call" | custom-call | tf_op jit(solution)/shard_map/multiply_2/pallas_call | solution.py:105
  170.4 13.0 %all_to_all.50 = bf16[8,16,8,128]{3,2,1,0:T(8,128)(2,1)} all-to-all(bf16[8,16,8,128]{3,2,1,0:T(8,128)(2,1)} %multiply_2.1), channel_id=1, replica_groups=mesh['gx'=8,'gy'=4] {'gx'}, dimensions={0} | all-to-all | bytes 524288 | tf_op jit(solution)/shard_map/all_to_all | solution.py:160
  183.4 5.4 %pick_3.1 = bf16[32,17,8,128]{3,2,1,0:T(8,128)(2,1)} custom-call(s32[4,2,512]{2,1,0:T(2,128)} %bitcast.43, s32[32,4]{1,0:T(8,128)} %bitcast.39, s32[4,128]{1,0:T(4,128)} %bitcast.55, bf16[128,8,128]{2,1,0:T(8,128)(2,1)} %bitcast.33), custom_call_target="tpu_custom_call" | custom-call | tf_op jit(solution)/shard_map/pick_3/pallas_call | solution.py:39
  188.9 32.7 %all_to_all.51 = bf16[32,17,8,128]{3,2,1,0:T(8,128)(2,1)} all-to-all(bf16[32,17,8,128]{3,2,1,0:T(8,128)(2,1)} %pick_3.1), channel_id=1, replica_groups=mesh['gx'=8,'gy'=4] {'gx','gy'}, dimensions={0} | all-to-all | bytes 2228224 | tf_op jit(solution)/shard_map/all_to_all | solution.py:157
  221.5 4.7 %multiply_3.1 = bf16[8,16,8,128]{3,2,1,0:T(8,128)(2,1)} custom-call(s32[4,16]{1,0:T(4,128)} %bitcast.51, bf16[8,4,17,8,128]{4,3,2,1,0:T(8,128)(2,1)} %bitcast.30, bf16[8,4,17,8,128]{4,3,2,1,0:T(8,128)(2,1)} %bitcast.31, bf16[4,1,16,8,128,128]{5,4,3,2,1,0:T(8,128)(2,1)} %w_any.7, bf16[4,1,16,8,128,128]{5,4,3,2,1,0:T(8,128)(2,1)} %w_any.7, ...), custom_call_target="tpu_custom_call" | custom-call | tf_op jit(solution)/shard_map/multiply_3/pallas_call | solution.py:105
  226.2 12.3 %all_to_all.52 = bf16[8,16,8,128]{3,2,1,0:T(8,128)(2,1)S(1)} all-to-all(bf16[8,16,8,128]{3,2,1,0:T(8,128)(2,1)} %multiply_3.1), channel_id=1, replica_groups=mesh['gx'=8,'gy'=4] {'gx'}, dimensions={0} | all-to-all | bytes 524288 | tf_op jit(solution)/shard_map/all_to_all | solution.py:160
  238.5 0.7 copy.30
  (2 shorter events, 0.0 us)
Async XLA Ops:
  1.4 14.4 %all-to-all-start = ((s32[32,1,128]{2,1,0:T(1,128)}), s32[32,1,128]{2,1,0:T(1,128)S(1)}, u32[]{:S(2)}, u32[]{:S(2)}) async-start(s32[32,1,128]{2,1,0:T(1,128)} %broadcast_in_dim.18), calls=%async_computation | async-start | bytes 32768 | tf_op jit(solution)/shard_map/all_to_all | solution.py:146
  15.9 0.6 copy-start

commit v2 on v1

v2 whole, which is shorter than its diff:
```python
import functools

import jax
import jax.numpy as jnp
from jax import lax
from jax.experimental import pallas as pl
from jax.experimental.pallas import tpu as pltpu
from jax.sharding import Mesh, PartitionSpec as P

HALF, PAIR, REST, GROUP = "half", "pair", "rest", "gy"
ROWS_OVER = (HALF, PAIR, REST)
FETCH_OVER = (PAIR, REST, GROUP)


def pick_kernel(layer, owned, groups, where, table, heavy, live, *refs):
    *state_refs, out_ref, kept_ref = refs
    step = pl.program_id(0)
    blocks = kept_ref.shape[0]
    dests = out_ref.shape[0]
    half = where[0]

    @pl.when(step == 0)
    def _():
        if len(state_refs) == 2:
            own_ref, partner_ref = state_refs

            def mask(i, carry):
                own = own_ref[i]
                partner = partner_ref[i]
                kept_ref[i, half] = jnp.where(live[half, layer, i] > 0, own, jnp.zeros_like(own))
                kept_ref[i, 1 - half] = jnp.where(
                    live[1 - half, layer, i] > 0, partner, jnp.zeros_like(own)
                )
                return carry

            lax.fori_loop(0, blocks, mask, 0, unroll=8)
        else:
            (state_ref,) = state_refs
            batch = 8

            def mask(b, carry):
                pieces = []
                for i in range(batch):
                    for h in range(2):
                        tile = state_ref[b * batch + i, h]
                        alive = live[h, layer, b * batch + i] > 0
                        pieces.append(jnp.where(alive, tile, jnp.zeros_like(tile)))
                for i in range(batch):
                    for h in range(2):
                        kept_ref[b * batch + i, h] = pieces[2 * i + h]
                return carry

            lax.fori_loop(0, blocks // batch, mask, 0)

    def one_dest(d, carry):
        dest = step * dests + d
        owner = half * (dests * pl.num_programs(0) // groups) + dest // groups
        first = (dest % groups) * blocks + owner * owned
        spots = [table[layer, 0, first + k] for k in range(owned)]
        spots.append(table[layer, 1, first + heavy[dest, layer]])
        pieces = [kept_ref[spot] for spot in spots]
        for k, piece in enumerate(pieces):
            out_ref[d, k] = piece
        return carry

    lax.fori_loop(0, dests, one_dest, 0)


def pick(layer, owned, groups, where, table, heavy, live, states):
    blocks, (rows, side) = states[0].shape[0], states[0].shape[-2:]
    devices = heavy.shape[0]
    steps = 2
    return pl.pallas_call(
        functools.partial(pick_kernel, layer, owned, groups),
        out_shape=jax.ShapeDtypeStruct((devices, owned + 1, 2, rows, side), states[0].dtype),
        grid_spec=pltpu.PrefetchScalarGridSpec(
            num_scalar_prefetch=4,
            grid=(steps,),
            in_specs=[
                pl.BlockSpec(state.shape, lambda i, *_, n=state.ndim: (0,) * n) for state in states
            ],
            out_specs=pl.BlockSpec(
                (devices // steps, owned + 1, 2, rows, side), lambda i, *_: (i, 0, 0, 0, 0)
            ),
            scratch_shapes=[pltpu.VMEM((blocks, 2, rows, side), states[0].dtype)],
        ),
        name=f"pick_{layer}",
    )(where, table, heavy, live, *states)


def multiply_kernel(
    layer, last, where, counts, x_ref, rest_ref, w_ref, w_any, bias_ref, out_ref, acc_ref, wrest_ref, sem
):
    step = pl.program_id(0)
    across, groups, chunk, _, rows, side = x_ref.shape
    owned = counts.shape[1]
    total_rows = across * 2 * rows
    half = where[0]
    heavy = jnp.int32(0)
    for k in range(owned):
        heavy = jnp.where(counts[layer, k] > groups, k, heavy)
    copy = pltpu.make_async_copy(w_any.at[layer, 0, heavy, pl.ds(groups, groups)], wrest_ref, sem)

    @pl.when(step == 0)
    def _():
        copy.start()

    def gathered(ref, position, first, count):
        parts = []
        for g in range(groups):
            part = ref[:, g, position].reshape(total_rows, side)
            parts.append(jnp.where(first + g < count, part, jnp.zeros_like(part)))
        return jnp.concatenate(parts, axis=1)

    def write(k, summed):
        value = jnp.maximum(summed, 0.0).astype(out_ref.dtype)
        value = value.reshape(2, across // 2, 2, rows, side)
        if last:
            low, high = value[:, :, 0], value[:, :, 1]
            near = jnp.where(half == 0, low, high)
            far = jnp.where(half == 0, high, low)
        else:
            near = far = value
        out_ref[half, :, :, k] = near
        out_ref[1 - half, 0, :, k] = far[1]
        out_ref[1 - half, 1, :, k] = far[0]

    for c in range(chunk):
        k = step * chunk + c
        lhs = gathered(x_ref, c, 0, counts[layer, k])
        weight = w_ref[0, 0, c].reshape(groups * side, side)
        summed = jnp.dot(lhs, weight, preferred_element_type=jnp.float32)
        summed = summed + bias_ref[0, 0, pl.ds(k, 1), :]
        acc_ref[k] = summed
        write(k, summed)

    @pl.when(step == pl.num_programs(0) - 1)
    def _():
        copy.wait()
        lhs = gathered(rest_ref, 0, groups, counts[layer, heavy])
        weight = wrest_ref[...].reshape(groups * side, side)
        write(heavy, acc_ref[heavy] + jnp.dot(lhs, weight, preferred_element_type=jnp.float32))


def multiply(layer, last, where, counts, incoming, weight_tiles, bias_terms):
    across, groups, width, _, rows, side = incoming.shape
    owned = width - 1
    steps = 4 if owned % 4 == 0 else 1
    chunk = owned // steps
    out = (2, 2, across // 2, owned) + (() if last else (2,)) + (rows, side)
    return pl.pallas_call(
        functools.partial(multiply_kernel, layer, last),
        out_shape=jax.ShapeDtypeStruct(out, incoming.dtype),
        grid_spec=pltpu.PrefetchScalarGridSpec(
            num_scalar_prefetch=2,
            grid=(steps,),
            in_specs=[
                pl.BlockSpec(
                    (across, groups, chunk, 2, rows, side), lambda i, *_: (0, 0, i, 0, 0, 0)
                ),
                pl.BlockSpec(
                    (across, groups, 1, 2, rows, side), lambda i, *_: (0, 0, owned, 0, 0, 0)
                ),
                pl.BlockSpec(
                    (1, 1, chunk, groups, side, side), lambda i, *_: (layer, 0, i, 0, 0, 0)
                ),
                pl.BlockSpec(memory_space=pl.ANY),
                pl.BlockSpec((1, 1, owned, side), lambda i, *_: (layer, 0, 0, 0)),
            ],
            out_specs=pl.BlockSpec(out, lambda i, *_: (0,) * len(out)),
            scratch_shapes=[
                pltpu.VMEM((owned, across * 2 * rows, side), jnp.float32),
                pltpu.VMEM((groups, side, side), weight_tiles.dtype),
                pltpu.SemaphoreType.DMA,
            ],
        ),
        name=f"multiply_{layer}",
    )(where, counts, incoming, incoming, weight_tiles, weight_tiles, bias_terms)


def local(activations, live_blocks, tile_index, tile_count, weight_tiles, bias_terms):
    rest = lax.axis_size(REST)
    groups = lax.axis_size(GROUP)
    my_group = lax.axis_index(GROUP)
    my_half = lax.axis_index(HALF)
    layers = tile_index.shape[0]
    rows = activations.shape[0]
    side = weight_tiles.shape[-1]
    owned = weight_tiles.shape[2]
    blocks = activations.shape[1] // side
    devices = 2 * rest * groups
    partners = [
        ((h * 2 + p) * rest + r, ((1 - h) * 2 + 1 - p) * rest + r)
        for h in range(2)
        for p in range(2)
        for r in range(rest)
    ]

    own = jnp.transpose(activations.reshape(rows, blocks, side), (1, 0, 2))
    partner = lax.ppermute(own, ROWS_OVER, partners)
    live_own = live_blocks[:, 0]
    live_partner = lax.ppermute(live_own, ROWS_OVER, partners)
    live = jnp.where(
        my_half == 0, jnp.stack([live_own, live_partner]), jnp.stack([live_partner, live_own])
    )
    where = my_half.reshape(1)

    counts = tile_count[:, 0]
    spots = jnp.arange(owned, dtype=jnp.int32)
    heavy = jnp.sum(jnp.where(counts > groups, spots[None], 0), axis=1)
    heavy = jnp.pad(heavy, (0, side - layers))
    heavy_all = lax.all_to_all(
        jnp.broadcast_to(heavy, (devices, 1, side)), FETCH_OVER, 0, 0, tiled=True
    )[:, 0, :layers]

    slots = jnp.transpose(tile_index, (0, 2, 1)).reshape(layers, -1, groups, tile_index.shape[1])
    table = lax.dynamic_index_in_dim(slots, my_group, 2, keepdims=False) - my_group * blocks

    states = [own, partner]
    for layer in range(layers):
        last = layer == layers - 1
        outgoing = pick(layer, owned, groups, where, table, heavy_all, live, states)
        incoming = lax.all_to_all(outgoing, FETCH_OVER, 0, 0, tiled=True)
        incoming = incoming.reshape(2 * rest, groups, owned + 1, 2, rows, side)
        result = multiply(layer, last, where, counts, incoming, weight_tiles, bias_terms)
        result = result.reshape((4 * rest,) + result.shape[3:])
        returned = lax.all_to_all(result, ROWS_OVER, 0, 0, tiled=True)
        states = [returned.reshape((blocks,) + returned.shape[2:])]
    return jnp.transpose(states[0], (1, 0, 2)).reshape(rows, blocks * side)


def solution(mesh):
    across, groups = mesh.shape["gx"], mesh.shape["gy"]
    split = Mesh(mesh.devices.reshape(2, 2, across // 4, groups), (HALF, PAIR, REST, GROUP))
    placed = (
        P(ROWS_OVER, GROUP),
        P(None, ROWS_OVER, GROUP),
        P(),
        P(None, GROUP, ROWS_OVER),
        P(None, GROUP, ROWS_OVER, None, None, None),
        P(None, GROUP, ROWS_OVER, None),
    )
    return jax.shard_map(
        local, mesh=split, in_specs=placed, out_specs=P(ROWS_OVER, GROUP), check_vma=False
    )
```

time: 241 us -> 212 us (0.88)
  blocking collectives: 182 us -> 154 us
  starting transfers between devices: 7.33 us -> 10.5 us
  waiting for transfers between devices: 5.58 us -> 2.65 us
  Pallas kernels: 39.9 us -> 37.2 us
    all_to_all x8, blocking collectives: 182 us -> 154 us  [the longest x4 84.9 us: local(): incoming = lax.all_to_all(outgoing, FETCH_OVER, 0, 0, tiled=True)]
    ppermute x0 -> x2, starting transfers between devices: none -> 6.67 us  [the longest x1 5.08 us: local(): partner = lax.ppermute(own, ROWS_OVER, partners)]
    all_to_all x1, waiting for transfers between devices: 5.58 us -> 0.01 us  [local(): lax.all_to_all(jnp.broadcast_to(heavy, (devices, 1, side)), FETCH_OVER, 0...]
    all_to_all x1, starting transfers between devices: 7.33 us -> 3.83 us  [local(): lax.all_to_all(jnp.broadcast_to(heavy, (devices, 1, side)), FETCH_OVER, 0...]
    pallas_call x4, Pallas kernels: 21.3 us -> 18.3 us  [pick(): pl.pallas_call(functools.partial(pick_kernel, layer, owned, groups), out_...]
    ppermute x0 -> x2, waiting for transfers between devices: none -> 2.65 us  [the longest x1 2.64 us: local(): live_partner = lax.ppermute(live_own, ROWS_OVER, partners)]
  transfers between devices with their start and end apart: 1 -> 3, of which waited for: 1 -> 1; matrix products, arithmetic and copies ran while one was open for 1% -> 2% of each run, Pallas kernels for 0% -> 0%
where the time goes in v2:
time: 212 us; the launch traced here: 210 us
  blocking collectives  154 us (73%)
  Pallas kernels  37.2 us (18%)
  starting transfers between devices  10.5 us (5%)
  local copies, waits for them, and re-layouts  3.51 us (2%)
  waiting for transfers between devices  2.65 us (1%)
  other arithmetic  2.16 us (1%)
    all_to_all x4, blocking collectives, local(): incoming = lax.all_to_all(outgoing, FETCH_OVER, 0, 0, tiled=True)  84.9 us
    all_to_all x4, blocking collectives, local(): returned = lax.all_to_all(result, ROWS_OVER, 0, 0, tiled=True)  68.9 us
    pallas_call x4, Pallas kernels, multiply(): pl.pallas_call(functools.partial(multiply_kernel, layer, last), out_shape...  18.9 us
    pallas_call x4, Pallas kernels, pick(): pl.pallas_call(functools.partial(pick_kernel, layer, owned, groups), out_...  18.3 us
    ppermute x1, starting transfers between devices, local(): partner = lax.ppermute(own, ROWS_OVER, partners)  5.08 us
  transfers between devices with their start and end apart: 3, of which 1 were waited for; matrix products, arithmetic and copies ran while one was open for 2% of the time, Pallas kernels for 0%

profile of v2, /device:TPU:0, one launch (start us, length us, event | category | flops | bytes accessed | tf_op | source)
XLA Modules:
  0.0 209.9 jit_solution(7159608413072404632)
XLA Ops:
  0.0 5.1 %collective-permute-start.1 = (bf16[128,8,128]{2,1,0:T(8,128)(2,1)}, bf16[128,8,128]{2,1,0:T(8,128)(2,1)S(1)}, u32[]{:S(2)}, u32[]{:S(2)}) collective-permute-start(bf16[128,8,128]{2,1,0:T(8,128)(2,1)} %bitcast.51), channel_id=1, source_target_pairs={{0,24},{4,28},{8,16},{12,20},{16,8},{20,12},{24,0},{28,4},{1,25},{... | collective-permute-start | bytes 786440 | tf_op jit(solution)/shard_map/ppermute | solution.py:200
  5.1 0.8 select_reduce_fusion
  5.9 0.6 broadcast_in_dim.18
  6.5 3.8 %all-to-all-start = ((s32[16,1,128]{2,1,0:T(1,128)}), s32[16,1,128]{2,1,0:T(1,128)S(1)}, u32[]{:S(2)}, u32[]{:S(2)}) async-start(s32[16,1,128]{2,1,0:T(1,128)} %broadcast_in_dim.18), calls=%async_computation | async-start | bytes 16384 | tf_op jit(solution)/shard_map/all_to_all | solution.py:212
  10.3 1.6 collective-permute-start
  11.9 0.9 copy.17
  12.8 0.6 copy.28
  13.4 2.6 %collective-permute-done = s32[4,128]{1,0:T(4,128)S(1)} collective-permute-done((s32[4,128]{1,0:T(4,128)}, s32[4,128]{1,0:T(4,128)S(1)}, u32[]{:S(2)}, u32[]{:S(2)}) %collective-permute-start) | collective-permute-done | bytes 2080 | tf_op jit(solution)/shard_map/ppermute | solution.py:202
  16.1 1.3 add_select_fusion.live
  17.4 0.0 all-to-all-done
  17.4 0.0 copy-start.1
  17.4 0.0 collective-permute-done.1.refs_1_
  17.4 0.0 copy-start
  17.5 0.6 copy-done.1
  18.0 0.1 copy-done
  18.2 4.5 %pick_0.1 = bf16[16,17,2,8,128]{4,3,2,1,0:T(8,128)(2,1)} custom-call(s32[1]{0:T(128)} %bitcast.where, s32[4,2,512]{2,1,0:T(2,128)} %bitcast.47, s32[16,4]{1,0:T(8,128)} %bitcast.53, s32[2,4,128]{2,1,0:T(4,128)} %add_select_fusion.live, bf16[128,8,128]{2,1,0:T(8,128)(2,1)} %bitcast.52, bf16[128,8,128]{2,1,0:T(8,128)(2,1)} %copy-done), custom_call_target="tpu_custom_call" | custom-call | tf_op jit(solution)/shard_map/pick_0/pallas_call | solution.py:73
  22.7 21.2 %all_to_all.45 = bf16[16,17,2,8,128]{4,3,2,1,0:T(8,128)(2,1)} all-to-all(bf16[16,17,2,8,128]{4,3,2,1,0:T(8,128)(2,1)} %pick_0.1), channel_id=1, replica_groups=mesh['half'=2,'pair'=2,'rest'=2,'gy'=4] {'pair','rest','gy'}, dimensions={0} | all-to-all | bytes 2228224 | tf_op jit(solution)/shard_map/all_to_all | solution.py:223
  43.9 4.8 %multiply_0.1 = bf16[2,2,2,16,2,8,128]{6,5,4,3,2,1,0:T(8,128)(2,1)} custom-call(s32[1]{0:T(128)} %bitcast.where, s32[4,16]{1,0:T(4,128)} %bitcast.60, bf16[4,4,17,2,8,128]{5,4,3,2,1,0:T(8,128)(2,1)} %bitcast.33, bf16[4,4,17,2,8,128]{5,4,3,2,1,0:T(8,128)(2,1)} %bitcast.34, bf16[4,1,16,8,128,128]{5,4,3,2,1,0:T(8,128)(2,1)} %w_any.7, ...), custom_call_target="tpu_custom_call" | custom-call | tf_op jit(solution)/shard_map/multiply_0/pallas_call | solution.py:151
  48.7 18.8 %all_to_all.46 = bf16[8,16,2,8,128]{4,3,2,1,0:T(8,128)(2,1)} all-to-all(bf16[8,16,2,8,128]{4,3,2,1,0:T(8,128)(2,1)} %bitcast.39), channel_id=1, replica_groups=mesh['half'=2,'pair'=2,'rest'=2,'gy'=4] {'half','pair','rest'}, dimensions={0} | all-to-all | bytes 1048576 | tf_op jit(solution)/shard_map/all_to_all | solution.py:227
  67.5 4.6 %pick_1.1 = bf16[16,17,2,8,128]{4,3,2,1,0:T(8,128)(2,1)} custom-call(s32[1]{0:T(128)} %bitcast.where, s32[4,2,512]{2,1,0:T(2,128)} %bitcast.48, s32[16,4]{1,0:T(8,128)} %bitcast.54, s32[2,4,128]{2,1,0:T(4,128)} %add_select_fusion.live, bf16[128,2,8,128]{3,2,1,0:T(8,128)(2,1)} %bitcast.43), custom_call_target="tpu_custom_call" | custom-call | tf_op jit(solution)/shard_map/pick_1/pallas_call | solution.py:73
  72.1 21.2 %all_to_all.47 = bf16[16,17,2,8,128]{4,3,2,1,0:T(8,128)(2,1)} all-to-all(bf16[16,17,2,8,128]{4,3,2,1,0:T(8,128)(2,1)} %pick_1.1), channel_id=1, replica_groups=mesh['half'=2,'pair'=2,'rest'=2,'gy'=4] {'pair','rest','gy'}, dimensions={0} | all-to-all | bytes 2228224 | tf_op jit(solution)/shard_map/all_to_all | solution.py:223
  93.3 4.8 %multiply_1.1 = bf16[2,2,2,16,2,8,128]{6,5,4,3,2,1,0:T(8,128)(2,1)} custom-call(s32[1]{0:T(128)} %bitcast.where, s32[4,16]{1,0:T(4,128)} %bitcast.61, bf16[4,4,17,2,8,128]{5,4,3,2,1,0:T(8,128)(2,1)} %bitcast.35, bf16[4,4,17,2,8,128]{5,4,3,2,1,0:T(8,128)(2,1)} %bitcast.36, bf16[4,1,16,8,128,128]{5,4,3,2,1,0:T(8,128)(2,1)} %w_any.7, ...), custom_call_target="tpu_custom_call" | custom-call | tf_op jit(solution)/shard_map/multiply_1/pallas_call | solution.py:151
  98.1 18.8 %all_to_all.48 = bf16[8,16,2,8,128]{4,3,2,1,0:T(8,128)(2,1)} all-to-all(bf16[8,16,2,8,128]{4,3,2,1,0:T(8,128)(2,1)} %bitcast.40), channel_id=1, replica_groups=mesh['half'=2,'pair'=2,'rest'=2,'gy'=4] {'half','pair','rest'}, dimensions={0} | all-to-all | bytes 1048576 | tf_op jit(solution)/shard_map/all_to_all | solution.py:227
  116.9 4.6 %pick_2.1 = bf16[16,17,2,8,128]{4,3,2,1,0:T(8,128)(2,1)} custom-call(s32[1]{0:T(128)} %bitcast.where, s32[4,2,512]{2,1,0:T(2,128)} %bitcast.49, s32[16,4]{1,0:T(8,128)} %bitcast.55, s32[2,4,128]{2,1,0:T(4,128)} %add_select_fusion.live, bf16[128,2,8,128]{3,2,1,0:T(8,128)(2,1)} %bitcast.44), custom_call_target="tpu_custom_call" | custom-call | tf_op jit(solution)/shard_map/pick_2/pallas_call | solution.py:73
  121.5 21.2 %all_to_all.49 = bf16[16,17,2,8,128]{4,3,2,1,0:T(8,128)(2,1)} all-to-all(bf16[16,17,2,8,128]{4,3,2,1,0:T(8,128)(2,1)} %pick_2.1), channel_id=1, replica_groups=mesh['half'=2,'pair'=2,'rest'=2,'gy'=4] {'pair','rest','gy'}, dimensions={0} | all-to-all | bytes 2228224 | tf_op jit(solution)/shard_map/all_to_all | solution.py:223
  142.7 4.8 %multiply_2.1 = bf16[2,2,2,16,2,8,128]{6,5,4,3,2,1,0:T(8,128)(2,1)} custom-call(s32[1]{0:T(128)} %bitcast.where, s32[4,16]{1,0:T(4,128)} %bitcast.62, bf16[4,4,17,2,8,128]{5,4,3,2,1,0:T(8,128)(2,1)} %bitcast.37, bf16[4,4,17,2,8,128]{5,4,3,2,1,0:T(8,128)(2,1)} %bitcast.38, bf16[4,1,16,8,128,128]{5,4,3,2,1,0:T(8,128)(2,1)} %w_any.7, ...), custom_call_target="tpu_custom_call" | custom-call | tf_op jit(solution)/shard_map/multiply_2/pallas_call | solution.py:151
  147.5 18.8 %all_to_all.50 = bf16[8,16,2,8,128]{4,3,2,1,0:T(8,128)(2,1)} all-to-all(bf16[8,16,2,8,128]{4,3,2,1,0:T(8,128)(2,1)} %bitcast.41), channel_id=1, replica_groups=mesh['half'=2,'pair'=2,'rest'=2,'gy'=4] {'half','pair','rest'}, dimensions={0} | all-to-all | bytes 1048576 | tf_op jit(solution)/shard_map/all_to_all | solution.py:227
  166.3 4.6 %pick_3.1 = bf16[16,17,2,8,128]{4,3,2,1,0:T(8,128)(2,1)} custom-call(s32[1]{0:T(128)} %bitcast.where, s32[4,2,512]{2,1,0:T(2,128)} %bitcast.50, s32[16,4]{1,0:T(8,128)} %bitcast.56, s32[2,4,128]{2,1,0:T(4,128)} %add_select_fusion.live, bf16[128,2,8,128]{3,2,1,0:T(8,128)(2,1)} %bitcast.42), custom_call_target="tpu_custom_call" | custom-call | tf_op jit(solution)/shard_map/pick_3/pallas_call | solution.py:73
  170.9 21.2 %all_to_all.51 = bf16[16,17,2,8,128]{4,3,2,1,0:T(8,128)(2,1)} all-to-all(bf16[16,17,2,8,128]{4,3,2,1,0:T(8,128)(2,1)} %pick_3.1), channel_id=1, replica_groups=mesh['half'=2,'pair'=2,'rest'=2,'gy'=4] {'pair','rest','gy'}, dimensions={0} | all-to-all | bytes 2228224 | tf_op jit(solution)/shard_map/all_to_all | solution.py:223
  192.1 4.7 %multiply_3.1 = bf16[2,2,2,16,8,128]{5,4,3,2,1,0:T(8,128)(2,1)} custom-call(s32[1]{0:T(128)} %bitcast.where, s32[4,16]{1,0:T(4,128)} %bitcast.63, bf16[4,4,17,2,8,128]{5,4,3,2,1,0:T(8,128)(2,1)} %bitcast.31, bf16[4,4,17,2,8,128]{5,4,3,2,1,0:T(8,128)(2,1)} %bitcast.32, bf16[4,1,16,8,128,128]{5,4,3,2,1,0:T(8,128)(2,1)} %w_any.7, ...), custom_call_target="tpu_custom_call" | custom-call | tf_op jit(solution)/shard_map/multiply_3/pallas_call | solution.py:151
  196.8 12.5 %all_to_all.52 = bf16[8,16,8,128]{3,2,1,0:T(8,128)(2,1)S(1)} all-to-all(bf16[8,16,8,128]{3,2,1,0:T(8,128)(2,1)} %bitcast.45), channel_id=1, replica_groups=mesh['half'=2,'pair'=2,'rest'=2,'gy'=4] {'half','pair','rest'}, dimensions={0} | all-to-all | bytes 524288 | tf_op jit(solution)/shard_map/all_to_all | solution.py:227
  209.2 0.7 copy.30
  (2 shorter events, 0.0 us)
Async XLA Ops:
  0.0 17.4 %collective-permute-start.1 = (bf16[128,8,128]{2,1,0:T(8,128)(2,1)}, bf16[128,8,128]{2,1,0:T(8,128)(2,1)S(1)}, u32[]{:S(2)}, u32[]{:S(2)}) collective-permute-start(bf16[128,8,128]{2,1,0:T(8,128)(2,1)} %bitcast.51), channel_id=1, source_target_pairs={{0,24},{4,28},{8,16},{12,20},{16,8},{20,12},{24,0},{28,4},{1,25},{... | collective-permute-start | bytes 786440 | tf_op jit(solution)/shard_map/ppermute | solution.py:200
  6.5 10.9 %all-to-all-start = ((s32[16,1,128]{2,1,0:T(1,128)}), s32[16,1,128]{2,1,0:T(1,128)S(1)}, u32[]{:S(2)}, u32[]{:S(2)}) async-start(s32[16,1,128]{2,1,0:T(1,128)} %broadcast_in_dim.18), calls=%async_computation | async-start | bytes 16384 | tf_op jit(solution)/shard_map/all_to_all | solution.py:212
  10.3 5.8 %collective-permute-start = (s32[4,128]{1,0:T(4,128)}, s32[4,128]{1,0:T(4,128)S(1)}, u32[]{:S(2)}, u32[]{:S(2)}) collective-permute-start(s32[4,128]{1,0:T(4,128)} %bitcast.64), channel_id=1, source_target_pairs={{0,24},{4,28},{8,16},{12,20},{16,8},{20,12},{24,0},{28,4},{1,25},{... | collective-permute-start | bytes 6152 | tf_op jit(solution)/shard_map/ppermute | solution.py:202
  17.4 0.6 copy-start.1
  17.4 0.7 copy-start

commit v3 on v2

--- a/solution.py
+++ b/solution.py
@@ -12,69 +12,64 @@
 FETCH_OVER = (PAIR, REST, GROUP)
 
 
-def pick_kernel(layer, owned, groups, where, table, heavy, live, *refs):
+def pick_kernel(
+    layer, layers, owned, groups, where, table, heavy, live_own, live_partner, *refs
+):
     *state_refs, out_ref, kept_ref = refs
     step = pl.program_id(0)
     blocks = kept_ref.shape[0]
     dests = out_ref.shape[0]
     half = where[0]
+    batch = 8
+
+    def masked(alive, tile):
+        return jnp.where(alive > 0, tile, jnp.zeros_like(tile))
 
     @pl.when(step == 0)
     def _():
-        if len(state_refs) == 2:
-            own_ref, partner_ref = state_refs
-
-            def mask(i, carry):
-                own = own_ref[i]
-                partner = partner_ref[i]
-                kept_ref[i, half] = jnp.where(live[half, layer, i] > 0, own, jnp.zeros_like(own))
-                kept_ref[i, 1 - half] = jnp.where(
-                    live[1 - half, layer, i] > 0, partner, jnp.zeros_like(own)
-                )
-                return carry
-
-            lax.fori_loop(0, blocks, mask, 0, unroll=8)
-        else:
-            (state_ref,) = state_refs
-            batch = 8
-
-            def mask(b, carry):
-                pieces = []
-                for i in range(batch):
-                    for h in range(2):
-                        tile = state_ref[b * batch + i, h]
-                        alive = live[h, layer, b * batch + i] > 0
-                        pieces.append(jnp.where(alive, tile, jnp.zeros_like(tile)))
-                for i in range(batch):
-                    for h in range(2):
-                        kept_ref[b * batch + i, h] = pieces[2 * i + h]
-                return carry
-
-            lax.fori_loop(0, blocks // batch, mask, 0)
-
-    def one_dest(d, carry):
-        dest = step * dests + d
-        owner = half * (dests * pl.num_programs(0) // groups) + dest // groups
-        first = (dest % groups) * blocks + owner * owned
-        spots = [table[layer, 0, first + k] for k in range(owned)]
-        spots.append(table[layer, 1, first + heavy[dest, layer]])
-        pieces = [kept_ref[spot] for spot in spots]
-        for k, piece in enumerate(pieces):
-            out_ref[d, k] = piece
+        def mask(b, carry):
+            first = b * batch
+            own, partner = [], []
+            for i in range(batch):
+                if len(state_refs) == 2:
+                    mine, other = state_refs[0][first + i], state_refs[1][first + i]
+                else:
+                    mine = state_refs[0][first + i, half]
+                    other = state_refs[0][first + i, 1 - half]
+                own.append(masked(live_own[layer * blocks + first + i], mine))
+                partner.append(masked(live_partner[layer * blocks + first + i], other))
+            for i in range(batch):
+                kept_ref[first + i, half] = own[i]
+                kept_ref[first + i, 1 - half] = partner[i]
+            return carry
+
+        lax.fori_loop(0, blocks // batch, mask, 0)
+
+    across = dests * pl.num_programs(0) // groups
+    slots = table.shape[0] // (2 * layers)
+
+    def one_owner(o, carry):
+        owner = step * (dests // groups) + o
+        for g in range(groups):
+            first = 2 * layer * slots + g * blocks + (half * across + owner) * owned
+            spots = [table[first + k] for k in range(owned)]
+            spots.append(table[first + slots + heavy[owner * groups + g, layer]])
+            for k, spot in enumerate(spots):
+                out_ref[o * groups + g, k] = kept_ref[spot]
         return carry
 
-    lax.fori_loop(0, dests, one_dest, 0)
-
-
-def pick(layer, owned, groups, where, table, heavy, live, states):
+    lax.fori_loop(0, dests // groups, one_owner, 0)
+
+
+def pick(layer, layers, owned, groups, where, table, heavy, live_own, live_partner, states):
     blocks, (rows, side) = states[0].shape[0], states[0].shape[-2:]
     devices = heavy.shape[0]
     steps = 2
     return pl.pallas_call(
-        functools.partial(pick_kernel, layer, owned, groups),
+        functools.partial(pick_kernel, layer, layers, owned, groups),
         out_shape=jax.ShapeDtypeStruct((devices, owned + 1, 2, rows, side), states[0].dtype),
         grid_spec=pltpu.PrefetchScalarGridSpec(
-            num_scalar_prefetch=4,
+            num_scalar_prefetch=5,
             grid=(steps,),
             in_specs=[
                 pl.BlockSpec(state.shape, lambda i, *_, n=state.ndim: (0,) * n) for state in states
@@ -84,14 +79,16 @@
             ),
             scratch_shapes=[pltpu.VMEM((blocks, 2, rows, side), states[0].dtype)],
         ),
+        compiler_params=pltpu.CompilerParams(vmem_limit_bytes=6 << 20),
         name=f"pick_{layer}",
-    )(where, table, heavy, live, *states)
+    )(where, table, heavy, live_own, live_partner, *states)
 
 
 def multiply_kernel(
-    layer, last, where, counts, x_ref, rest_ref, w_ref, w_any, bias_ref, out_ref, acc_ref, wrest_ref, sem
+    layer, last, where, counts, x_ref, rest_ref, w_hbm, bias_ref, out_ref, acc_ref, w_ref, wrest_ref, sems
 ):
     step = pl.program_id(0)
+    steps = w_ref.shape[0]
     across, groups, chunk, _, rows, side = x_ref.shape
     owned = counts.shape[1]
     total_rows = across * 2 * rows
@@ -99,11 +96,21 @@
     heavy = jnp.int32(0)
     for k in range(owned):
         heavy = jnp.where(counts[layer, k] > groups, k, heavy)
-    copy = pltpu.make_async_copy(w_any.at[layer, 0, heavy, pl.ds(groups, groups)], wrest_ref, sem)
+
+    def fetch(i):
+        return pltpu.make_async_copy(
+            w_hbm.at[layer, 0, pl.ds(i * chunk, chunk), pl.ds(0, groups)], w_ref.at[i], sems.at[i]
+        )
+
+    fetch_rest = pltpu.make_async_copy(
+        w_hbm.at[layer, 0, heavy, pl.ds(groups, groups)], wrest_ref, sems.at[steps]
+    )
 
     @pl.when(step == 0)
     def _():
-        copy.start()
+        for i in range(steps):
+            fetch(i).start()
+        fetch_rest.start()
 
     def gathered(ref, position, first, count):
         parts = []
@@ -125,18 +132,19 @@
         out_ref[1 - half, 0, :, k] = far[1]
         out_ref[1 - half, 1, :, k] = far[0]
 
+    fetch(step).wait()
     for c in range(chunk):
         k = step * chunk + c
         lhs = gathered(x_ref, c, 0, counts[layer, k])
-        weight = w_ref[0, 0, c].reshape(groups * side, side)
+        weight = w_ref[step, c].reshape(groups * side, side)
         summed = jnp.dot(lhs, weight, preferred_element_type=jnp.float32)
         summed = summed + bias_ref[0, 0, pl.ds(k, 1), :]
         acc_ref[k] = summed
         write(k, summed)
 
-    @pl.when(step == pl.num_programs(0) - 1)
+    @pl.when(step == steps - 1)
     def _():
-        copy.wait()
+        fetch_rest.wait()
         lhs = gathered(rest_ref, 0, groups, counts[layer, heavy])
         weight = wrest_ref[...].reshape(groups * side, side)
         write(heavy, acc_ref[heavy] + jnp.dot(lhs, weight, preferred_element_type=jnp.float32))
@@ -161,21 +169,20 @@
                 pl.BlockSpec(
                     (across, groups, 1, 2, rows, side), lambda i, *_: (0, 0, owned, 0, 0, 0)
                 ),
-                pl.BlockSpec(
-                    (1, 1, chunk, groups, side, side), lambda i, *_: (layer, 0, i, 0, 0, 0)
-                ),
                 pl.BlockSpec(memory_space=pl.ANY),
                 pl.BlockSpec((1, 1, owned, side), lambda i, *_: (layer, 0, 0, 0)),
             ],
             out_specs=pl.BlockSpec(out, lambda i, *_: (0,) * len(out)),
             scratch_shapes=[
                 pltpu.VMEM((owned, across * 2 * rows, side), jnp.float32),
+                pltpu.VMEM((steps, chunk, groups, side, side), weight_tiles.dtype),
                 pltpu.VMEM((groups, side, side), weight_tiles.dtype),
-                pltpu.SemaphoreType.DMA,
+                pltpu.SemaphoreType.DMA((steps + 1,)),
             ],
         ),
+        compiler_params=pltpu.CompilerParams(vmem_limit_bytes=50 << 20),
         name=f"multiply_{layer}",
-    )(where, counts, incoming, incoming, weight_tiles, weight_tiles, bias_terms)
+    )(where, counts, incoming, incoming, weight_tiles, bias_terms)
 
 
 def local(activations, live_blocks, tile_index, tile_count, weight_tiles, bias_terms):
@@ -198,11 +205,8 @@
 
     own = jnp.transpose(activations.reshape(rows, blocks, side), (1, 0, 2))
     partner = lax.ppermute(own, ROWS_OVER, partners)
-    live_own = live_blocks[:, 0]
-    live_partner = lax.ppermute(live_own, ROWS_OVER, partners)
-    live = jnp.where(
-        my_half == 0, jnp.stack([live_own, live_partner]), jnp.stack([live_partner, live_own])
-    )
+    live_own = live_blocks[:, 0].reshape(-1)
+    live_partner = lax.ppermute(live_blocks[:, 0], ROWS_OVER, partners).reshape(-1)
     where = my_half.reshape(1)
 
     counts = tile_count[:, 0]
@@ -215,11 +219,14 @@
 
     slots = jnp.transpose(tile_index, (0, 2, 1)).reshape(layers, -1, groups, tile_index.shape[1])
     table = lax.dynamic_index_in_dim(slots, my_group, 2, keepdims=False) - my_group * blocks
+    table = table.reshape(-1)
 
     states = [own, partner]
     for layer in range(layers):
         last = layer == layers - 1
-        outgoing = pick(layer, owned, groups, where, table, heavy_all, live, states)
+        outgoing = pick(
+            layer, layers, owned, groups, where, table, heavy_all, live_own, live_partner, states
+        )
         incoming = lax.all_to_all(outgoing, FETCH_OVER, 0, 0, tiled=True)
         incoming = incoming.reshape(2 * rest, groups, owned + 1, 2, rows, side)
         result = multiply(layer, last, where, counts, incoming, weight_tiles, bias_terms)

time: 212 us -> 182 us (0.86)
  Pallas kernels: 37.2 us -> 19.8 us
  blocking collectives: 154 us -> 143 us
    pallas_call x4, Pallas kernels: 18.3 us -> 7.23 us  [pick(): pl.pallas_call(functools.partial(pick_kernel, layer, layers, owned, group...]
    pallas_call x4, Pallas kernels: 18.9 us -> 12.5 us  [multiply(): pl.pallas_call(functools.partial(multiply_kernel, layer, last), out_shape...]
    all_to_all x4, blocking collectives: 68.9 us -> 63.4 us  [local(): returned = lax.all_to_all(result, ROWS_OVER, 0, 0, tiled=True)]
    all_to_all x4, blocking collectives: 84.9 us -> 79.4 us  [local(): incoming = lax.all_to_all(outgoing, FETCH_OVER, 0, 0, tiled=True)]
  transfers between devices with their start and end apart: 3 -> 3, of which waited for: 1 -> 1; matrix products, arithmetic and copies ran while one was open for 2% -> 1% of each run, Pallas kernels for 0% -> 0%
where the time goes in v3:
time: 182 us; the launch traced here: 181 us
  blocking collectives  143 us (79%)
  Pallas kernels  19.8 us (11%)
  starting transfers between devices  10.5 us (6%)
  local copies, waits for them, and re-layouts  3.82 us (2%)
  waiting for transfers between devices  3.28 us (2%)
    all_to_all x4, blocking collectives, local(): incoming = lax.all_to_all(outgoing, FETCH_OVER, 0, 0, tiled=True)  79.4 us
    all_to_all x4, blocking collectives, local(): returned = lax.all_to_all(result, ROWS_OVER, 0, 0, tiled=True)  63.4 us
    pallas_call x4, Pallas kernels, multiply(): pl.pallas_call(functools.partial(multiply_kernel, layer, last), out_shape...  12.5 us
    pallas_call x4, Pallas kernels, pick(): pl.pallas_call(functools.partial(pick_kernel, layer, layers, owned, group...  7.23 us
    ppermute x1, starting transfers between devices, local(): partner = lax.ppermute(own, ROWS_OVER, partners)  5.08 us
    all_to_all x1, starting transfers between devices, local(): lax.all_to_all(jnp.broadcast_to(heavy, (devices, 1, side)), FETCH_OVER, 0...  3.83 us
  transfers between devices with their start and end apart: 3, of which 1 were waited for; matrix products, arithmetic and copies ran while one was open for 1% of the time, Pallas kernels for 0%

profile of v3, /device:TPU:0, one launch (start us, length us, event | category | flops | bytes accessed | tf_op | source)
XLA Modules:
  0.0 181.1 jit_solution(15859656761630009043)
XLA Ops:
  0.0 5.1 %collective-permute-start.1 = (bf16[128,8,128]{2,1,0:T(8,128)(2,1)}, bf16[128,8,128]{2,1,0:T(8,128)(2,1)S(1)}, u32[]{:S(2)}, u32[]{:S(2)}) collective-permute-start(bf16[128,8,128]{2,1,0:T(8,128)(2,1)} %bitcast.47), channel_id=1, source_target_pairs={{0,24},{4,28},{8,16},{12,20},{16,8},{20,12},{24,0},{28,4},{1,25},{... | collective-permute-start | bytes 786440 | tf_op jit(solution)/shard_map/ppermute | solution.py:207
  5.1 0.8 select_reduce_fusion
  5.9 0.6 broadcast_in_dim.18
  6.5 3.8 %all-to-all-start = ((s32[16,1,128]{2,1,0:T(1,128)}), s32[16,1,128]{2,1,0:T(1,128)S(1)}, u32[]{:S(2)}, u32[]{:S(2)}) async-start(s32[16,1,128]{2,1,0:T(1,128)} %broadcast_in_dim.18), calls=%async_computation | async-start | bytes 16384 | tf_op jit(solution)/shard_map/all_to_all | solution.py:216
  10.3 1.6 collective-permute-start
  11.9 0.9 reshape.56
  12.8 3.3 %collective-permute-done = s32[4,128]{1,0:T(4,128)S(1)} collective-permute-done((s32[4,128]{1,0:T(4,128)}, s32[4,128]{1,0:T(4,128)S(1)}, u32[]{:S(2)}, u32[]{:S(2)}) %collective-permute-start) | collective-permute-done | bytes 2080 | tf_op jit(solution)/shard_map/ppermute | solution.py:209
  16.1 0.0 all-to-all-done
  16.1 0.0 collective-permute-done.1.refs_1_
  16.1 0.0 copy-start.1
  16.1 0.9 copy-done.1
  17.0 0.0 copy-start.3
  17.0 0.7 copy-done.3
  17.7 1.8 pick_0.1
  19.5 0.0 copy-start
  19.5 0.0 copy-start.2
  19.6 20.8 %all_to_all.45 = bf16[16,17,2,8,128]{4,3,2,1,0:T(8,128)(2,1)S(1)} all-to-all(bf16[16,17,2,8,128]{4,3,2,1,0:T(8,128)(2,1)S(1)} %pick_0.1), channel_id=1, replica_groups=mesh['half'=2,'pair'=2,'rest'=2,'gy'=4] {'pair','rest','gy'}, dimensions={0} | all-to-all | bytes 2228224 | tf_op jit(solution)/shard_map/all_to_all | solution.py:230
  40.4 0.0 copy-done
  40.4 0.0 copy-done.2
  40.4 0.0 copy-start.4
  40.4 3.1 %multiply_0.1 = bf16[2,2,2,16,2,8,128]{6,5,4,3,2,1,0:T(8,128)(2,1)S(1)} custom-call(s32[1]{0:T(128)} %bitcast.where, s32[4,16]{1,0:T(4,128)S(1)} %bitcast.54, bf16[4,4,17,2,8,128]{5,4,3,2,1,0:T(8,128)(2,1)S(1)} %bitcast.30, bf16[4,4,17,2,8,128]{5,4,3,2,1,0:T(8,128)(2,1)S(1)} %bitcast.31, bf16[4,1,16,8,128,128]{5,4,3,2,1,0:T(8,128)(2,1)} %w_hbm.7, ...), custom_call_target="tpu_custom_call" | custom-call | tf_op jit(solution)/shard_map/multiply_0/pallas_call | solution.py:159
  43.5 17.3 %all_to_all.46 = bf16[8,16,2,8,128]{4,3,2,1,0:T(8,128)(2,1)S(1)} all-to-all(bf16[8,16,2,8,128]{4,3,2,1,0:T(8,128)(2,1)S(1)} %bitcast.36), channel_id=1, replica_groups=mesh['half'=2,'pair'=2,'rest'=2,'gy'=4] {'half','pair','rest'}, dimensions={0} | all-to-all | bytes 1048576 | tf_op jit(solution)/shard_map/all_to_all | solution.py:234
  60.9 0.0 copy-done.4
  60.9 1.8 pick_1.1
  62.7 19.5 %all_to_all.47 = bf16[16,17,2,8,128]{4,3,2,1,0:T(8,128)(2,1)S(1)} all-to-all(bf16[16,17,2,8,128]{4,3,2,1,0:T(8,128)(2,1)S(1)} %pick_1.1), channel_id=1, replica_groups=mesh['half'=2,'pair'=2,'rest'=2,'gy'=4] {'pair','rest','gy'}, dimensions={0} | all-to-all | bytes 2228224 | tf_op jit(solution)/shard_map/all_to_all | solution.py:230
  82.2 3.1 %multiply_1.1 = bf16[2,2,2,16,2,8,128]{6,5,4,3,2,1,0:T(8,128)(2,1)S(1)} custom-call(s32[1]{0:T(128)} %bitcast.where, s32[4,16]{1,0:T(4,128)S(1)} %bitcast.55, bf16[4,4,17,2,8,128]{5,4,3,2,1,0:T(8,128)(2,1)S(1)} %bitcast.32, bf16[4,4,17,2,8,128]{5,4,3,2,1,0:T(8,128)(2,1)S(1)} %bitcast.33, bf16[4,1,16,8,128,128]{5,4,3,2,1,0:T(8,128)(2,1)} %w_hbm.7, ...), custom_call_target="tpu_custom_call" | custom-call | tf_op jit(solution)/shard_map/multiply_1/pallas_call | solution.py:159
  85.4 17.2 %all_to_all.48 = bf16[8,16,2,8,128]{4,3,2,1,0:T(8,128)(2,1)S(1)} all-to-all(bf16[8,16,2,8,128]{4,3,2,1,0:T(8,128)(2,1)S(1)} %bitcast.37), channel_id=1, replica_groups=mesh['half'=2,'pair'=2,'rest'=2,'gy'=4] {'half','pair','rest'}, dimensions={0} | all-to-all | bytes 1048576 | tf_op jit(solution)/shard_map/all_to_all | solution.py:234
  102.6 1.8 pick_2.1
  104.4 19.5 %all_to_all.49 = bf16[16,17,2,8,128]{4,3,2,1,0:T(8,128)(2,1)S(1)} all-to-all(bf16[16,17,2,8,128]{4,3,2,1,0:T(8,128)(2,1)S(1)} %pick_2.1), channel_id=1, replica_groups=mesh['half'=2,'pair'=2,'rest'=2,'gy'=4] {'pair','rest','gy'}, dimensions={0} | all-to-all | bytes 2228224 | tf_op jit(solution)/shard_map/all_to_all | solution.py:230
  123.9 3.1 %multiply_2.1 = bf16[2,2,2,16,2,8,128]{6,5,4,3,2,1,0:T(8,128)(2,1)S(1)} custom-call(s32[1]{0:T(128)} %bitcast.where, s32[4,16]{1,0:T(4,128)S(1)} %bitcast.56, bf16[4,4,17,2,8,128]{5,4,3,2,1,0:T(8,128)(2,1)S(1)} %bitcast.34, bf16[4,4,17,2,8,128]{5,4,3,2,1,0:T(8,128)(2,1)S(1)} %bitcast.35, bf16[4,1,16,8,128,128]{5,4,3,2,1,0:T(8,128)(2,1)} %w_hbm.7, ...), custom_call_target="tpu_custom_call" | custom-call | tf_op jit(solution)/shard_map/multiply_2/pallas_call | solution.py:159
  127.1 17.2 %all_to_all.50 = bf16[8,16,2,8,128]{4,3,2,1,0:T(8,128)(2,1)S(1)} all-to-all(bf16[8,16,2,8,128]{4,3,2,1,0:T(8,128)(2,1)S(1)} %bitcast.38), channel_id=1, replica_groups=mesh['half'=2,'pair'=2,'rest'=2,'gy'=4] {'half','pair','rest'}, dimensions={0} | all-to-all | bytes 1048576 | tf_op jit(solution)/shard_map/all_to_all | solution.py:234
  144.3 1.8 pick_3.1
  146.1 19.5 %all_to_all.51 = bf16[16,17,2,8,128]{4,3,2,1,0:T(8,128)(2,1)S(1)} all-to-all(bf16[16,17,2,8,128]{4,3,2,1,0:T(8,128)(2,1)S(1)} %pick_3.1), channel_id=1, replica_groups=mesh['half'=2,'pair'=2,'rest'=2,'gy'=4] {'pair','rest','gy'}, dimensions={0} | all-to-all | bytes 2228224 | tf_op jit(solution)/shard_map/all_to_all | solution.py:230
  165.6 3.1 %multiply_3.1 = bf16[2,2,2,16,8,128]{5,4,3,2,1,0:T(8,128)(2,1)S(1)} custom-call(s32[1]{0:T(128)} %bitcast.where, s32[4,16]{1,0:T(4,128)S(1)} %bitcast.57, bf16[4,4,17,2,8,128]{5,4,3,2,1,0:T(8,128)(2,1)S(1)} %bitcast.28, bf16[4,4,17,2,8,128]{5,4,3,2,1,0:T(8,128)(2,1)S(1)} %bitcast.29, bf16[4,1,16,8,128,128]{5,4,3,2,1,0:T(8,128)(2,1)} %w_hbm.7, ...), custom_call_target="tpu_custom_call" | custom-call | tf_op jit(solution)/shard_map/multiply_3/pallas_call | solution.py:159
  168.8 11.6 %all_to_all.52 = bf16[8,16,8,128]{3,2,1,0:T(8,128)(2,1)S(1)} all-to-all(bf16[8,16,8,128]{3,2,1,0:T(8,128)(2,1)S(1)} %bitcast.42), channel_id=1, replica_groups=mesh['half'=2,'pair'=2,'rest'=2,'gy'=4] {'half','pair','rest'}, dimensions={0} | all-to-all | bytes 524288 | tf_op jit(solution)/shard_map/all_to_all | solution.py:234
  180.4 0.7 copy.18
  (2 shorter events, 0.0 us)
Async XLA Ops:
  0.0 16.1 %collective-permute-start.1 = (bf16[128,8,128]{2,1,0:T(8,128)(2,1)}, bf16[128,8,128]{2,1,0:T(8,128)(2,1)S(1)}, u32[]{:S(2)}, u32[]{:S(2)}) collective-permute-start(bf16[128,8,128]{2,1,0:T(8,128)(2,1)} %bitcast.47), channel_id=1, source_target_pairs={{0,24},{4,28},{8,16},{12,20},{16,8},{20,12},{24,0},{28,4},{1,25},{... | collective-permute-start | bytes 786440 | tf_op jit(solution)/shard_map/ppermute | solution.py:207
  6.5 9.6 %all-to-all-start = ((s32[16,1,128]{2,1,0:T(1,128)}), s32[16,1,128]{2,1,0:T(1,128)S(1)}, u32[]{:S(2)}, u32[]{:S(2)}) async-start(s32[16,1,128]{2,1,0:T(1,128)} %broadcast_in_dim.18), calls=%async_computation | async-start | bytes 16384 | tf_op jit(solution)/shard_map/all_to_all | solution.py:216
  10.3 5.8 %collective-permute-start = (s32[4,128]{1,0:T(4,128)}, s32[4,128]{1,0:T(4,128)S(1)}, u32[]{:S(2)}, u32[]{:S(2)}) collective-permute-start(s32[4,128]{1,0:T(4,128)} %bitcast.58), channel_id=1, source_target_pairs={{0,24},{4,28},{8,16},{12,20},{16,8},{20,12},{24,0},{28,4},{1,25},{... | collective-permute-start | bytes 6152 | tf_op jit(solution)/shard_map/ppermute | solution.py:209
  16.1 1.0 copy-start.1
  17.0 0.7 copy-start.3
  19.5 20.9 %copy-start = (f32[4,1,16,128]{3,2,1,0:T(8,128)S(1)}, f32[4,1,16,128]{3,2,1,0:T(8,128)}, u32[]{:S(2)}) copy-start(f32[4,1,16,128]{3,2,1,0:T(8,128)} %bias_ref.7) | copy-start | bytes 98308
  19.5 20.8 %copy-start.2 = (s32[4,1,16]{2,1,0:T(1,128)S(1)}, s32[4,1,16]{2,1,0:T(1,128)}, u32[]{:S(2)}) copy-start(s32[4,1,16]{2,1,0:T(1,128)} %param.9) | copy-start | bytes 772
  40.4 20.5 %copy-start.4 = (s32[4,1,128]{2,1,0:T(1,128)S(1)}, s32[4,1,128]{2,1,0:T(1,128)}, u32[]{:S(2)}) copy-start(s32[4,1,128]{2,1,0:T(1,128)} %param.7) | copy-start | bytes 6148

commit v4 on v3

v4 whole, which is shorter than its diff:
```python
import functools

import jax
import jax.numpy as jnp
from jax import lax
from jax.experimental import pallas as pl
from jax.experimental.pallas import tpu as pltpu
from jax.sharding import Mesh, PartitionSpec as P

HALF, PAIR, REST, GROUP = "half", "pair", "rest", "gy"
ROWS_OVER = (HALF, PAIR, REST)
FETCH_OVER = (PAIR, REST, GROUP)


def masked(alive, tile):
    return jnp.where(alive > 0, tile, jnp.zeros_like(tile))


def prepare_kernel(groups, live, counts, rows_ref, live_ref, sent_ref, heavy_ref):
    layers, blocks = live_ref.shape
    tile = sent_ref.shape[1:]
    batch = 8

    def mask(b, carry):
        first = b * batch
        kept = [masked(live[first + i], rows_ref[first + i]) for i in range(batch)]
        for i in range(batch):
            sent_ref[first + i] = kept[i]
        return carry

    lax.fori_loop(0, blocks // batch, mask, 0)
    masks = live_ref[...].astype(jnp.float32)
    masks = jnp.concatenate([masks, jnp.zeros((tile[0] - layers, tile[1]), jnp.float32)], axis=0)
    sent_ref[blocks] = masks.astype(sent_ref.dtype)

    lane = lax.broadcasted_iota(jnp.int32, heavy_ref.shape[1:], 1)
    found = jnp.zeros_like(lane)
    for layer in range(layers):
        found = jnp.where(lane == layer, heavy_of(counts, layer, groups), found)
    heavy_ref[...] = jnp.broadcast_to(found[None], heavy_ref.shape)


def heavy_of(counts, layer, groups):
    heavy = jnp.int32(0)
    for k in range(counts.shape[1]):
        heavy = jnp.where(counts[layer, k] > groups, k, heavy)
    return heavy


def prepare(groups, devices, live, counts, own):
    blocks, rows, side = own.shape
    return pl.pallas_call(
        functools.partial(prepare_kernel, groups),
        out_shape=(
            jax.ShapeDtypeStruct((blocks + 1, rows, side), own.dtype),
            jax.ShapeDtypeStruct((devices, 1, side), jnp.int32),
        ),
        grid_spec=pltpu.PrefetchScalarGridSpec(
            num_scalar_prefetch=2,
            grid=(1,),
            in_specs=[
                pl.BlockSpec(own.shape, lambda i, *_: (0, 0, 0)),
                pl.BlockSpec(live.shape, lambda i, *_: (0, 0)),
            ],
            out_specs=(
                pl.BlockSpec((blocks + 1, rows, side), lambda i, *_: (0, 0, 0)),
                pl.BlockSpec((devices, 1, side), lambda i, *_: (0, 0, 0)),
            ),
        ),
        compiler_params=pltpu.CompilerParams(vmem_limit_bytes=6 << 20),
        name="prepare",
    )(*(pltpu.with_memory_space_constraint(x, pltpu.HBM) for x in (live.reshape(-1), counts, own, live)))


def pick_kernel(layer, layers, owned, groups, where, table, heavy, *refs):
    step = pl.program_id(0)
    half = where[0]
    if layer == 0:
        own_ref, partner_ref, out_ref, masks_ref = refs
        blocks = own_ref.shape[0] - 1

        @pl.when(step == 0)
        def _():
            masks = partner_ref[blocks].astype(jnp.float32).astype(jnp.int32)
            for i in range(layers):
                masks_ref[i] = masks[i : i + 1]

    else:
        live_own, live_partner, state_ref, out_ref, kept_ref = refs
        blocks = kept_ref.shape[0]
        batch = 8

        @pl.when(step == 0)
        def _():
            def mask(b, carry):
                first = b * batch
                kept = []
                for i in range(batch):
                    spot = layer * blocks + first + i
                    kept.append(masked(live_own[spot], state_ref[first + i, half]))
                    kept.append(masked(live_partner[spot], state_ref[first + i, 1 - half]))
                for i in range(batch):
                    kept_ref[first + i, half] = kept[2 * i]
                    kept_ref[first + i, 1 - half] = kept[2 * i + 1]
                return carry

            lax.fori_loop(0, blocks // batch, mask, 0)

    dests = out_ref.shape[0]
    across = dests * pl.num_programs(0) // groups
    slots = table.shape[0] // (2 * layers)

    def one_owner(o, carry):
        owner = step * (dests // groups) + o
        for g in range(groups):
            first = 2 * layer * slots + g * blocks + (half * across + owner) * owned
            spots = [table[first + k] for k in range(owned)]
            spots.append(table[first + slots + heavy[owner * groups + g, layer]])
            for k, spot in enumerate(spots):
                if layer == 0:
                    out_ref[o * groups + g, k, half] = own_ref[spot]
                    out_ref[o * groups + g, k, 1 - half] = partner_ref[spot]
                else:
                    out_ref[o * groups + g, k] = kept_ref[spot]
        return carry

    lax.fori_loop(0, dests // groups, one_owner, 0)


def pick(layer, layers, owned, groups, tables, states):
    blocks, (rows, side) = states[0].shape[0], states[0].shape[-2:]
    devices = tables[2].shape[0]
    steps = 2
    kept = [] if layer == 0 else [pltpu.VMEM((blocks, 2, rows, side), states[0].dtype)]
    out_shape = [jax.ShapeDtypeStruct((devices, owned + 1, 2, rows, side), states[0].dtype)]
    out_specs = [
        pl.BlockSpec((devices // steps, owned + 1, 2, rows, side), lambda i, *_: (i, 0, 0, 0, 0))
    ]
    if layer == 0:
        out_shape.append(jax.ShapeDtypeStruct((layers, 1, side), jnp.int32))
        out_specs.append(pl.BlockSpec((layers, 1, side), lambda i, *_: (0, 0, 0)))
    return pl.pallas_call(
        functools.partial(pick_kernel, layer, layers, owned, groups),
        out_shape=out_shape,
        grid_spec=pltpu.PrefetchScalarGridSpec(
            num_scalar_prefetch=len(tables),
            grid=(steps,),
            in_specs=[
                pl.BlockSpec(state.shape, lambda i, *_, n=state.ndim: (0,) * n) for state in states
            ],
            out_specs=out_specs,
            scratch_shapes=kept,
        ),
        compiler_params=pltpu.CompilerParams(vmem_limit_bytes=6 << 20),
        name=f"pick_{layer}",
    )(*tables, *states)


def multiply_kernel(
    layer, last, where, counts, x_ref, w_hbm, bias_ref, out_ref, acc_ref, w_ref, wrest_ref, sems
):
    step = pl.program_id(0)
    steps, chunk = w_ref.shape[:2]
    across, groups, _, _, rows, side = x_ref.shape
    owned = counts.shape[1]
    total_rows = across * 2 * rows
    half = where[0]
    heavy = heavy_of(counts, layer, groups)

    def fetch(i):
        return pltpu.make_async_copy(
            w_hbm.at[layer, 0, pl.ds(i * chunk, chunk), pl.ds(0, groups)], w_ref.at[i], sems.at[i]
        )

    fetch_rest = pltpu.make_async_copy(
        w_hbm.at[layer, 0, heavy, pl.ds(groups, groups)], wrest_ref, sems.at[steps]
    )

    @pl.when(step == 0)
    def _():
        for i in range(steps):
            fetch(i).start()
        fetch_rest.start()

    def gathered(position, first, count):
        parts = []
        for g in range(groups):
            part = x_ref[:, g, position].reshape(total_rows, side)
            parts.append(jnp.where(first + g < count, part, jnp.zeros_like(part)))
        return jnp.concatenate(parts, axis=1)

    def write(k, summed):
        value = jnp.maximum(summed, 0.0).astype(out_ref.dtype)
        value = value.reshape(2, across // 2, 2, rows, side)
        if last:
            low, high = value[:, :, 0], value[:, :, 1]
            near = jnp.where(half == 0, low, high)
            far = jnp.where(half == 0, high, low)
        else:
            near = far = value
        out_ref[half, :, :, k] = near
        out_ref[1 - half, 0, :, k] = far[1]
        out_ref[1 - half, 1, :, k] = far[0]

    fetch(step).wait()
    for c in range(chunk):
        k = step * chunk + c
        lhs = gathered(k, 0, counts[layer, k])
        weight = w_ref[step, c].reshape(groups * side, side)
        summed = jnp.dot(lhs, weight, preferred_element_type=jnp.float32)
        summed = summed + bias_ref[0, 0, pl.ds(k, 1), :]
        acc_ref[k] = summed
        write(k, summed)

    @pl.when(step == steps - 1)
    def _():
        fetch_rest.wait()
        lhs = gathered(owned, groups, counts[layer, heavy])
        weight = wrest_ref[...].reshape(groups * side, side)
        write(heavy, acc_ref[heavy] + jnp.dot(lhs, weight, preferred_element_type=jnp.float32))


def multiply(layer, last, where, counts, incoming, weight_tiles, bias_terms):
    across, groups, width, _, rows, side = incoming.shape
    owned = width - 1
    steps = 4 if owned % 4 == 0 else 1
    chunk = owned // steps
    out = (2, 2, across // 2, owned) + (() if last else (2,)) + (rows, side)
    return pl.pallas_call(
        functools.partial(multiply_kernel, layer, last),
        out_shape=jax.ShapeDtypeStruct(out, incoming.dtype),
        grid_spec=pltpu.PrefetchScalarGridSpec(
            num_scalar_prefetch=2,
            grid=(steps,),
            in_specs=[
                pl.BlockSpec(incoming.shape, lambda i, *_: (0,) * incoming.ndim),
                pl.BlockSpec(memory_space=pl.ANY),
                pl.BlockSpec((1, 1, owned, side), lambda i, *_: (layer, 0, 0, 0)),
            ],
            out_specs=pl.BlockSpec(out, lambda i, *_: (0,) * len(out)),
            scratch_shapes=[
                pltpu.VMEM((owned, across * 2 * rows, side), jnp.float32),
                pltpu.VMEM((steps, chunk, groups, side, side), weight_tiles.dtype),
                pltpu.VMEM((groups, side, side), weight_tiles.dtype),
                pltpu.SemaphoreType.DMA((steps + 1,)),
            ],
        ),
        compiler_params=pltpu.CompilerParams(vmem_limit_bytes=50 << 20),
        name=f"multiply_{layer}",
    )(where, counts, incoming, weight_tiles, bias_terms)


def local(activations, live_blocks, tile_index, tile_count, weight_tiles, bias_terms):
    rest = lax.axis_size(REST)
    groups = lax.axis_size(GROUP)
    my_group = lax.axis_index(GROUP)
    my_half = lax.axis_index(HALF)
    layers = tile_index.shape[0]
    rows = activations.shape[0]
    side = weight_tiles.shape[-1]
    owned = weight_tiles.shape[2]
    blocks = activations.shape[1] // side
    devices = 2 * rest * groups
    partners = [
        ((h * 2 + p) * rest + r, ((1 - h) * 2 + 1 - p) * rest + r)
        for h in range(2)
        for p in range(2)
        for r in range(rest)
    ]

    counts = tile_count[:, 0]
    live = live_blocks[:, 0]
    rows_first = jnp.transpose(activations.reshape(rows, blocks, side), (1, 0, 2))
    own, heavy = prepare(groups, devices, live, counts, rows_first)
    partner = lax.ppermute(own, ROWS_OVER, partners)
    heavy = lax.all_to_all(heavy, FETCH_OVER, 0, 0, tiled=True)[:, 0, :layers]
    live_own = live.reshape(-1)
    where = my_half.reshape(1)

    slots = jnp.transpose(tile_index, (0, 2, 1)).reshape(layers, -1, groups, tile_index.shape[1])
    table = lax.dynamic_index_in_dim(slots, my_group, 2, keepdims=False) - my_group * blocks
    table = table.reshape(-1)

    for layer in range(layers):
        last = layer == layers - 1
        if layer == 0:
            tables = (where, table, heavy)
            outgoing, masks = pick(layer, layers, owned, groups, tables, (own, partner))
            live_partner = masks.reshape(-1)
        else:
            tables = (where, table, heavy, live_own, live_partner)
            (outgoing,) = pick(layer, layers, owned, groups, tables, (state,))
        incoming = lax.all_to_all(outgoing, FETCH_OVER, 0, 0, tiled=True)
        incoming = incoming.reshape(2 * rest, groups, owned + 1, 2, rows, side)
        result = multiply(layer, last, where, counts, incoming, weight_tiles, bias_terms)
        result = result.reshape((4 * rest,) + result.shape[3:])
        returned = lax.all_to_all(result, ROWS_OVER, 0, 0, tiled=True)
        state = returned.reshape((blocks,) + returned.shape[2:])
    return jnp.transpose(state, (1, 0, 2)).reshape(rows, blocks * side)


def solution(mesh):
    across, groups = mesh.shape["gx"], mesh.shape["gy"]
    split = Mesh(mesh.devices.reshape(2, 2, across // 4, groups), (HALF, PAIR, REST, GROUP))
    placed = (
        P(ROWS_OVER, GROUP),
        P(None, ROWS_OVER, GROUP),
        P(),
        P(None, GROUP, ROWS_OVER),
        P(None, GROUP, ROWS_OVER, None, None, None),
        P(None, GROUP, ROWS_OVER, None),
    )
    return jax.shard_map(
        local, mesh=split, in_specs=placed, out_specs=P(ROWS_OVER, GROUP), check_vma=False
    )
```

time: 182 us -> 181 us (level)
  local copies, waits for them, and re-layouts: 3.82 us -> 1.58 us
    all_to_all x1, waiting for transfers between devices: 0.01 us -> 4.53 us  [local(): heavy = lax.all_to_all(heavy, FETCH_OVER, 0, 0, tiled=True)[:, 0, :layers]]
    ppermute x1 -> x0, waiting for transfers between devices: 3.27 us -> none  [local(): lax.ppermute(live_blocks[:, 0], ROWS_OVER, partners).reshape(-1)]
    pallas_call x0 -> x1, Pallas kernels: none -> 2.58 us  [prepare(): pl.pallas_call(functools.partial(prepare_kernel, groups), out_shape=(jax....]
  transfers between devices with their start and end apart: 3 -> 2, of which waited for: 1 -> 1; matrix products, arithmetic and copies ran while one was open for 1% -> 0% of each run, Pallas kernels for 0% -> 0%
where the time goes in v4:
time: 181 us; the launch traced here: 180 us
  blocking collectives  144 us (80%)
  Pallas kernels  20.9 us (12%)
  starting transfers between devices  8.9 us (5%)
  waiting for transfers between devices  4.53 us (3%)
    all_to_all x4, blocking collectives, local(): incoming = lax.all_to_all(outgoing, FETCH_OVER, 0, 0, tiled=True)  81 us
    all_to_all x4, blocking collectives, local(): returned = lax.all_to_all(result, ROWS_OVER, 0, 0, tiled=True)  63.4 us
    pallas_call x4, Pallas kernels, multiply(): pl.pallas_call(functools.partial(multiply_kernel, layer, last), out_shape...  11.5 us
    pallas_call x4, Pallas kernels, pick(): pl.pallas_call(functools.partial(pick_kernel, layer, layers, owned, group...  6.83 us
    ppermute x1, starting transfers between devices, local(): partner = lax.ppermute(own, ROWS_OVER, partners)  5.08 us
    all_to_all x1, waiting for transfers between devices, local(): heavy = lax.all_to_all(heavy, FETCH_OVER, 0, 0, tiled=True)[:, 0, :layers]  4.53 us
    all_to_all x1, starting transfers between devices, local(): heavy = lax.all_to_all(heavy, FETCH_OVER, 0, 0, tiled=True)[:, 0, :layers]  3.83 us
  transfers between devices with their start and end apart: 2, of which 1 were waited for; matrix products, arithmetic and copies ran while one was open for 0% of the time, Pallas kernels for 0%

profile of v4, /device:TPU:0, one launch (start us, length us, event | category | flops | bytes accessed | tf_op | source)
XLA Modules:
  0.0 180.4 jit_solution(11866513878419446885)
XLA Ops:
  0.0 2.6 %prepare.1 = (bf16[129,8,128]{2,1,0:T(8,128)(2,1)S(1)}, s32[16,1,128]{2,1,0:T(1,128)}) custom-call(s32[512]{0:T(512)} %bitcast.47, s32[4,16]{1,0:T(4,128)} %bitcast.52, bf16[128,8,128]{2,1,0:T(8,128)(2,1)} %bitcast.61, s32[4,128]{1,0:T(4,128)} %bitcast.48), custom_call_target="tpu_custom_call" | custom-call | tf_op jit(solution)/shard_map/prepare/pallas_call | solution.py:52
  2.6 5.1 %collective-permute-start = (bf16[129,8,128]{2,1,0:T(8,128)(2,1)S(1)}, bf16[129,8,128]{2,1,0:T(8,128)(2,1)S(1)}, u32[]{:S(2)}, u32[]{:S(2)}) collective-permute-start(bf16[129,8,128]{2,1,0:T(8,128)(2,1)S(1)} %get-tuple-element.10.refs_0_), channel_id=1, source_target_pairs={{0,24},{4,28},{8,16},{12,20},{16,8},{20,12},{24,0},{28,4},{1,25},{... | collective-permute-start | bytes 792584 | tf_op jit(solution)/shard_map/ppermute | solution.py:275
  7.7 3.8 %all-to-all-start = ((s32[16,1,128]{2,1,0:T(1,128)}), s32[16,1,128]{2,1,0:T(1,128)S(1)}, u32[]{:S(2)}, u32[]{:S(2)}) async-start(s32[16,1,128]{2,1,0:T(1,128)} %get-tuple-element.9), calls=%async_computation | async-start | bytes 16384 | tf_op jit(solution)/shard_map/all_to_all | solution.py:276
  11.5 0.9 reshape.56
  12.4 4.5 %all-to-all-done = s32[16,1,128]{2,1,0:T(1,128)S(1)} async-done(((s32[16,1,128]{2,1,0:T(1,128)}), s32[16,1,128]{2,1,0:T(1,128)S(1)}, u32[]{:S(2)}, u32[]{:S(2)}) %all-to-all-start) | async-done | bytes 8224 | tf_op jit(solution)/shard_map/all_to_all | solution.py:276
  16.9 0.0 collective-permute-done.refs_1_
  16.9 1.4 pick_0.1
  18.3 0.0 copy-start
  18.3 0.0 copy-start.2
  18.4 22.3 %all_to_all.45 = bf16[16,17,2,8,128]{4,3,2,1,0:T(8,128)(2,1)S(1)} all-to-all(bf16[16,17,2,8,128]{4,3,2,1,0:T(8,128)(2,1)S(1)} %get-tuple-element.12), channel_id=1, replica_groups=mesh['half'=2,'pair'=2,'rest'=2,'gy'=4] {'pair','rest','gy'}, dimensions={0} | all-to-all | bytes 2228224 | tf_op jit(solution)/shard_map/all_to_all | solution.py:293
  40.7 0.0 copy-done
  40.7 0.0 copy-done.2
  40.7 0.0 copy-start.1
  40.7 2.9 %multiply_0.1 = bf16[2,2,2,16,2,8,128]{6,5,4,3,2,1,0:T(8,128)(2,1)S(1)} custom-call(s32[1]{0:T(128)} %bitcast.where, s32[4,16]{1,0:T(4,128)S(1)} %bitcast.53, bf16[4,4,17,2,8,128]{5,4,3,2,1,0:T(8,128)(2,1)S(1)} %bitcast.29, bf16[4,1,16,8,128,128]{5,4,3,2,1,0:T(8,128)(2,1)} %w_hbm.7, f32[4,1,16,128]{3,2,1,0:T(8,128)S(1)} %copy-done), custom_call_target="tpu_custom_call" | custom-call | tf_op jit(solution)/shard_map/multiply_0/pallas_call | solution.py:229
  43.6 17.3 %all_to_all.46 = bf16[8,16,2,8,128]{4,3,2,1,0:T(8,128)(2,1)S(1)} all-to-all(bf16[8,16,2,8,128]{4,3,2,1,0:T(8,128)(2,1)S(1)} %bitcast.32), channel_id=1, replica_groups=mesh['half'=2,'pair'=2,'rest'=2,'gy'=4] {'half','pair','rest'}, dimensions={0} | all-to-all | bytes 1048576 | tf_op jit(solution)/shard_map/all_to_all | solution.py:297
  60.9 0.0 copy-done.1
  60.9 1.8 %pick_1.1 = bf16[16,17,2,8,128]{4,3,2,1,0:T(8,128)(2,1)S(1)} custom-call(s32[1]{0:T(128)} %bitcast.where, s32[4096]{0:T(1024)S(1)} %bitcast.40, s32[16,4]{1,0:T(8,128)S(1)} %bitcast.44, s32[512]{0:T(512)S(1)} %bitcast.49, s32[512]{0:T(512)S(1)} %bitcast.57, bf16[128,2,8,128]{3,2,1,0:T(8,128)(2,1)S(1)} %bitcast.36), custom_call_target="tpu_custom_call" | custom-call | tf_op jit(solution)/shard_map/pick_1/pallas_call | solution.py:142
  62.7 19.5 %all_to_all.47 = bf16[16,17,2,8,128]{4,3,2,1,0:T(8,128)(2,1)S(1)} all-to-all(bf16[16,17,2,8,128]{4,3,2,1,0:T(8,128)(2,1)S(1)} %pick_1.1), channel_id=1, replica_groups=mesh['half'=2,'pair'=2,'rest'=2,'gy'=4] {'pair','rest','gy'}, dimensions={0} | all-to-all | bytes 2228224 | tf_op jit(solution)/shard_map/all_to_all | solution.py:293
  82.3 2.9 %multiply_1.1 = bf16[2,2,2,16,2,8,128]{6,5,4,3,2,1,0:T(8,128)(2,1)S(1)} custom-call(s32[1]{0:T(128)} %bitcast.where, s32[4,16]{1,0:T(4,128)S(1)} %bitcast.54, bf16[4,4,17,2,8,128]{5,4,3,2,1,0:T(8,128)(2,1)S(1)} %bitcast.30, bf16[4,1,16,8,128,128]{5,4,3,2,1,0:T(8,128)(2,1)} %w_hbm.7, f32[4,1,16,128]{3,2,1,0:T(8,128)S(1)} %copy-done), custom_call_target="tpu_custom_call" | custom-call | tf_op jit(solution)/shard_map/multiply_1/pallas_call | solution.py:229
  85.1 17.2 %all_to_all.48 = bf16[8,16,2,8,128]{4,3,2,1,0:T(8,128)(2,1)S(1)} all-to-all(bf16[8,16,2,8,128]{4,3,2,1,0:T(8,128)(2,1)S(1)} %bitcast.33), channel_id=1, replica_groups=mesh['half'=2,'pair'=2,'rest'=2,'gy'=4] {'half','pair','rest'}, dimensions={0} | all-to-all | bytes 1048576 | tf_op jit(solution)/shard_map/all_to_all | solution.py:297
  102.3 1.8 %pick_2.1 = bf16[16,17,2,8,128]{4,3,2,1,0:T(8,128)(2,1)S(1)} custom-call(s32[1]{0:T(128)} %bitcast.where, s32[4096]{0:T(1024)S(1)} %bitcast.41, s32[16,4]{1,0:T(8,128)S(1)} %bitcast.45, s32[512]{0:T(512)S(1)} %bitcast.50, s32[512]{0:T(512)S(1)} %bitcast.58, bf16[128,2,8,128]{3,2,1,0:T(8,128)(2,1)S(1)} %bitcast.37), custom_call_target="tpu_custom_call" | custom-call | tf_op jit(solution)/shard_map/pick_2/pallas_call | solution.py:142
  104.2 19.5 %all_to_all.49 = bf16[16,17,2,8,128]{4,3,2,1,0:T(8,128)(2,1)S(1)} all-to-all(bf16[16,17,2,8,128]{4,3,2,1,0:T(8,128)(2,1)S(1)} %pick_2.1), channel_id=1, replica_groups=mesh['half'=2,'pair'=2,'rest'=2,'gy'=4] {'pair','rest','gy'}, dimensions={0} | all-to-all | bytes 2228224 | tf_op jit(solution)/shard_map/all_to_all | solution.py:293
  123.7 2.9 %multiply_2.1 = bf16[2,2,2,16,2,8,128]{6,5,4,3,2,1,0:T(8,128)(2,1)S(1)} custom-call(s32[1]{0:T(128)} %bitcast.where, s32[4,16]{1,0:T(4,128)S(1)} %bitcast.55, bf16[4,4,17,2,8,128]{5,4,3,2,1,0:T(8,128)(2,1)S(1)} %bitcast.31, bf16[4,1,16,8,128,128]{5,4,3,2,1,0:T(8,128)(2,1)} %w_hbm.7, f32[4,1,16,128]{3,2,1,0:T(8,128)S(1)} %copy-done), custom_call_target="tpu_custom_call" | custom-call | tf_op jit(solution)/shard_map/multiply_2/pallas_call | solution.py:229
  126.6 17.2 %all_to_all.50 = bf16[8,16,2,8,128]{4,3,2,1,0:T(8,128)(2,1)S(1)} all-to-all(bf16[8,16,2,8,128]{4,3,2,1,0:T(8,128)(2,1)S(1)} %bitcast.34), channel_id=1, replica_groups=mesh['half'=2,'pair'=2,'rest'=2,'gy'=4] {'half','pair','rest'}, dimensions={0} | all-to-all | bytes 1048576 | tf_op jit(solution)/shard_map/all_to_all | solution.py:297
  143.8 1.8 %pick_3.1 = bf16[16,17,2,8,128]{4,3,2,1,0:T(8,128)(2,1)S(1)} custom-call(s32[1]{0:T(128)} %bitcast.where, s32[4096]{0:T(1024)S(1)} %bitcast.42, s32[16,4]{1,0:T(8,128)S(1)} %bitcast.46, s32[512]{0:T(512)S(1)} %bitcast.51, s32[512]{0:T(512)S(1)} %bitcast.59, bf16[128,2,8,128]{3,2,1,0:T(8,128)(2,1)S(1)} %bitcast.35), custom_call_target="tpu_custom_call" | custom-call | tf_op jit(solution)/shard_map/pick_3/pallas_call | solution.py:142
  145.6 19.5 %all_to_all.51 = bf16[16,17,2,8,128]{4,3,2,1,0:T(8,128)(2,1)S(1)} all-to-all(bf16[16,17,2,8,128]{4,3,2,1,0:T(8,128)(2,1)S(1)} %pick_3.1), channel_id=1, replica_groups=mesh['half'=2,'pair'=2,'rest'=2,'gy'=4] {'pair','rest','gy'}, dimensions={0} | all-to-all | bytes 2228224 | tf_op jit(solution)/shard_map/all_to_all | solution.py:293
  165.1 2.9 %multiply_3.1 = bf16[2,2,2,16,8,128]{5,4,3,2,1,0:T(8,128)(2,1)S(1)} custom-call(s32[1]{0:T(128)} %bitcast.where, s32[4,16]{1,0:T(4,128)S(1)} %bitcast.56, bf16[4,4,17,2,8,128]{5,4,3,2,1,0:T(8,128)(2,1)S(1)} %bitcast.28, bf16[4,1,16,8,128,128]{5,4,3,2,1,0:T(8,128)(2,1)} %w_hbm.7, f32[4,1,16,128]{3,2,1,0:T(8,128)S(1)} %copy-done), custom_call_target="tpu_custom_call" | custom-call | tf_op jit(solution)/shard_map/multiply_3/pallas_call | solution.py:229
  168.0 11.6 %all_to_all.52 = bf16[8,16,8,128]{3,2,1,0:T(8,128)(2,1)S(1)} all-to-all(bf16[8,16,8,128]{3,2,1,0:T(8,128)(2,1)S(1)} %bitcast.38), channel_id=1, replica_groups=mesh['half'=2,'pair'=2,'rest'=2,'gy'=4] {'half','pair','rest'}, dimensions={0} | all-to-all | bytes 524288 | tf_op jit(solution)/shard_map/all_to_all | solution.py:297
  179.7 0.7 copy.14
  (1 shorter events, 0.0 us)
Async XLA Ops:
  2.6 14.4 %collective-permute-start = (bf16[129,8,128]{2,1,0:T(8,128)(2,1)S(1)}, bf16[129,8,128]{2,1,0:T(8,128)(2,1)S(1)}, u32[]{:S(2)}, u32[]{:S(2)}) collective-permute-start(bf16[129,8,128]{2,1,0:T(8,128)(2,1)S(1)} %get-tuple-element.10.refs_0_), channel_id=1, source_target_pairs={{0,24},{4,28},{8,16},{12,20},{16,8},{20,12},{24,0},{28,4},{1,25},{... | collective-permute-start | bytes 792584 | tf_op jit(solution)/shard_map/ppermute | solution.py:275
  7.7 9.3 %all-to-all-start = ((s32[16,1,128]{2,1,0:T(1,128)}), s32[16,1,128]{2,1,0:T(1,128)S(1)}, u32[]{:S(2)}, u32[]{:S(2)}) async-start(s32[16,1,128]{2,1,0:T(1,128)} %get-tuple-element.9), calls=%async_computation | async-start | bytes 16384 | tf_op jit(solution)/shard_map/all_to_all | solution.py:276
  18.3 22.4 %copy-start = (f32[4,1,16,128]{3,2,1,0:T(8,128)S(1)}, f32[4,1,16,128]{3,2,1,0:T(8,128)}, u32[]{:S(2)}) copy-start(f32[4,1,16,128]{3,2,1,0:T(8,128)} %bias_ref.7) | copy-start | bytes 98308
  18.3 22.4 %copy-start.2 = (s32[4,1,16]{2,1,0:T(1,128)S(1)}, s32[4,1,16]{2,1,0:T(1,128)}, u32[]{:S(2)}) copy-start(s32[4,1,16]{2,1,0:T(1,128)} %param.9) | copy-start | bytes 772
  40.7 20.2 %copy-start.1 = (s32[4,1,128]{2,1,0:T(1,128)S(1)}, s32[4,1,128]{2,1,0:T(1,128)}, u32[]{:S(2)}) copy-start(s32[4,1,128]{2,1,0:T(1,128)} %param.7) | copy-start | bytes 6148

commit v5 on v3

v5 whole, which is shorter than its diff:
```python
import functools

import jax
import jax.numpy as jnp
from jax import lax
from jax.experimental import pallas as pl
from jax.experimental.pallas import tpu as pltpu
from jax.sharding import Mesh, PartitionSpec as P

HALF, PAIR, REST, GROUP = "half", "pair", "rest", "gy"
ROWS_OVER = (HALF, PAIR, REST)
FETCH_OVER = (PAIR, REST, GROUP)


def masked(alive, tile):
    return jnp.where(alive > 0, tile, jnp.zeros_like(tile))


def announce_kernel(layers, groups, counts, heavy_ref):
    lane = lax.broadcasted_iota(jnp.int32, heavy_ref.shape[1:], 1)
    found = jnp.zeros_like(lane)
    for layer in range(layers):
        found = jnp.where(lane == layer, heavy_of(counts, layer, groups), found)
    heavy_ref[...] = jnp.broadcast_to(found[None], heavy_ref.shape)


def heavy_of(counts, layer, groups):
    heavy = jnp.int32(0)
    for k in range(counts.shape[1]):
        heavy = jnp.where(counts[layer, k] > groups, k, heavy)
    return heavy


def announce(groups, devices, side, counts):
    return pl.pallas_call(
        functools.partial(announce_kernel, counts.shape[0], groups),
        out_shape=jax.ShapeDtypeStruct((devices, 1, side), jnp.int32),
        grid_spec=pltpu.PrefetchScalarGridSpec(
            num_scalar_prefetch=1,
            grid=(1,),
            in_specs=[],
            out_specs=pl.BlockSpec((devices, 1, side), lambda i, *_: (0, 0, 0)),
        ),
        compiler_params=pltpu.CompilerParams(vmem_limit_bytes=4 << 20),
        name="announce",
    )(counts)


def mask_kernel(live, rows_ref, own_ref):
    batch = 8

    def mask(b, carry):
        first = b * batch
        kept = [masked(live[first + i], rows_ref[first + i]) for i in range(batch)]
        for i in range(batch):
            own_ref[first + i] = kept[i]
        return carry

    lax.fori_loop(0, rows_ref.shape[0] // batch, mask, 0)


def mask(live, own):
    live, own = (pltpu.with_memory_space_constraint(x, pltpu.HBM) for x in (live, own))
    spec = pl.BlockSpec(own.shape, lambda i, *_: (0, 0, 0))
    return pl.pallas_call(
        mask_kernel,
        out_shape=jax.ShapeDtypeStruct(own.shape, own.dtype),
        grid_spec=pltpu.PrefetchScalarGridSpec(
            num_scalar_prefetch=1, grid=(1,), in_specs=[spec], out_specs=spec
        ),
        compiler_params=pltpu.CompilerParams(vmem_limit_bytes=4 << 20),
        name="mask",
    )(live, own)


def pick_kernel(layer, layers, owned, groups, where, table, heavy, counts, *refs):
    step = pl.program_id(0)
    half = where[0]
    batch = 8
    *live_refs, w_hbm, out_ref, used_ref, rest_ref, kept_ref, sems = refs
    blocks = kept_ref.shape[0]
    copies = (
        pltpu.make_async_copy(w_hbm.at[layer, 0, :, pl.ds(0, groups)], used_ref, sems.at[0]),
        pltpu.make_async_copy(
            w_hbm.at[layer, 0, heavy_of(counts, layer, groups), pl.ds(groups, groups)],
            rest_ref,
            sems.at[1],
        ),
    )

    @pl.when(step == 0)
    def _():
        for copy in copies:
            copy.start()

    @pl.when(step == 0)
    def _():
        def mask(b, carry):
            first = b * batch
            kept = []
            for i in range(batch):
                spot = layer * blocks + first + i
                if layer == 0:
                    live_partner, own_ref, partner_ref = live_refs
                    kept.append(own_ref[first + i])
                    kept.append(masked(live_partner[spot], partner_ref[first + i]))
                else:
                    live_own, live_partner, state_ref = live_refs
                    kept.append(masked(live_own[spot], state_ref[first + i, half]))
                    kept.append(masked(live_partner[spot], state_ref[first + i, 1 - half]))
            for i in range(batch):
                kept_ref[first + i, half] = kept[2 * i]
                kept_ref[first + i, 1 - half] = kept[2 * i + 1]
            return carry

        lax.fori_loop(0, blocks // batch, mask, 0)

    dests = out_ref.shape[0]
    across = dests * pl.num_programs(0) // groups
    slots = table.shape[0] // (2 * layers)

    def one_owner(o, carry):
        owner = step * (dests // groups) + o
        for g in range(groups):
            first = 2 * layer * slots + g * blocks + (half * across + owner) * owned
            spots = [table[first + k] for k in range(owned)]
            spots.append(table[first + slots + heavy[owner * groups + g, layer]])
            for k, spot in enumerate(spots):
                out_ref[o * groups + g, k] = kept_ref[spot]
        return carry

    lax.fori_loop(0, dests // groups, one_owner, 0)

    @pl.when(step == pl.num_programs(0) - 1)
    def _():
        for copy in copies:
            copy.wait()


def pick(layer, layers, owned, groups, tables, states, weight_tiles):
    blocks, (rows, side) = states[0].shape[0], states[0].shape[-2:]
    devices = tables[2].shape[0]
    steps = 2
    used = (owned, groups, side, side)
    rest = (groups, side, side)
    return pl.pallas_call(
        functools.partial(pick_kernel, layer, layers, owned, groups),
        out_shape=(
            jax.ShapeDtypeStruct((devices, owned + 1, 2, rows, side), states[0].dtype),
            jax.ShapeDtypeStruct(used, weight_tiles.dtype),
            jax.ShapeDtypeStruct(rest, weight_tiles.dtype),
        ),
        grid_spec=pltpu.PrefetchScalarGridSpec(
            num_scalar_prefetch=len(tables),
            grid=(steps,),
            in_specs=[
                pl.BlockSpec(state.shape, lambda i, *_, n=state.ndim: (0,) * n) for state in states
            ]
            + [pl.BlockSpec(memory_space=pl.ANY)],
            out_specs=(
                pl.BlockSpec(
                    (devices // steps, owned + 1, 2, rows, side), lambda i, *_: (i, 0, 0, 0, 0)
                ),
                pl.BlockSpec(used, lambda i, *_: (0, 0, 0, 0)),
                pl.BlockSpec(rest, lambda i, *_: (0, 0, 0)),
            ),
            scratch_shapes=[
                pltpu.VMEM((blocks, 2, rows, side), states[0].dtype),
                pltpu.SemaphoreType.DMA((2,)),
            ],
        ),
        compiler_params=pltpu.CompilerParams(vmem_limit_bytes=12 << 20),
        name=f"pick_{layer}",
    )(*tables, *states, pltpu.with_memory_space_constraint(weight_tiles, pltpu.HBM))


def multiply_kernel(layer, last, where, counts, x_ref, w_ref, wrest_ref, bias_ref, out_ref, acc_ref):
    step = pl.program_id(0)
    across, groups, _, _, rows, side = x_ref.shape
    owned = counts.shape[1]
    chunk = owned // pl.num_programs(0)
    total_rows = across * 2 * rows
    half = where[0]

    def gathered(position, first, count):
        parts = []
        for g in range(groups):
            part = x_ref[:, g, position].reshape(total_rows, side)
            parts.append(jnp.where(first + g < count, part, jnp.zeros_like(part)))
        return jnp.concatenate(parts, axis=1)

    def write(k, summed):
        value = jnp.maximum(summed, 0.0).astype(out_ref.dtype)
        value = value.reshape(2, across // 2, 2, rows, side)
        if last:
            low, high = value[:, :, 0], value[:, :, 1]
            near = jnp.where(half == 0, low, high)
            far = jnp.where(half == 0, high, low)
        else:
            near = far = value
        out_ref[half, :, :, k] = near
        out_ref[1 - half, 0, :, k] = far[1]
        out_ref[1 - half, 1, :, k] = far[0]

    for c in range(chunk):
        k = step * chunk + c
        lhs = gathered(k, 0, counts[layer, k])
        weight = w_ref[k].reshape(groups * side, side)
        summed = jnp.dot(lhs, weight, preferred_element_type=jnp.float32)
        summed = summed + bias_ref[0, 0, pl.ds(k, 1), :]
        acc_ref[k] = summed
        write(k, summed)

    @pl.when(step == pl.num_programs(0) - 1)
    def _():
        heavy = heavy_of(counts, layer, groups)
        lhs = gathered(owned, groups, counts[layer, heavy])
        weight = wrest_ref[...].reshape(groups * side, side)
        write(heavy, acc_ref[heavy] + jnp.dot(lhs, weight, preferred_element_type=jnp.float32))


def multiply(layer, last, where, counts, incoming, used, rest, bias_terms):
    across, groups, width, _, rows, side = incoming.shape
    owned = width - 1
    steps = 4 if owned % 4 == 0 else 1
    out = (2, 2, across // 2, owned) + (() if last else (2,)) + (rows, side)
    return pl.pallas_call(
        functools.partial(multiply_kernel, layer, last),
        out_shape=jax.ShapeDtypeStruct(out, incoming.dtype),
        grid_spec=pltpu.PrefetchScalarGridSpec(
            num_scalar_prefetch=2,
            grid=(steps,),
            in_specs=[
                pl.BlockSpec(incoming.shape, lambda i, *_: (0,) * incoming.ndim),
                pl.BlockSpec(used.shape, lambda i, *_: (0, 0, 0, 0)),
                pl.BlockSpec(rest.shape, lambda i, *_: (0, 0, 0)),
                pl.BlockSpec((1, 1, owned, side), lambda i, *_: (layer, 0, 0, 0)),
            ],
            out_specs=pl.BlockSpec(out, lambda i, *_: (0,) * len(out)),
            scratch_shapes=[pltpu.VMEM((owned, across * 2 * rows, side), jnp.float32)],
        ),
        compiler_params=pltpu.CompilerParams(vmem_limit_bytes=12 << 20),
        name=f"multiply_{layer}",
    )(where, counts, incoming, used, rest, bias_terms)


def local(activations, live_blocks, tile_index, tile_count, weight_tiles, bias_terms):
    rest = lax.axis_size(REST)
    groups = lax.axis_size(GROUP)
    my_group = lax.axis_index(GROUP)
    my_half = lax.axis_index(HALF)
    layers = tile_index.shape[0]
    rows = activations.shape[0]
    side = weight_tiles.shape[-1]
    owned = weight_tiles.shape[2]
    blocks = activations.shape[1] // side
    devices = 2 * rest * groups
    partners = [
        ((h * 2 + p) * rest + r, ((1 - h) * 2 + 1 - p) * rest + r)
        for h in range(2)
        for p in range(2)
        for r in range(rest)
    ]

    counts = tile_count[:, 0]
    live = live_blocks[:, 0]
    own = jnp.transpose(activations.reshape(rows, blocks, side), (1, 0, 2))
    partner = lax.ppermute(own, ROWS_OVER, partners)
    counts_hbm = pltpu.with_memory_space_constraint(counts, pltpu.HBM)
    heavy = announce(groups, devices, side, counts_hbm)
    heavy = lax.all_to_all(heavy, FETCH_OVER, 0, 0, tiled=True)[:, 0, :layers]
    live_own = live.reshape(-1)
    live_partner = lax.ppermute(live, ROWS_OVER, partners).reshape(-1)
    own = mask(live_own, own)
    where = my_half.reshape(1)

    slots = jnp.transpose(tile_index, (0, 2, 1)).reshape(layers, -1, groups, tile_index.shape[1])
    table = lax.dynamic_index_in_dim(slots, my_group, 2, keepdims=False) - my_group * blocks
    table = table.reshape(-1)

    for layer in range(layers):
        last = layer == layers - 1
        if layer == 0:
            tables, states = (where, table, heavy, counts_hbm, live_partner), (own, partner)
        else:
            tables, states = (where, table, heavy, counts, live_own, live_partner), (state,)
        outgoing, used, extra = pick(layer, layers, owned, groups, tables, states, weight_tiles)
        incoming = lax.all_to_all(outgoing, FETCH_OVER, 0, 0, tiled=True)
        incoming = incoming.reshape(2 * rest, groups, owned + 1, 2, rows, side)
        result = multiply(layer, last, where, counts, incoming, used, extra, bias_terms)
        result = result.reshape((4 * rest,) + result.shape[3:])
        returned = lax.all_to_all(result, ROWS_OVER, 0, 0, tiled=True)
        state = returned.reshape((blocks,) + returned.shape[2:])
    return jnp.transpose(state, (1, 0, 2)).reshape(rows, blocks * side)


def solution(mesh):
    across, groups = mesh.shape["gx"], mesh.shape["gy"]
    split = Mesh(mesh.devices.reshape(2, 2, across // 4, groups), (HALF, PAIR, REST, GROUP))
    placed = (
        P(ROWS_OVER, GROUP),
        P(None, ROWS_OVER, GROUP),
        P(),
        P(None, GROUP, ROWS_OVER),
        P(None, GROUP, ROWS_OVER, None, None, None),
        P(None, GROUP, ROWS_OVER, None),
    )
    return jax.shard_map(
        local, mesh=split, in_specs=placed, out_specs=P(ROWS_OVER, GROUP), check_vma=False
    )
```

time: 182 us -> 178 us (0.978)
  local copies, waits for them, and re-layouts: 3.82 us -> 1.58 us
  waiting for transfers between devices: 3.28 us -> 1.39 us
    pallas_call x4, Pallas kernels: 12.5 us -> 6.61 us  [multiply(): pl.pallas_call(functools.partial(multiply_kernel, layer, last), out_shape...]
    pallas_call x4, Pallas kernels: 7.23 us -> 10.7 us  [pick(): pl.pallas_call(functools.partial(pick_kernel, layer, layers, owned, group...]
    pallas_call x0 -> x2, Pallas kernels: none -> 3.23 us  [the longest x1 1.88 us: mask(): pl.pallas_call(mask_kernel, out_shape=jax.ShapeDtypeStruct(own.shape, own...]
    ppermute x1, waiting for transfers between devices: 3.27 us -> 1.38 us  [local(): live_partner = lax.ppermute(live, ROWS_OVER, partners).reshape(-1)]
  transfers between devices with their start and end apart: 3 -> 3, of which waited for: 1 -> 1; matrix products, arithmetic and copies ran while one was open for 1% -> 0% of each run, Pallas kernels for 0% -> 2%
where the time goes in v5:
time: 178 us; the launch traced here: 177 us
  blocking collectives  143 us (80%)
  Pallas kernels  20.6 us (12%)
  starting transfers between devices  10.5 us (6%)
    all_to_all x4, blocking collectives, local(): incoming = lax.all_to_all(outgoing, FETCH_OVER, 0, 0, tiled=True)  79.5 us
    all_to_all x4, blocking collectives, local(): returned = lax.all_to_all(result, ROWS_OVER, 0, 0, tiled=True)  63.4 us
    pallas_call x4, Pallas kernels, pick(): pl.pallas_call(functools.partial(pick_kernel, layer, layers, owned, group...  10.7 us
    pallas_call x4, Pallas kernels, multiply(): pl.pallas_call(functools.partial(multiply_kernel, layer, last), out_shape...  6.61 us
    ppermute x1, starting transfers between devices, local(): partner = lax.ppermute(own, ROWS_OVER, partners)  5.08 us
    all_to_all x1, starting transfers between devices, local(): heavy = lax.all_to_all(heavy, FETCH_OVER, 0, 0, tiled=True)[:, 0, :layers]  3.83 us
  transfers between devices with their start and end apart: 3, of which 1 were waited for; matrix products, arithmetic and copies ran while one was open for 0% of the time, Pallas kernels for 2%

profile of v5, /device:TPU:0, one launch (start us, length us, event | category | flops | bytes accessed | tf_op | source)
XLA Modules:
  0.0 177.1 jit_solution(11563985771864430223)
XLA Ops:
  0.0 5.1 %collective-permute-start.1 = (bf16[128,8,128]{2,1,0:T(8,128)(2,1)}, bf16[128,8,128]{2,1,0:T(8,128)(2,1)S(1)}, u32[]{:S(2)}, u32[]{:S(2)}) collective-permute-start(bf16[128,8,128]{2,1,0:T(8,128)(2,1)} %bitcast.66), channel_id=1, source_target_pairs={{0,24},{4,28},{8,16},{12,20},{16,8},{20,12},{24,0},{28,4},{1,25},{... | collective-permute-start | bytes 786440 | tf_op jit(solution)/shard_map/ppermute | solution.py:268
  5.1 1.3 announce.1
  6.4 3.8 %all-to-all-start = ((s32[16,1,128]{2,1,0:T(1,128)}), s32[16,1,128]{2,1,0:T(1,128)S(1)}, u32[]{:S(2)}, u32[]{:S(2)}) async-start(s32[16,1,128]{2,1,0:T(1,128)} %announce.1), calls=%async_computation | async-start | bytes 16384 | tf_op jit(solution)/shard_map/all_to_all | solution.py:271
  10.3 1.6 collective-permute-start
  11.8 0.9 reshape.56
  12.7 1.9 %mask.1.refs_1_ = bf16[128,8,128]{2,1,0:T(8,128)(2,1)S(1)} custom-call(s32[512]{0:T(512)} %bitcast.57, bf16[128,8,128]{2,1,0:T(8,128)(2,1)} %bitcast.67), custom_call_target="tpu_custom_call" | custom-call | tf_op jit(solution)/shard_map/mask/pallas_call | solution.py:65
  14.6 1.4 collective-permute-done
  16.0 0.0 all-to-all-done
  16.0 0.0 collective-permute-done.1.refs_2_
  16.0 2.7 %pick_0.1 = (bf16[16,17,2,8,128]{4,3,2,1,0:T(8,128)(2,1)S(1)}, bf16[16,4,128,128]{3,2,1,0:T(8,128)(2,1)S(1)}, bf16[4,128,128]{2,1,0:T(8,128)(2,1)S(1)}) custom-call(s32[1]{0:T(128)} %bitcast.where, s32[4096]{0:T(1024)S(1)} %bitcast.39, s32[16,4]{1,0:T(8,128)S(1)} %bitcast.43, s32[4,16]{1,0:T(4,128)} %bitcast.48, s32[512]{0:T(512)S(1)} %bitcast.61, ...), custom_call_target="tpu_custom_call" | custom-call | tf_op jit(solution)/shard_map/pick_0/pallas_call | solution.py:146
  18.8 0.0 copy-start
  18.8 0.0 copy-start.1
  18.8 20.9 %all_to_all.45 = bf16[16,17,2,8,128]{4,3,2,1,0:T(8,128)(2,1)S(1)} all-to-all(bf16[16,17,2,8,128]{4,3,2,1,0:T(8,128)(2,1)S(1)} %get-tuple-element.17), channel_id=1, replica_groups=mesh['half'=2,'pair'=2,'rest'=2,'gy'=4] {'pair','rest','gy'}, dimensions={0} | all-to-all | bytes 2228224 | tf_op jit(solution)/shard_map/all_to_all | solution.py:288
  39.7 0.0 copy-done
  39.7 0.0 copy-done.1
  39.7 0.0 copy-start.2
  39.7 1.7 multiply_0.1
  41.4 17.3 %all_to_all.46 = bf16[8,16,2,8,128]{4,3,2,1,0:T(8,128)(2,1)S(1)} all-to-all(bf16[8,16,2,8,128]{4,3,2,1,0:T(8,128)(2,1)S(1)} %bitcast.35), channel_id=1, replica_groups=mesh['half'=2,'pair'=2,'rest'=2,'gy'=4] {'half','pair','rest'}, dimensions={0} | all-to-all | bytes 1048576 | tf_op jit(solution)/shard_map/all_to_all | solution.py:292
  58.7 0.0 copy-done.2
  58.7 2.7 %pick_1.1 = (bf16[16,17,2,8,128]{4,3,2,1,0:T(8,128)(2,1)S(1)}, bf16[16,4,128,128]{3,2,1,0:T(8,128)(2,1)S(1)}, bf16[4,128,128]{2,1,0:T(8,128)(2,1)S(1)}) custom-call(s32[1]{0:T(128)} %bitcast.where, s32[4096]{0:T(1024)S(1)} %bitcast.40, s32[16,4]{1,0:T(8,128)S(1)} %bitcast.44, s32[4,16]{1,0:T(4,128)S(1)} %bitcast.50, s32[512]{0:T(512)S(1)} %bitcast.58, ...), custom_call_target="tpu_custom_call" | custom-call | tf_op jit(solution)/shard_map/pick_1/pallas_call | solution.py:146
  61.4 19.5 %all_to_all.47 = bf16[16,17,2,8,128]{4,3,2,1,0:T(8,128)(2,1)S(1)} all-to-all(bf16[16,17,2,8,128]{4,3,2,1,0:T(8,128)(2,1)S(1)} %get-tuple-element.20), channel_id=1, replica_groups=mesh['half'=2,'pair'=2,'rest'=2,'gy'=4] {'pair','rest','gy'}, dimensions={0} | all-to-all | bytes 2228224 | tf_op jit(solution)/shard_map/all_to_all | solution.py:288
  80.9 1.7 multiply_1.1
  82.6 17.2 %all_to_all.48 = bf16[8,16,2,8,128]{4,3,2,1,0:T(8,128)(2,1)S(1)} all-to-all(bf16[8,16,2,8,128]{4,3,2,1,0:T(8,128)(2,1)S(1)} %bitcast.36), channel_id=1, replica_groups=mesh['half'=2,'pair'=2,'rest'=2,'gy'=4] {'half','pair','rest'}, dimensions={0} | all-to-all | bytes 1048576 | tf_op jit(solution)/shard_map/all_to_all | solution.py:292
  99.8 2.7 %pick_2.1 = (bf16[16,17,2,8,128]{4,3,2,1,0:T(8,128)(2,1)S(1)}, bf16[16,4,128,128]{3,2,1,0:T(8,128)(2,1)S(1)}, bf16[4,128,128]{2,1,0:T(8,128)(2,1)S(1)}) custom-call(s32[1]{0:T(128)} %bitcast.where, s32[4096]{0:T(1024)S(1)} %bitcast.41, s32[16,4]{1,0:T(8,128)S(1)} %bitcast.45, s32[4,16]{1,0:T(4,128)S(1)} %bitcast.52, s32[512]{0:T(512)S(1)} %bitcast.59, ...), custom_call_target="tpu_custom_call" | custom-call | tf_op jit(solution)/shard_map/pick_2/pallas_call | solution.py:146
  102.5 19.5 %all_to_all.49 = bf16[16,17,2,8,128]{4,3,2,1,0:T(8,128)(2,1)S(1)} all-to-all(bf16[16,17,2,8,128]{4,3,2,1,0:T(8,128)(2,1)S(1)} %get-tuple-element.23), channel_id=1, replica_groups=mesh['half'=2,'pair'=2,'rest'=2,'gy'=4] {'pair','rest','gy'}, dimensions={0} | all-to-all | bytes 2228224 | tf_op jit(solution)/shard_map/all_to_all | solution.py:288
  122.0 1.7 multiply_2.1
  123.6 17.2 %all_to_all.50 = bf16[8,16,2,8,128]{4,3,2,1,0:T(8,128)(2,1)S(1)} all-to-all(bf16[8,16,2,8,128]{4,3,2,1,0:T(8,128)(2,1)S(1)} %bitcast.37), channel_id=1, replica_groups=mesh['half'=2,'pair'=2,'rest'=2,'gy'=4] {'half','pair','rest'}, dimensions={0} | all-to-all | bytes 1048576 | tf_op jit(solution)/shard_map/all_to_all | solution.py:292
  140.9 2.7 %pick_3.1 = (bf16[16,17,2,8,128]{4,3,2,1,0:T(8,128)(2,1)S(1)}, bf16[16,4,128,128]{3,2,1,0:T(8,128)(2,1)S(1)}, bf16[4,128,128]{2,1,0:T(8,128)(2,1)S(1)}) custom-call(s32[1]{0:T(128)} %bitcast.where, s32[4096]{0:T(1024)S(1)} %bitcast.42, s32[16,4]{1,0:T(8,128)S(1)} %bitcast.46, s32[4,16]{1,0:T(4,128)S(1)} %bitcast.54, s32[512]{0:T(512)S(1)} %bitcast.60, ...), custom_call_target="tpu_custom_call" | custom-call | tf_op jit(solution)/shard_map/pick_3/pallas_call | solution.py:146
  143.5 19.5 %all_to_all.51 = bf16[16,17,2,8,128]{4,3,2,1,0:T(8,128)(2,1)S(1)} all-to-all(bf16[16,17,2,8,128]{4,3,2,1,0:T(8,128)(2,1)S(1)} %get-tuple-element.26), channel_id=1, replica_groups=mesh['half'=2,'pair'=2,'rest'=2,'gy'=4] {'pair','rest','gy'}, dimensions={0} | all-to-all | bytes 2228224 | tf_op jit(solution)/shard_map/all_to_all | solution.py:288
  163.1 1.7 multiply_3.1
  164.7 11.6 %all_to_all.52 = bf16[8,16,8,128]{3,2,1,0:T(8,128)(2,1)S(1)} all-to-all(bf16[8,16,8,128]{3,2,1,0:T(8,128)(2,1)S(1)} %bitcast.38), channel_id=1, replica_groups=mesh['half'=2,'pair'=2,'rest'=2,'gy'=4] {'half','pair','rest'}, dimensions={0} | all-to-all | bytes 524288 | tf_op jit(solution)/shard_map/all_to_all | solution.py:292
  176.4 0.7 copy.14
  (1 shorter events, 0.0 us)
Async XLA Ops:
  0.0 16.0 %collective-permute-start.1 = (bf16[128,8,128]{2,1,0:T(8,128)(2,1)}, bf16[128,8,128]{2,1,0:T(8,128)(2,1)S(1)}, u32[]{:S(2)}, u32[]{:S(2)}) collective-permute-start(bf16[128,8,128]{2,1,0:T(8,128)(2,1)} %bitcast.66), channel_id=1, source_target_pairs={{0,24},{4,28},{8,16},{12,20},{16,8},{20,12},{24,0},{28,4},{1,25},{... | collective-permute-start | bytes 786440 | tf_op jit(solution)/shard_map/ppermute | solution.py:268
  6.4 9.6 %all-to-all-start = ((s32[16,1,128]{2,1,0:T(1,128)}), s32[16,1,128]{2,1,0:T(1,128)S(1)}, u32[]{:S(2)}, u32[]{:S(2)}) async-start(s32[16,1,128]{2,1,0:T(1,128)} %announce.1), calls=%async_computation | async-start | bytes 16384 | tf_op jit(solution)/shard_map/all_to_all | solution.py:271
  10.3 5.8 %collective-permute-start = (s32[4,128]{1,0:T(4,128)}, s32[4,128]{1,0:T(4,128)S(1)}, u32[]{:S(2)}, u32[]{:S(2)}) collective-permute-start(s32[4,128]{1,0:T(4,128)} %bitcast.56), channel_id=1, source_target_pairs={{0,24},{4,28},{8,16},{12,20},{16,8},{20,12},{24,0},{28,4},{1,25},{... | collective-permute-start | bytes 6152 | tf_op jit(solution)/shard_map/ppermute | solution.py:273
  18.8 20.9 %copy-start = (f32[4,1,16,128]{3,2,1,0:T(8,128)S(1)}, f32[4,1,16,128]{3,2,1,0:T(8,128)}, u32[]{:S(2)}) copy-start(f32[4,1,16,128]{3,2,1,0:T(8,128)} %bias_ref.7) | copy-start | bytes 98308
  18.8 20.9 %copy-start.1 = (s32[4,1,16]{2,1,0:T(1,128)S(1)}, s32[4,1,16]{2,1,0:T(1,128)}, u32[]{:S(2)}) copy-start(s32[4,1,16]{2,1,0:T(1,128)} %param.9) | copy-start | bytes 772
  39.7 19.0 %copy-start.2 = (s32[4,1,128]{2,1,0:T(1,128)S(1)}, s32[4,1,128]{2,1,0:T(1,128)}, u32[]{:S(2)}) copy-start(s32[4,1,128]{2,1,0:T(1,128)} %param.7) | copy-start | bytes 6148

commit v6 on v5

v6 whole, which is shorter than its diff:
```python
import functools

import jax
import jax.numpy as jnp
from jax import lax
from jax.experimental import pallas as pl
from jax.experimental.pallas import tpu as pltpu
from jax.sharding import Mesh, PartitionSpec as P

HALF, PAIR, REST, GROUP = "half", "pair", "rest", "gy"
ROWS_OVER = (HALF, PAIR, REST)
FETCH_OVER = (PAIR, REST, GROUP)


def masked(alive, tile):
    return jnp.where(alive > 0, tile, jnp.zeros_like(tile))


def announce_kernel(layers, groups, counts, heavy_ref):
    lane = lax.broadcasted_iota(jnp.int32, heavy_ref.shape[1:], 1)
    found = jnp.zeros_like(lane)
    for layer in range(layers):
        found = jnp.where(lane == layer, heavy_of(counts, layer, groups), found)
    heavy_ref[...] = jnp.broadcast_to(found[None], heavy_ref.shape)


def heavy_of(counts, layer, groups):
    heavy = jnp.int32(0)
    for k in range(counts.shape[1]):
        heavy = jnp.where(counts[layer, k] > groups, k, heavy)
    return heavy


def announce(groups, devices, side, counts):
    return pl.pallas_call(
        functools.partial(announce_kernel, counts.shape[0], groups),
        out_shape=jax.ShapeDtypeStruct((devices, 1, side), jnp.int32),
        grid_spec=pltpu.PrefetchScalarGridSpec(
            num_scalar_prefetch=1,
            grid=(1,),
            in_specs=[],
            out_specs=pl.BlockSpec((devices, 1, side), lambda i, *_: (0, 0, 0)),
        ),
        compiler_params=pltpu.CompilerParams(vmem_limit_bytes=4 << 20),
        name="announce",
    )(counts)


def mask_kernel(live, rows_ref, own_ref):
    batch = 8

    def mask(b, carry):
        first = b * batch
        kept = [masked(live[first + i], rows_ref[first + i]) for i in range(batch)]
        for i in range(batch):
            own_ref[first + i] = kept[i]
        return carry

    lax.fori_loop(0, rows_ref.shape[0] // batch, mask, 0)


def mask(live, own):
    live, own = (pltpu.with_memory_space_constraint(x, pltpu.HBM) for x in (live, own))
    spec = pl.BlockSpec(own.shape, lambda i, *_: (0, 0, 0))
    return pl.pallas_call(
        mask_kernel,
        out_shape=jax.ShapeDtypeStruct(own.shape, own.dtype),
        grid_spec=pltpu.PrefetchScalarGridSpec(
            num_scalar_prefetch=1, grid=(1,), in_specs=[spec], out_specs=spec
        ),
        compiler_params=pltpu.CompilerParams(vmem_limit_bytes=4 << 20),
        name="mask",
    )(live, own)


def pick_kernel(layer, owned, groups, where, heavy, *refs):
    half = where[0]
    batch = 8
    *live_refs, table, w_hbm, out_ref, used_ref, kept_ref, sem = refs
    blocks = kept_ref.shape[0]
    fetch = pltpu.make_async_copy(
        w_hbm.at[layer, 0, pl.ds(0, used_ref.shape[0]), pl.ds(0, groups)], used_ref, sem
    )
    fetch.start()

    def mask(b, carry):
        first = b * batch
        kept = []
        for i in range(batch):
            spot = layer * blocks + first + i
            if layer == 0:
                live_partner, own_ref, partner_ref = live_refs
                kept.append(own_ref[first + i])
                kept.append(masked(live_partner[spot], partner_ref[first + i]))
            else:
                live_own, live_partner, state_ref = live_refs
                kept.append(masked(live_own[spot], state_ref[first + i, half]))
                kept.append(masked(live_partner[spot], state_ref[first + i, 1 - half]))
        for i in range(batch):
            kept_ref[first + i, half] = kept[2 * i]
            kept_ref[first + i, 1 - half] = kept[2 * i + 1]
        return carry

    lax.fori_loop(0, blocks // batch, mask, 0)

    across = out_ref.shape[0] // groups
    slots = table.shape[0] // 2

    def one_owner(owner, carry):
        for g in range(groups):
            first = g * blocks + (half * across + owner) * owned
            spots = [table[first + k] for k in range(owned)]
            spots.append(table[first + slots + heavy[owner * groups + g, layer]])
            for k, spot in enumerate(spots):
                out_ref[owner * groups + g, k] = kept_ref[spot]
        return carry

    lax.fori_loop(0, across, one_owner, 0)
    fetch.wait()


def early(owned):
    return owned // 2 if owned % 2 == 0 else owned


def pick(layer, layers, owned, groups, table, scalars, states, weight_tiles):
    blocks, (rows, side) = states[0].shape[0], states[0].shape[-2:]
    devices = scalars[1].shape[0]
    shapes = ((devices, owned + 1, 2, rows, side), (early(owned), groups, side, side))
    return pl.pallas_call(
        functools.partial(pick_kernel, layer, owned, groups),
        out_shape=tuple(jax.ShapeDtypeStruct(shape, weight_tiles.dtype) for shape in shapes),
        grid_spec=pltpu.PrefetchScalarGridSpec(
            num_scalar_prefetch=len(scalars),
            grid=(1,),
            in_specs=[
                pl.BlockSpec(state.shape, lambda i, *_, n=state.ndim: (0,) * n) for state in states
            ]
            + [
                pl.BlockSpec(
                    (table.shape[0] // layers,), lambda i, *_: (layer,), memory_space=pltpu.SMEM
                ),
                pl.BlockSpec(memory_space=pl.ANY),
            ],
            out_specs=tuple(
                pl.BlockSpec(shape, lambda i, *_, n=len(shape): (0,) * n) for shape in shapes
            ),
            scratch_shapes=[
                pltpu.VMEM((blocks, 2, rows, side), states[0].dtype),
                pltpu.SemaphoreType.DMA,
            ],
        ),
        compiler_params=pltpu.CompilerParams(vmem_limit_bytes=12 << 20),
    )(*scalars, *states, table, pltpu.with_memory_space_constraint(weight_tiles, pltpu.HBM))


def multiply_kernel(
    layer, last, where, counts, x_ref, used_ref, w_hbm, bias_ref, out_ref, acc_ref, late_ref, rest_ref, sems
):
    step = pl.program_id(0)
    steps = pl.num_programs(0)
    across, groups, _, _, rows, side = x_ref.shape
    owned = counts.shape[1]
    chunk = used_ref.shape[0]
    total_rows = across * 2 * rows
    half = where[0]
    heavy = heavy_of(counts, layer, groups)
    fetches = [
        pltpu.make_async_copy(
            w_hbm.at[layer, 0, heavy, pl.ds(groups, groups)], rest_ref, sems.at[0]
        )
    ]
    if chunk < owned:
        fetches.append(
            pltpu.make_async_copy(
                w_hbm.at[layer, 0, pl.ds(chunk, chunk), pl.ds(0, groups)], late_ref, sems.at[1]
            )
        )

    @pl.when(step == 0)
    def _():
        for fetch in reversed(fetches):
            fetch.start()

    def gathered(position, first, count):
        parts = []
        for g in range(groups):
            part = x_ref[:, g, position].reshape(total_rows, side)
            parts.append(jnp.where(first + g < count, part, jnp.zeros_like(part)))
        return jnp.concatenate(parts, axis=1)

    def write(k, summed):
        value = jnp.maximum(summed, 0.0).astype(out_ref.dtype)
        value = value.reshape(2, across // 2, 2, rows, side)
        if last:
            low, high = value[:, :, 0], value[:, :, 1]
            near = jnp.where(half == 0, low, high)
            far = jnp.where(half == 0, high, low)
        else:
            near = far = value
        out_ref[half, :, :, k] = near
        out_ref[1 - half, 0, :, k] = far[1]
        out_ref[1 - half, 1, :, k] = far[0]

    def blocks_of(first, weights):
        for c in range(chunk):
            k = first + c
            weight = weights[c].reshape(groups * side, side)
            summed = jnp.dot(
                gathered(k, 0, counts[layer, k]), weight, preferred_element_type=jnp.float32
            )
            summed = summed + bias_ref[0, 0, k : k + 1, :]
            acc_ref[k] = summed
            write(k, summed)

    @pl.when(step == 0)
    def _():
        blocks_of(0, used_ref)

    @pl.when(step == steps - 1)
    def _():
        for fetch in fetches:
            fetch.wait()
        if chunk < owned:
            blocks_of(chunk, late_ref)
        lhs = gathered(owned, groups, counts[layer, heavy])
        weight = rest_ref[...].reshape(groups * side, side)
        write(heavy, acc_ref[heavy] + jnp.dot(lhs, weight, preferred_element_type=jnp.float32))


def multiply(layer, last, where, counts, incoming, used, weight_tiles, bias_terms):
    across, groups, width, _, rows, side = incoming.shape
    owned = width - 1
    out = (2, 2, across // 2, owned) + (() if last else (2,)) + (rows, side)
    return pl.pallas_call(
        functools.partial(multiply_kernel, layer, last),
        out_shape=jax.ShapeDtypeStruct(out, incoming.dtype),
        grid_spec=pltpu.PrefetchScalarGridSpec(
            num_scalar_prefetch=2,
            grid=(owned // used.shape[0],),
            in_specs=[
                pl.BlockSpec(incoming.shape, lambda i, *_: (0,) * incoming.ndim),
                pl.BlockSpec(used.shape, lambda i, *_: (0, 0, 0, 0)),
                pl.BlockSpec(memory_space=pl.ANY),
                pl.BlockSpec((1, 1, owned, side), lambda i, *_: (layer, 0, 0, 0)),
            ],
            out_specs=pl.BlockSpec(out, lambda i, *_: (0,) * len(out)),
            scratch_shapes=[
                pltpu.VMEM((owned, across * 2 * rows, side), jnp.float32),
                pltpu.VMEM(used.shape, used.dtype),
                pltpu.VMEM((groups, side, side), used.dtype),
                pltpu.SemaphoreType.DMA((2,)),
            ],
        ),
        compiler_params=pltpu.CompilerParams(vmem_limit_bytes=12 << 20),
    )(
        where,
        counts,
        incoming,
        used,
        pltpu.with_memory_space_constraint(weight_tiles, pltpu.HBM),
        bias_terms,
    )


def local(activations, live_blocks, tile_index, tile_count, weight_tiles, bias_terms):
    rest = lax.axis_size(REST)
    groups = lax.axis_size(GROUP)
    my_group = lax.axis_index(GROUP)
    my_half = lax.axis_index(HALF)
    layers = tile_index.shape[0]
    rows = activations.shape[0]
    side = weight_tiles.shape[-1]
    owned = weight_tiles.shape[2]
    blocks = activations.shape[1] // side
    devices = 2 * rest * groups
    partners = [
        ((h * 2 + p) * rest + r, ((1 - h) * 2 + 1 - p) * rest + r)
        for h in range(2)
        for p in range(2)
        for r in range(rest)
    ]

    counts = tile_count[:, 0]
    live = live_blocks[:, 0]
    own = jnp.transpose(activations.reshape(rows, blocks, side), (1, 0, 2))
    partner = lax.ppermute(own, ROWS_OVER, partners)
    counts_hbm = pltpu.with_memory_space_constraint(counts, pltpu.HBM)
    heavy = announce(groups, devices, side, counts_hbm)
    heavy = lax.all_to_all(heavy, FETCH_OVER, 0, 0, tiled=True)
    heavy = heavy[:, 0, :layers]
    live_own = live.reshape(-1)
    live_partner = lax.ppermute(live, ROWS_OVER, partners)
    live_partner = live_partner.reshape(-1)
    own = mask(live_own, own)
    where = my_half.reshape(1)

    slots = jnp.transpose(tile_index, (0, 2, 1)).reshape(layers, -1, groups, tile_index.shape[1])
    table = lax.dynamic_index_in_dim(slots, my_group, 2, keepdims=False) - my_group * blocks
    table = table.reshape(-1)

    for layer in range(layers):
        last = layer == layers - 1
        if layer == 0:
            scalars, states = (where, heavy, live_partner), (own, partner)
        else:
            scalars, states = (where, heavy, live_own, live_partner), (state,)
        outgoing, used = pick(
            layer, layers, owned, groups, table, scalars, states, weight_tiles
        )
        incoming = lax.all_to_all(outgoing, FETCH_OVER, 0, 0, tiled=True)
        incoming = incoming.reshape(2 * rest, groups, owned + 1, 2, rows, side)
        result = multiply(layer, last, where, counts, incoming, used, weight_tiles, bias_terms)
        result = result.reshape((4 * rest,) + result.shape[3:])
        returned = lax.all_to_all(result, ROWS_OVER, 0, 0, tiled=True)
        state = returned.reshape((blocks,) + returned.shape[2:])
    return jnp.transpose(state, (1, 0, 2)).reshape(rows, blocks * side)


def solution(mesh):
    across, groups = mesh.shape["gx"], mesh.shape["gy"]
    split = Mesh(mesh.devices.reshape(2, 2, across // 4, groups), (HALF, PAIR, REST, GROUP))
    placed = (
        P(ROWS_OVER, GROUP),
        P(None, ROWS_OVER, GROUP),
        P(),
        P(None, GROUP, ROWS_OVER),
        P(None, GROUP, ROWS_OVER, None, None, None),
        P(None, GROUP, ROWS_OVER, None),
    )
    return jax.shard_map(
        local, mesh=split, in_specs=placed, out_specs=P(ROWS_OVER, GROUP), check_vma=False
    )
```

time: 178 us -> 180 us (1.011)
  Pallas kernels: 20.6 us -> 23.1 us
    pallas_call x4, Pallas kernels: 6.61 us -> 9.69 us  [multiply(): pl.pallas_call(functools.partial(multiply_kernel, layer, last), out_shape...]
where the time goes in v6:
time: 180 us
  blocking collectives  143 us (79%)
  Pallas kernels  23.1 us (13%)
  starting transfers between devices  10.5 us (6%)
    all_to_all x4, blocking collectives, local(): incoming = lax.all_to_all(outgoing, FETCH_OVER, 0, 0, tiled=True)  79.5 us
    all_to_all x4, blocking collectives, local(): returned = lax.all_to_all(result, ROWS_OVER, 0, 0, tiled=True)  63.4 us
    pallas_call x4, Pallas kernels, pick(): pl.pallas_call(functools.partial(pick_kernel, layer, owned, groups), out_...  10.2 us
    pallas_call x4, Pallas kernels, multiply(): pl.pallas_call(functools.partial(multiply_kernel, layer, last), out_shape...  9.69 us
    ppermute x1, starting transfers between devices, local(): partner = lax.ppermute(own, ROWS_OVER, partners)  5.08 us
    all_to_all x1, starting transfers between devices, local(): heavy = lax.all_to_all(heavy, FETCH_OVER, 0, 0, tiled=True)  3.83 us
  transfers between devices with their start and end apart: 3, of which 1 were waited for; matrix products, arithmetic and copies ran while one was open for 0% of the time, Pallas kernels for 2%

profile of v6, /device:TPU:0, one launch (start us, length us, event | category | flops | bytes accessed | tf_op | source)
XLA Modules:
  0.0 179.6 jit_solution(13654205371718821606)
XLA Ops:
  0.0 5.1 %collective-permute-start.1 = (bf16[128,8,128]{2,1,0:T(8,128)(2,1)}, bf16[128,8,128]{2,1,0:T(8,128)(2,1)S(1)}, u32[]{:S(2)}, u32[]{:S(2)}) collective-permute-start(bf16[128,8,128]{2,1,0:T(8,128)(2,1)} %bitcast.62), channel_id=1, source_target_pairs={{0,24},{4,28},{8,16},{12,20},{16,8},{20,12},{24,0},{28,4},{1,25},{... | collective-permute-start | bytes 786440 | tf_op jit(solution)/shard_map/ppermute | solution.py:287
  5.1 1.3 announce.1
  6.4 3.8 %all-to-all-start = ((s32[16,1,128]{2,1,0:T(1,128)}), s32[16,1,128]{2,1,0:T(1,128)S(1)}, u32[]{:S(2)}, u32[]{:S(2)}) async-start(s32[16,1,128]{2,1,0:T(1,128)} %announce.1), calls=%async_computation | async-start | bytes 16384 | tf_op jit(solution)/shard_map/all_to_all | solution.py:290
  10.3 1.6 collective-permute-start
  11.8 0.9 reshape.58
  12.7 1.9 %mask.1.refs_1_ = bf16[128,8,128]{2,1,0:T(8,128)(2,1)S(1)} custom-call(s32[512]{0:T(512)} %bitcast.53, bf16[128,8,128]{2,1,0:T(8,128)(2,1)} %bitcast.63), custom_call_target="tpu_custom_call" | custom-call | tf_op jit(solution)/shard_map/mask/pallas_call | solution.py:65
  14.6 1.4 collective-permute-done
  16.0 0.0 all-to-all-done
  16.0 0.0 collective-permute-done.1.refs_2_
  16.0 2.5 %shard_map.64 = (bf16[16,17,2,8,128]{4,3,2,1,0:T(8,128)(2,1)S(1)}, bf16[8,4,128,128]{3,2,1,0:T(8,128)(2,1)S(1)}) custom-call(s32[1]{0:T(128)} %bitcast.where, s32[16,4]{1,0:T(8,128)S(1)} %bitcast.43, s32[512]{0:T(512)S(1)} %bitcast.57, bf16[128,8,128]{2,1,0:T(8,128)(2,1)S(1)} %mask.1.refs_1_, bf16[128,8,128]{2,1,0:T(8,128)(2,1)S(1)} %collective-permute-done.1.refs_2_, ...), custom_call_target="tpu_custom_call" | custom-call | tf_op jit(solution)/shard_map/pallas_call | solution.py:130
  18.6 0.0 copy-start
  18.6 0.0 copy-start.1
  18.6 20.9 %all_to_all.45 = bf16[16,17,2,8,128]{4,3,2,1,0:T(8,128)(2,1)S(1)} all-to-all(bf16[16,17,2,8,128]{4,3,2,1,0:T(8,128)(2,1)S(1)} %get-tuple-element.13), channel_id=1, replica_groups=mesh['half'=2,'pair'=2,'rest'=2,'gy'=4] {'pair','rest','gy'}, dimensions={0} | all-to-all | bytes 2228224 | tf_op jit(solution)/shard_map/all_to_all | solution.py:311
  39.5 0.0 copy-done
  39.5 0.0 copy-done.1
  39.5 0.0 copy-start.2
  39.5 2.4 %shard_map.65 = bf16[2,2,2,16,2,8,128]{6,5,4,3,2,1,0:T(8,128)(2,1)S(1)} custom-call(s32[1]{0:T(128)} %bitcast.where, s32[4,16]{1,0:T(4,128)S(1)} %bitcast.48, bf16[4,4,17,2,8,128]{5,4,3,2,1,0:T(8,128)(2,1)S(1)} %bitcast.29, bf16[8,4,128,128]{3,2,1,0:T(8,128)(2,1)S(1)} %get-tuple-element.14.used_ref, bf16[4,1,16,8,128,128]{5,4,3,2,1,0:T(8,128)(2,1)} %w_hbm.7, ...), custom_call_target="tpu_custom_call" | custom-call | tf_op jit(solution)/shard_map/pallas_call | solution.py:235
  41.9 17.3 %all_to_all.46 = bf16[8,16,2,8,128]{4,3,2,1,0:T(8,128)(2,1)S(1)} all-to-all(bf16[8,16,2,8,128]{4,3,2,1,0:T(8,128)(2,1)S(1)} %bitcast.35), channel_id=1, replica_groups=mesh['half'=2,'pair'=2,'rest'=2,'gy'=4] {'half','pair','rest'}, dimensions={0} | all-to-all | bytes 1048576 | tf_op jit(solution)/shard_map/all_to_all | solution.py:315
  59.2 0.0 copy-done.2
  59.2 2.6 %shard_map.66 = (bf16[16,17,2,8,128]{4,3,2,1,0:T(8,128)(2,1)S(1)}, bf16[8,4,128,128]{3,2,1,0:T(8,128)(2,1)S(1)}) custom-call(s32[1]{0:T(128)} %bitcast.where, s32[16,4]{1,0:T(8,128)S(1)} %bitcast.44, s32[512]{0:T(512)S(1)} %bitcast.54, s32[512]{0:T(512)S(1)} %bitcast.58, bf16[128,2,8,128]{3,2,1,0:T(8,128)(2,1)S(1)} %bitcast.33, s32[4096]{0:T(1024)S(1)} %bitcast.40, ...), custom_call_target="tpu_custom_call" | custom-call | tf_op jit(solution)/shard_map/pallas_call | solution.py:130
  61.8 19.5 %all_to_all.47 = bf16[16,17,2,8,128]{4,3,2,1,0:T(8,128)(2,1)S(1)} all-to-all(bf16[16,17,2,8,128]{4,3,2,1,0:T(8,128)(2,1)S(1)} %get-tuple-element.15), channel_id=1, replica_groups=mesh['half'=2,'pair'=2,'rest'=2,'gy'=4] {'pair','rest','gy'}, dimensions={0} | all-to-all | bytes 2228224 | tf_op jit(solution)/shard_map/all_to_all | solution.py:311
  81.3 2.4 %shard_map.67 = bf16[2,2,2,16,2,8,128]{6,5,4,3,2,1,0:T(8,128)(2,1)S(1)} custom-call(s32[1]{0:T(128)} %bitcast.where, s32[4,16]{1,0:T(4,128)S(1)} %bitcast.49, bf16[4,4,17,2,8,128]{5,4,3,2,1,0:T(8,128)(2,1)S(1)} %bitcast.30, bf16[8,4,128,128]{3,2,1,0:T(8,128)(2,1)S(1)} %get-tuple-element.16.used_ref, bf16[4,1,16,8,128,128]{5,4,3,2,1,0:T(8,128)(2,1)} %w_hbm.7, ...), custom_call_target="tpu_custom_call" | custom-call | tf_op jit(solution)/shard_map/pallas_call | solution.py:235
  83.8 17.2 %all_to_all.48 = bf16[8,16,2,8,128]{4,3,2,1,0:T(8,128)(2,1)S(1)} all-to-all(bf16[8,16,2,8,128]{4,3,2,1,0:T(8,128)(2,1)S(1)} %bitcast.36), channel_id=1, replica_groups=mesh['half'=2,'pair'=2,'rest'=2,'gy'=4] {'half','pair','rest'}, dimensions={0} | all-to-all | bytes 1048576 | tf_op jit(solution)/shard_map/all_to_all | solution.py:315
  101.0 2.6 %shard_map.68 = (bf16[16,17,2,8,128]{4,3,2,1,0:T(8,128)(2,1)S(1)}, bf16[8,4,128,128]{3,2,1,0:T(8,128)(2,1)S(1)}) custom-call(s32[1]{0:T(128)} %bitcast.where, s32[16,4]{1,0:T(8,128)S(1)} %bitcast.45, s32[512]{0:T(512)S(1)} %bitcast.55, s32[512]{0:T(512)S(1)} %bitcast.59, bf16[128,2,8,128]{3,2,1,0:T(8,128)(2,1)S(1)} %bitcast.34, s32[4096]{0:T(1024)S(1)} %bitcast.41, ...), custom_call_target="tpu_custom_call" | custom-call | tf_op jit(solution)/shard_map/pallas_call | solution.py:130
  103.6 19.5 %all_to_all.49 = bf16[16,17,2,8,128]{4,3,2,1,0:T(8,128)(2,1)S(1)} all-to-all(bf16[16,17,2,8,128]{4,3,2,1,0:T(8,128)(2,1)S(1)} %get-tuple-element.17), channel_id=1, replica_groups=mesh['half'=2,'pair'=2,'rest'=2,'gy'=4] {'pair','rest','gy'}, dimensions={0} | all-to-all | bytes 2228224 | tf_op jit(solution)/shard_map/all_to_all | solution.py:311
  123.1 2.4 %shard_map.69 = bf16[2,2,2,16,2,8,128]{6,5,4,3,2,1,0:T(8,128)(2,1)S(1)} custom-call(s32[1]{0:T(128)} %bitcast.where, s32[4,16]{1,0:T(4,128)S(1)} %bitcast.50, bf16[4,4,17,2,8,128]{5,4,3,2,1,0:T(8,128)(2,1)S(1)} %bitcast.31, bf16[8,4,128,128]{3,2,1,0:T(8,128)(2,1)S(1)} %get-tuple-element.18.used_ref, bf16[4,1,16,8,128,128]{5,4,3,2,1,0:T(8,128)(2,1)} %w_hbm.7, ...), custom_call_target="tpu_custom_call" | custom-call | tf_op jit(solution)/shard_map/pallas_call | solution.py:235
  125.5 17.2 %all_to_all.50 = bf16[8,16,2,8,128]{4,3,2,1,0:T(8,128)(2,1)S(1)} all-to-all(bf16[8,16,2,8,128]{4,3,2,1,0:T(8,128)(2,1)S(1)} %bitcast.37), channel_id=1, replica_groups=mesh['half'=2,'pair'=2,'rest'=2,'gy'=4] {'half','pair','rest'}, dimensions={0} | all-to-all | bytes 1048576 | tf_op jit(solution)/shard_map/all_to_all | solution.py:315
  142.7 2.6 %shard_map.70 = (bf16[16,17,2,8,128]{4,3,2,1,0:T(8,128)(2,1)S(1)}, bf16[8,4,128,128]{3,2,1,0:T(8,128)(2,1)S(1)}) custom-call(s32[1]{0:T(128)} %bitcast.where, s32[16,4]{1,0:T(8,128)S(1)} %bitcast.46, s32[512]{0:T(512)S(1)} %bitcast.56, s32[512]{0:T(512)S(1)} %bitcast.60, bf16[128,2,8,128]{3,2,1,0:T(8,128)(2,1)S(1)} %bitcast.32, s32[4096]{0:T(1024)S(1)} %bitcast.42, ...), custom_call_target="tpu_custom_call" | custom-call | tf_op jit(solution)/shard_map/pallas_call | solution.py:130
  145.3 19.5 %all_to_all.51 = bf16[16,17,2,8,128]{4,3,2,1,0:T(8,128)(2,1)S(1)} all-to-all(bf16[16,17,2,8,128]{4,3,2,1,0:T(8,128)(2,1)S(1)} %get-tuple-element.19), channel_id=1, replica_groups=mesh['half'=2,'pair'=2,'rest'=2,'gy'=4] {'pair','rest','gy'}, dimensions={0} | all-to-all | bytes 2228224 | tf_op jit(solution)/shard_map/all_to_all | solution.py:311
  164.8 2.4 %shard_map.71 = bf16[2,2,2,16,8,128]{5,4,3,2,1,0:T(8,128)(2,1)S(1)} custom-call(s32[1]{0:T(128)} %bitcast.where, s32[4,16]{1,0:T(4,128)S(1)} %bitcast.51, bf16[4,4,17,2,8,128]{5,4,3,2,1,0:T(8,128)(2,1)S(1)} %bitcast.28, bf16[8,4,128,128]{3,2,1,0:T(8,128)(2,1)S(1)} %get-tuple-element.20.used_ref, bf16[4,1,16,8,128,128]{5,4,3,2,1,0:T(8,128)(2,1)} %w_hbm.7, ...), custom_call_target="tpu_custom_call" | custom-call | tf_op jit(solution)/shard_map/pallas_call | solution.py:235
  167.3 11.6 %all_to_all.52 = bf16[8,16,8,128]{3,2,1,0:T(8,128)(2,1)S(1)} all-to-all(bf16[8,16,8,128]{3,2,1,0:T(8,128)(2,1)S(1)} %bitcast.38), channel_id=1, replica_groups=mesh['half'=2,'pair'=2,'rest'=2,'gy'=4] {'half','pair','rest'}, dimensions={0} | all-to-all | bytes 524288 | tf_op jit(solution)/shard_map/all_to_all | solution.py:315
  178.9 0.7 copy.14
  (1 shorter events, 0.0 us)
Async XLA Ops:
  0.0 16.0 %collective-permute-start.1 = (bf16[128,8,128]{2,1,0:T(8,128)(2,1)}, bf16[128,8,128]{2,1,0:T(8,128)(2,1)S(1)}, u32[]{:S(2)}, u32[]{:S(2)}) collective-permute-start(bf16[128,8,128]{2,1,0:T(8,128)(2,1)} %bitcast.62), channel_id=1, source_target_pairs={{0,24},{4,28},{8,16},{12,20},{16,8},{20,12},{24,0},{28,4},{1,25},{... | collective-permute-start | bytes 786440 | tf_op jit(solution)/shard_map/ppermute | solution.py:287
  6.4 9.6 %all-to-all-start = ((s32[16,1,128]{2,1,0:T(1,128)}), s32[16,1,128]{2,1,0:T(1,128)S(1)}, u32[]{:S(2)}, u32[]{:S(2)}) async-start(s32[16,1,128]{2,1,0:T(1,128)} %announce.1), calls=%async_computation | async-start | bytes 16384 | tf_op jit(solution)/shard_map/all_to_all | solution.py:290
  10.3 5.8 %collective-permute-start = (s32[4,128]{1,0:T(4,128)}, s32[4,128]{1,0:T(4,128)S(1)}, u32[]{:S(2)}, u32[]{:S(2)}) collective-permute-start(s32[4,128]{1,0:T(4,128)} %bitcast.52), channel_id=1, source_target_pairs={{0,24},{4,28},{8,16},{12,20},{16,8},{20,12},{24,0},{28,4},{1,25},{... | collective-permute-start | bytes 6152 | tf_op jit(solution)/shard_map/ppermute | solution.py:293
  18.6 20.9 %copy-start = (f32[4,1,16,128]{3,2,1,0:T(8,128)S(1)}, f32[4,1,16,128]{3,2,1,0:T(8,128)}, u32[]{:S(2)}) copy-start(f32[4,1,16,128]{3,2,1,0:T(8,128)} %bias_ref.7) | copy-start | bytes 98308
  18.6 20.9 %copy-start.1 = (s32[4,1,16]{2,1,0:T(1,128)S(1)}, s32[4,1,16]{2,1,0:T(1,128)}, u32[]{:S(2)}) copy-start(s32[4,1,16]{2,1,0:T(1,128)} %param.9) | copy-start | bytes 772
  39.5 19.8 %copy-start.2 = (s32[4,1,128]{2,1,0:T(1,128)S(1)}, s32[4,1,128]{2,1,0:T(1,128)}, u32[]{:S(2)}) copy-start(s32[4,1,128]{2,1,0:T(1,128)} %param.7) | copy-start | bytes 6148

commit v7 on v6

--- a/solution.py
+++ b/solution.py
@@ -76,12 +76,20 @@
 def pick_kernel(layer, owned, groups, where, heavy, *refs):
     half = where[0]
     batch = 8
-    *live_refs, table, w_hbm, out_ref, used_ref, kept_ref, sem = refs
+    if layer == 0:
+        counts, *live_refs, table, w_hbm, out_ref, used_ref, rest_ref, kept_ref, sems = refs
+        extra = heavy_of(counts, layer, groups)
+        fetches = (
+            pltpu.make_async_copy(w_hbm.at[layer, 0, :, pl.ds(0, groups)], used_ref, sems.at[0]),
+            pltpu.make_async_copy(
+                w_hbm.at[layer, 0, extra, pl.ds(groups, groups)], rest_ref, sems.at[1]
+            ),
+        )
+        for fetch in fetches:
+            fetch.start()
+    else:
+        *live_refs, table, out_ref, kept_ref = refs
     blocks = kept_ref.shape[0]
-    fetch = pltpu.make_async_copy(
-        w_hbm.at[layer, 0, pl.ds(0, used_ref.shape[0]), pl.ds(0, groups)], used_ref, sem
-    )
-    fetch.start()
 
     def mask(b, carry):
         first = b * batch
@@ -116,71 +124,51 @@
         return carry
 
     lax.fori_loop(0, across, one_owner, 0)
-    fetch.wait()
-
-
-def early(owned):
-    return owned // 2 if owned % 2 == 0 else owned
+    if layer == 0:
+        for fetch in fetches:
+            fetch.wait()
+
+
+def whole(shape):
+    return pl.BlockSpec(shape, lambda i, *_: (0,) * len(shape))
 
 
 def pick(layer, layers, owned, groups, table, scalars, states, weight_tiles):
     blocks, (rows, side) = states[0].shape[0], states[0].shape[-2:]
     devices = scalars[1].shape[0]
-    shapes = ((devices, owned + 1, 2, rows, side), (early(owned), groups, side, side))
+    piece = pl.BlockSpec(
+        (table.shape[0] // layers,), lambda i, *_: (layer,), memory_space=pltpu.SMEM
+    )
+    operands = [*states, table]
+    in_specs = [whole(state.shape) for state in states] + [piece]
+    shapes = [(devices, owned + 1, 2, rows, side)]
+    scratch = [pltpu.VMEM((blocks, 2, rows, side), states[0].dtype)]
+    if layer == 0:
+        operands.append(pltpu.with_memory_space_constraint(weight_tiles, pltpu.HBM))
+        in_specs.append(pl.BlockSpec(memory_space=pl.ANY))
+        shapes += [(owned, groups, side, side), (groups, side, side)]
+        scratch.append(pltpu.SemaphoreType.DMA((2,)))
     return pl.pallas_call(
         functools.partial(pick_kernel, layer, owned, groups),
-        out_shape=tuple(jax.ShapeDtypeStruct(shape, weight_tiles.dtype) for shape in shapes),
+        out_shape=[jax.ShapeDtypeStruct(shape, states[0].dtype) for shape in shapes],
         grid_spec=pltpu.PrefetchScalarGridSpec(
             num_scalar_prefetch=len(scalars),
             grid=(1,),
-            in_specs=[
-                pl.BlockSpec(state.shape, lambda i, *_, n=state.ndim: (0,) * n) for state in states
-            ]
-            + [
-                pl.BlockSpec(
-                    (table.shape[0] // layers,), lambda i, *_: (layer,), memory_space=pltpu.SMEM
-                ),
-                pl.BlockSpec(memory_space=pl.ANY),
-            ],
-            out_specs=tuple(
-                pl.BlockSpec(shape, lambda i, *_, n=len(shape): (0,) * n) for shape in shapes
-            ),
-            scratch_shapes=[
-                pltpu.VMEM((blocks, 2, rows, side), states[0].dtype),
-                pltpu.SemaphoreType.DMA,
-            ],
-        ),
-        compiler_params=pltpu.CompilerParams(vmem_limit_bytes=12 << 20),
-    )(*scalars, *states, table, pltpu.with_memory_space_constraint(weight_tiles, pltpu.HBM))
-
-
-def multiply_kernel(
-    layer, last, where, counts, x_ref, used_ref, w_hbm, bias_ref, out_ref, acc_ref, late_ref, rest_ref, sems
-):
-    step = pl.program_id(0)
-    steps = pl.num_programs(0)
+            in_specs=in_specs,
+            out_specs=[whole(shape) for shape in shapes],
+            scratch_shapes=scratch,
+        ),
+        compiler_params=pltpu.CompilerParams(vmem_limit_bytes=(12 if layer == 0 else 6) << 20),
+    )(*scalars, *operands)
+
+
+def multiply_kernel(layer, last, where, counts, x_ref, *refs):
+    *w_refs, bias_ref, out_ref, acc_ref = refs
     across, groups, _, _, rows, side = x_ref.shape
     owned = counts.shape[1]
-    chunk = used_ref.shape[0]
     total_rows = across * 2 * rows
     half = where[0]
     heavy = heavy_of(counts, layer, groups)
-    fetches = [
-        pltpu.make_async_copy(
-            w_hbm.at[layer, 0, heavy, pl.ds(groups, groups)], rest_ref, sems.at[0]
-        )
-    ]
-    if chunk < owned:
-        fetches.append(
-            pltpu.make_async_copy(
-                w_hbm.at[layer, 0, pl.ds(chunk, chunk), pl.ds(0, groups)], late_ref, sems.at[1]
-            )
-        )
-
-    @pl.when(step == 0)
-    def _():
-        for fetch in reversed(fetches):
-            fetch.start()
 
     def gathered(position, first, count):
         parts = []
@@ -202,34 +190,23 @@
         out_ref[1 - half, 0, :, k] = far[1]
         out_ref[1 - half, 1, :, k] = far[0]
 
-    def blocks_of(first, weights):
-        for c in range(chunk):
-            k = first + c
-            weight = weights[c].reshape(groups * side, side)
-            summed = jnp.dot(
-                gathered(k, 0, counts[layer, k]), weight, preferred_element_type=jnp.float32
-            )
-            summed = summed + bias_ref[0, 0, k : k + 1, :]
-            acc_ref[k] = summed
-            write(k, summed)
-
-    @pl.when(step == 0)
-    def _():
-        blocks_of(0, used_ref)
-
-    @pl.when(step == steps - 1)
-    def _():
-        for fetch in fetches:
-            fetch.wait()
-        if chunk < owned:
-            blocks_of(chunk, late_ref)
-        lhs = gathered(owned, groups, counts[layer, heavy])
-        weight = rest_ref[...].reshape(groups * side, side)
-        write(heavy, acc_ref[heavy] + jnp.dot(lhs, weight, preferred_element_type=jnp.float32))
-
-
-def multiply(layer, last, where, counts, incoming, used, weight_tiles, bias_terms):
-    across, groups, width, _, rows, side = incoming.shape
+    def product(position, first, count, weight):
+        weight = weight.reshape(groups * side, side)
+        lhs = gathered(position, first, count)
+        return jnp.dot(lhs, weight, preferred_element_type=jnp.float32)
+
+    for k in range(owned):
+        weight = w_refs[0][k] if layer == 0 else w_refs[0][layer, 0, k, :groups]
+        summed = product(k, 0, counts[layer, k], weight) + bias_ref[0, 0, k : k + 1, :]
+        acc_ref[k] = summed
+        write(k, summed)
+
+    weight = w_refs[1][...] if layer == 0 else w_refs[0][layer, 0, heavy, groups:]
+    write(heavy, acc_ref[heavy] + product(owned, groups, counts[layer, heavy], weight))
+
+
+def multiply(layer, last, where, counts, incoming, weights, bias_terms):
+    across, _, width, _, rows, side = incoming.shape
     owned = width - 1
     out = (2, 2, across // 2, owned) + (() if last else (2,)) + (rows, side)
     return pl.pallas_call(
@@ -237,30 +214,17 @@
         out_shape=jax.ShapeDtypeStruct(out, incoming.dtype),
         grid_spec=pltpu.PrefetchScalarGridSpec(
             num_scalar_prefetch=2,
-            grid=(owned // used.shape[0],),
+            grid=(1,),
             in_specs=[
-                pl.BlockSpec(incoming.shape, lambda i, *_: (0,) * incoming.ndim),
-                pl.BlockSpec(used.shape, lambda i, *_: (0, 0, 0, 0)),
-                pl.BlockSpec(memory_space=pl.ANY),
+                whole(incoming.shape),
+                *(whole(weight.shape) for weight in weights),
                 pl.BlockSpec((1, 1, owned, side), lambda i, *_: (layer, 0, 0, 0)),
             ],
-            out_specs=pl.BlockSpec(out, lambda i, *_: (0,) * len(out)),
-            scratch_shapes=[
-                pltpu.VMEM((owned, across * 2 * rows, side), jnp.float32),
-                pltpu.VMEM(used.shape, used.dtype),
-                pltpu.VMEM((groups, side, side), used.dtype),
-                pltpu.SemaphoreType.DMA((2,)),
-            ],
-        ),
-        compiler_params=pltpu.CompilerParams(vmem_limit_bytes=12 << 20),
-    )(
-        where,
-        counts,
-        incoming,
-        used,
-        pltpu.with_memory_space_constraint(weight_tiles, pltpu.HBM),
-        bias_terms,
-    )
+            out_specs=whole(out),
+            scratch_shapes=[pltpu.VMEM((owned, across * 2 * rows, side), jnp.float32)],
+        ),
+        compiler_params=pltpu.CompilerParams(vmem_limit_bytes=(12 if layer == 0 else 24) << 20),
+    )(where, counts, incoming, *weights, bias_terms)
 
 
 def local(activations, live_blocks, tile_index, tile_count, weight_tiles, bias_terms):
@@ -302,15 +266,16 @@
     for layer in range(layers):
         last = layer == layers - 1
         if layer == 0:
-            scalars, states = (where, heavy, live_partner), (own, partner)
+            scalars, states = (where, heavy, counts_hbm, live_partner), (own, partner)
         else:
             scalars, states = (where, heavy, live_own, live_partner), (state,)
-        outgoing, used = pick(
+        outgoing, *weights = pick(
             layer, layers, owned, groups, table, scalars, states, weight_tiles
         )
+        weights = weights or [weight_tiles]
         incoming = lax.all_to_all(outgoing, FETCH_OVER, 0, 0, tiled=True)
         incoming = incoming.reshape(2 * rest, groups, owned + 1, 2, rows, side)
-        result = multiply(layer, last, where, counts, incoming, used, weight_tiles, bias_terms)
+        result = multiply(layer, last, where, counts, incoming, weights, bias_terms)
         result = result.reshape((4 * rest,) + result.shape[3:])
         returned = lax.all_to_all(result, ROWS_OVER, 0, 0, tiled=True)
         state = returned.reshape((blocks,) + returned.shape[2:])

time: 180 us -> 175 us (0.972)
  Pallas kernels: 23.1 us -> 17.8 us
    pallas_call x4, Pallas kernels: 9.69 us -> 4.46 us  [multiply(): pl.pallas_call(functools.partial(multiply_kernel, layer, last), out_shape...]
  transfers between devices with their start and end apart: 3 -> 3, of which waited for: 1 -> 1; matrix products, arithmetic and copies ran while one was open for 0% -> 1% of each run, Pallas kernels for 2% -> 2%
where the time goes in v7:
time: 175 us
  blocking collectives  143 us (82%)
  Pallas kernels  17.8 us (10%)
  starting transfers between devices  10.5 us (6%)
    all_to_all x4, blocking collectives, local(): incoming = lax.all_to_all(outgoing, FETCH_OVER, 0, 0, tiled=True)  79.8 us
    all_to_all x4, blocking collectives, local(): returned = lax.all_to_all(result, ROWS_OVER, 0, 0, tiled=True)  63.4 us
    pallas_call x4, Pallas kernels, pick(): pl.pallas_call(functools.partial(pick_kernel, layer, owned, groups), out_...  10.1 us
    ppermute x1, starting transfers between devices, local(): partner = lax.ppermute(own, ROWS_OVER, partners)  5.08 us
    pallas_call x4, Pallas kernels, multiply(): pl.pallas_call(functools.partial(multiply_kernel, layer, last), out_shape...  4.46 us
    all_to_all x1, starting transfers between devices, local(): heavy = lax.all_to_all(heavy, FETCH_OVER, 0, 0, tiled=True)  3.83 us
  transfers between devices with their start and end apart: 3, of which 1 were waited for; matrix products, arithmetic and copies ran while one was open for 1% of the time, Pallas kernels for 2%

profile of v7, /device:TPU:0, one launch (start us, length us, event | category | flops | bytes accessed | tf_op | source)
XLA Modules:
  0.0 174.5 jit_solution(1072953729094410622)
XLA Ops:
  0.0 5.1 %collective-permute-start.1 = (bf16[128,8,128]{2,1,0:T(8,128)(2,1)}, bf16[128,8,128]{2,1,0:T(8,128)(2,1)S(1)}, u32[]{:S(2)}, u32[]{:S(2)}) collective-permute-start(bf16[128,8,128]{2,1,0:T(8,128)(2,1)} %bitcast.63), channel_id=1, source_target_pairs={{0,24},{4,28},{8,16},{12,20},{16,8},{20,12},{24,0},{28,4},{1,25},{... | collective-permute-start | bytes 786440 | tf_op jit(solution)/shard_map/ppermute | solution.py:251
  5.1 1.3 announce.1
  6.4 3.8 %all-to-all-start = ((s32[16,1,128]{2,1,0:T(1,128)}), s32[16,1,128]{2,1,0:T(1,128)S(1)}, u32[]{:S(2)}, u32[]{:S(2)}) async-start(s32[16,1,128]{2,1,0:T(1,128)} %announce.1), calls=%async_computation | async-start | bytes 16384 | tf_op jit(solution)/shard_map/all_to_all | solution.py:254
  10.3 1.6 collective-permute-start
  11.8 0.9 reshape.58
  12.7 1.9 %mask.1.refs_2_ = bf16[128,8,128]{2,1,0:T(8,128)(2,1)S(1)} custom-call(s32[512]{0:T(512)} %bitcast.54, bf16[128,8,128]{2,1,0:T(8,128)(2,1)} %bitcast.64), custom_call_target="tpu_custom_call" | custom-call | tf_op jit(solution)/shard_map/mask/pallas_call | solution.py:65
  14.6 1.4 collective-permute-done
  16.0 0.0 all-to-all-done
  16.0 0.0 collective-permute-done.1.refs_3_
  16.0 0.0 copy-start
  16.0 3.8 %shard_map.64 = (bf16[16,17,2,8,128]{4,3,2,1,0:T(8,128)(2,1)S(1)}, bf16[16,4,128,128]{3,2,1,0:T(8,128)(2,1)S(1)}, bf16[4,128,128]{2,1,0:T(8,128)(2,1)S(1)}) custom-call(s32[1]{0:T(128)} %bitcast.where, s32[16,4]{1,0:T(8,128)S(1)} %bitcast.43, s32[4,16]{1,0:T(4,128)} %bitcast.48, s32[512]{0:T(512)S(1)} %bitcast.58, bf16[128,8,128]{2,1,0:T(8,128)(2,1)S(1)} %mask.1.refs_2_, ...), custom_call_target="tpu_custom_call" | custom-call | tf_op jit(solution)/shard_map/pallas_call | solution.py:151
  19.9 0.0 copy-start.1
  19.9 0.0 copy-start.2
  19.9 21.2 %all_to_all.45 = bf16[16,17,2,8,128]{4,3,2,1,0:T(8,128)(2,1)S(1)} all-to-all(bf16[16,17,2,8,128]{4,3,2,1,0:T(8,128)(2,1)S(1)} %get-tuple-element.8), channel_id=1, replica_groups=mesh['half'=2,'pair'=2,'rest'=2,'gy'=4] {'pair','rest','gy'}, dimensions={0} | all-to-all | bytes 2228224 | tf_op jit(solution)/shard_map/all_to_all | solution.py:276
  41.0 0.0 copy-done.1
  41.0 0.0 copy-done.2
  41.0 0.0 copy-start.3
  41.0 1.1 shard_map.65
  42.2 17.3 %all_to_all.46 = bf16[8,16,2,8,128]{4,3,2,1,0:T(8,128)(2,1)S(1)} all-to-all(bf16[8,16,2,8,128]{4,3,2,1,0:T(8,128)(2,1)S(1)} %bitcast.37), channel_id=1, replica_groups=mesh['half'=2,'pair'=2,'rest'=2,'gy'=4] {'half','pair','rest'}, dimensions={0} | all-to-all | bytes 1048576 | tf_op jit(solution)/shard_map/all_to_all | solution.py:280
  59.5 0.0 copy-done.3
  59.5 2.1 %shard_map.66 = bf16[16,17,2,8,128]{4,3,2,1,0:T(8,128)(2,1)S(1)} custom-call(s32[1]{0:T(128)} %bitcast.where, s32[16,4]{1,0:T(8,128)S(1)} %bitcast.44, s32[512]{0:T(512)S(1)} %bitcast.55, s32[512]{0:T(512)S(1)} %bitcast.59, bf16[128,2,8,128]{3,2,1,0:T(8,128)(2,1)S(1)} %bitcast.35, s32[4096]{0:T(1024)S(1)} %bitcast.40), custom_call_target="tpu_custom_call" | custom-call | tf_op jit(solution)/shard_map/pallas_call | solution.py:151
  61.6 19.5 %all_to_all.47 = bf16[16,17,2,8,128]{4,3,2,1,0:T(8,128)(2,1)S(1)} all-to-all(bf16[16,17,2,8,128]{4,3,2,1,0:T(8,128)(2,1)S(1)} %shard_map.66), channel_id=1, replica_groups=mesh['half'=2,'pair'=2,'rest'=2,'gy'=4] {'pair','rest','gy'}, dimensions={0} | all-to-all | bytes 2228224 | tf_op jit(solution)/shard_map/all_to_all | solution.py:276
  81.1 0.0 copy-done
  81.1 1.1 shard_map.67
  82.2 17.2 %all_to_all.48 = bf16[8,16,2,8,128]{4,3,2,1,0:T(8,128)(2,1)S(1)} all-to-all(bf16[8,16,2,8,128]{4,3,2,1,0:T(8,128)(2,1)S(1)} %bitcast.32), channel_id=1, replica_groups=mesh['half'=2,'pair'=2,'rest'=2,'gy'=4] {'half','pair','rest'}, dimensions={0} | all-to-all | bytes 1048576 | tf_op jit(solution)/shard_map/all_to_all | solution.py:280
  99.5 2.1 %shard_map.68 = bf16[16,17,2,8,128]{4,3,2,1,0:T(8,128)(2,1)S(1)} custom-call(s32[1]{0:T(128)} %bitcast.where, s32[16,4]{1,0:T(8,128)S(1)} %bitcast.45, s32[512]{0:T(512)S(1)} %bitcast.56, s32[512]{0:T(512)S(1)} %bitcast.60, bf16[128,2,8,128]{3,2,1,0:T(8,128)(2,1)S(1)} %bitcast.36, s32[4096]{0:T(1024)S(1)} %bitcast.41), custom_call_target="tpu_custom_call" | custom-call | tf_op jit(solution)/shard_map/pallas_call | solution.py:151
  101.6 19.5 %all_to_all.49 = bf16[16,17,2,8,128]{4,3,2,1,0:T(8,128)(2,1)S(1)} all-to-all(bf16[16,17,2,8,128]{4,3,2,1,0:T(8,128)(2,1)S(1)} %shard_map.68), channel_id=1, replica_groups=mesh['half'=2,'pair'=2,'rest'=2,'gy'=4] {'pair','rest','gy'}, dimensions={0} | all-to-all | bytes 2228224 | tf_op jit(solution)/shard_map/all_to_all | solution.py:276
  121.1 1.1 shard_map.69
  122.2 17.2 %all_to_all.50 = bf16[8,16,2,8,128]{4,3,2,1,0:T(8,128)(2,1)S(1)} all-to-all(bf16[8,16,2,8,128]{4,3,2,1,0:T(8,128)(2,1)S(1)} %bitcast.33), channel_id=1, replica_groups=mesh['half'=2,'pair'=2,'rest'=2,'gy'=4] {'half','pair','rest'}, dimensions={0} | all-to-all | bytes 1048576 | tf_op jit(solution)/shard_map/all_to_all | solution.py:280
  139.4 2.1 %shard_map.70 = bf16[16,17,2,8,128]{4,3,2,1,0:T(8,128)(2,1)S(1)} custom-call(s32[1]{0:T(128)} %bitcast.where, s32[16,4]{1,0:T(8,128)S(1)} %bitcast.46, s32[512]{0:T(512)S(1)} %bitcast.57, s32[512]{0:T(512)S(1)} %bitcast.61, bf16[128,2,8,128]{3,2,1,0:T(8,128)(2,1)S(1)} %bitcast.34, s32[4096]{0:T(1024)S(1)} %bitcast.42), custom_call_target="tpu_custom_call" | custom-call | tf_op jit(solution)/shard_map/pallas_call | solution.py:151
  141.5 19.5 %all_to_all.51 = bf16[16,17,2,8,128]{4,3,2,1,0:T(8,128)(2,1)S(1)} all-to-all(bf16[16,17,2,8,128]{4,3,2,1,0:T(8,128)(2,1)S(1)} %shard_map.70), channel_id=1, replica_groups=mesh['half'=2,'pair'=2,'rest'=2,'gy'=4] {'pair','rest','gy'}, dimensions={0} | all-to-all | bytes 2228224 | tf_op jit(solution)/shard_map/all_to_all | solution.py:276
  161.1 1.1 shard_map.71
  162.2 11.6 %all_to_all.52 = bf16[8,16,8,128]{3,2,1,0:T(8,128)(2,1)S(1)} all-to-all(bf16[8,16,8,128]{3,2,1,0:T(8,128)(2,1)S(1)} %bitcast.38), channel_id=1, replica_groups=mesh['half'=2,'pair'=2,'rest'=2,'gy'=4] {'half','pair','rest'}, dimensions={0} | all-to-all | bytes 524288 | tf_op jit(solution)/shard_map/all_to_all | solution.py:280
  173.8 0.7 copy.14
  (1 shorter events, 0.0 us)
Async XLA Ops:
  0.0 16.0 %collective-permute-start.1 = (bf16[128,8,128]{2,1,0:T(8,128)(2,1)}, bf16[128,8,128]{2,1,0:T(8,128)(2,1)S(1)}, u32[]{:S(2)}, u32[]{:S(2)}) collective-permute-start(bf16[128,8,128]{2,1,0:T(8,128)(2,1)} %bitcast.63), channel_id=1, source_target_pairs={{0,24},{4,28},{8,16},{12,20},{16,8},{20,12},{24,0},{28,4},{1,25},{... | collective-permute-start | bytes 786440 | tf_op jit(solution)/shard_map/ppermute | solution.py:251
  6.4 9.6 %all-to-all-start = ((s32[16,1,128]{2,1,0:T(1,128)}), s32[16,1,128]{2,1,0:T(1,128)S(1)}, u32[]{:S(2)}, u32[]{:S(2)}) async-start(s32[16,1,128]{2,1,0:T(1,128)} %announce.1), calls=%async_computation | async-start | bytes 16384 | tf_op jit(solution)/shard_map/all_to_all | solution.py:254
  10.3 5.8 %collective-permute-start = (s32[4,128]{1,0:T(4,128)}, s32[4,128]{1,0:T(4,128)S(1)}, u32[]{:S(2)}, u32[]{:S(2)}) collective-permute-start(s32[4,128]{1,0:T(4,128)} %bitcast.53), channel_id=1, source_target_pairs={{0,24},{4,28},{8,16},{12,20},{16,8},{20,12},{24,0},{28,4},{1,25},{... | collective-permute-start | bytes 6152 | tf_op jit(solution)/shard_map/ppermute | solution.py:257
  16.0 65.1 %copy-start = (bf16[4,1,16,8,128,128]{5,4,3,2,1,0:T(8,128)(2,1)S(1)}, bf16[4,1,16,8,128,128]{5,4,3,2,1,0:T(8,128)(2,1)}, u32[]{:S(2)}) copy-start(bf16[4,1,16,8,128,128]{5,4,3,2,1,0:T(8,128)(2,1)} %refs_0_.5) | copy-start | bytes 50331652
  19.9 21.2 %copy-start.1 = (f32[4,1,16,128]{3,2,1,0:T(8,128)S(1)}, f32[4,1,16,128]{3,2,1,0:T(8,128)}, u32[]{:S(2)}) copy-start(f32[4,1,16,128]{3,2,1,0:T(8,128)} %refs_1_.5) | copy-start | bytes 98308
  19.9 21.2 %copy-start.2 = (s32[4,1,16]{2,1,0:T(1,128)S(1)}, s32[4,1,16]{2,1,0:T(1,128)}, u32[]{:S(2)}) copy-start(s32[4,1,16]{2,1,0:T(1,128)} %param.9) | copy-start | bytes 772
  41.0 18.5 %copy-start.3 = (s32[4,1,128]{2,1,0:T(1,128)S(1)}, s32[4,1,128]{2,1,0:T(1,128)}, u32[]{:S(2)}) copy-start(s32[4,1,128]{2,1,0:T(1,128)} %param.7) | copy-start | bytes 6148

commit v8 on v7

--- a/solution.py
+++ b/solution.py
@@ -73,22 +73,10 @@
     )(live, own)
 
 
-def pick_kernel(layer, owned, groups, where, heavy, *refs):
+def pick_kernel(layer, layers, owned, groups, where, table, heavy, *refs):
     half = where[0]
     batch = 8
-    if layer == 0:
-        counts, *live_refs, table, w_hbm, out_ref, used_ref, rest_ref, kept_ref, sems = refs
-        extra = heavy_of(counts, layer, groups)
-        fetches = (
-            pltpu.make_async_copy(w_hbm.at[layer, 0, :, pl.ds(0, groups)], used_ref, sems.at[0]),
-            pltpu.make_async_copy(
-                w_hbm.at[layer, 0, extra, pl.ds(groups, groups)], rest_ref, sems.at[1]
-            ),
-        )
-        for fetch in fetches:
-            fetch.start()
-    else:
-        *live_refs, table, out_ref, kept_ref = refs
+    *live_refs, out_ref, kept_ref = refs
     blocks = kept_ref.shape[0]
 
     def mask(b, carry):
@@ -112,11 +100,11 @@
     lax.fori_loop(0, blocks // batch, mask, 0)
 
     across = out_ref.shape[0] // groups
-    slots = table.shape[0] // 2
+    slots = table.shape[0] // (2 * layers)
 
     def one_owner(owner, carry):
         for g in range(groups):
-            first = g * blocks + (half * across + owner) * owned
+            first = 2 * layer * slots + g * blocks + (half * across + owner) * owned
             spots = [table[first + k] for k in range(owned)]
             spots.append(table[first + slots + heavy[owner * groups + g, layer]])
             for k, spot in enumerate(spots):
@@ -124,46 +112,32 @@
         return carry
 
     lax.fori_loop(0, across, one_owner, 0)
-    if layer == 0:
-        for fetch in fetches:
-            fetch.wait()
 
 
 def whole(shape):
     return pl.BlockSpec(shape, lambda i, *_: (0,) * len(shape))
 
 
-def pick(layer, layers, owned, groups, table, scalars, states, weight_tiles):
+def pick(layer, layers, owned, groups, scalars, states, cost):
     blocks, (rows, side) = states[0].shape[0], states[0].shape[-2:]
-    devices = scalars[1].shape[0]
-    piece = pl.BlockSpec(
-        (table.shape[0] // layers,), lambda i, *_: (layer,), memory_space=pltpu.SMEM
-    )
-    operands = [*states, table]
-    in_specs = [whole(state.shape) for state in states] + [piece]
-    shapes = [(devices, owned + 1, 2, rows, side)]
-    scratch = [pltpu.VMEM((blocks, 2, rows, side), states[0].dtype)]
-    if layer == 0:
-        operands.append(pltpu.with_memory_space_constraint(weight_tiles, pltpu.HBM))
-        in_specs.append(pl.BlockSpec(memory_space=pl.ANY))
-        shapes += [(owned, groups, side, side), (groups, side, side)]
-        scratch.append(pltpu.SemaphoreType.DMA((2,)))
-    return pl.pallas_call(
-        functools.partial(pick_kernel, layer, owned, groups),
-        out_shape=[jax.ShapeDtypeStruct(shape, states[0].dtype) for shape in shapes],
+    devices = scalars[2].shape[0]
+    shape = (devices, owned + 1, 2, rows, side)
+    return pl.pallas_call(
+        functools.partial(pick_kernel, layer, layers, owned, groups),
+        out_shape=jax.ShapeDtypeStruct(shape, states[0].dtype),
         grid_spec=pltpu.PrefetchScalarGridSpec(
             num_scalar_prefetch=len(scalars),
             grid=(1,),
-            in_specs=in_specs,
-            out_specs=[whole(shape) for shape in shapes],
-            scratch_shapes=scratch,
-        ),
-        compiler_params=pltpu.CompilerParams(vmem_limit_bytes=(12 if layer == 0 else 6) << 20),
-    )(*scalars, *operands)
-
-
-def multiply_kernel(layer, last, where, counts, x_ref, *refs):
-    *w_refs, bias_ref, out_ref, acc_ref = refs
+            in_specs=[whole(state.shape) for state in states],
+            out_specs=whole(shape),
+            scratch_shapes=[pltpu.VMEM((blocks, 2, rows, side), states[0].dtype)],
+        ),
+        compiler_params=pltpu.CompilerParams(vmem_limit_bytes=6 << 20),
+        cost_estimate=cost,
+    )(*scalars, *states)
+
+
+def multiply_kernel(layer, last, where, counts, x_ref, w_ref, bias_ref, out_ref, acc_ref):
     across, groups, _, _, rows, side = x_ref.shape
     owned = counts.shape[1]
     total_rows = across * 2 * rows
@@ -196,16 +170,16 @@
         return jnp.dot(lhs, weight, preferred_element_type=jnp.float32)
 
     for k in range(owned):
-        weight = w_refs[0][k] if layer == 0 else w_refs[0][layer, 0, k, :groups]
+        weight = w_ref[layer, 0, k, :groups]
         summed = product(k, 0, counts[layer, k], weight) + bias_ref[0, 0, k : k + 1, :]
         acc_ref[k] = summed
         write(k, summed)
 
-    weight = w_refs[1][...] if layer == 0 else w_refs[0][layer, 0, heavy, groups:]
+    weight = w_ref[layer, 0, heavy, groups:]
     write(heavy, acc_ref[heavy] + product(owned, groups, counts[layer, heavy], weight))
 
 
-def multiply(layer, last, where, counts, incoming, weights, bias_terms):
+def multiply(layer, last, where, counts, incoming, weight_tiles, bias_terms):
     across, _, width, _, rows, side = incoming.shape
     owned = width - 1
     out = (2, 2, across // 2, owned) + (() if last else (2,)) + (rows, side)
@@ -217,14 +191,14 @@
             grid=(1,),
             in_specs=[
                 whole(incoming.shape),
-                *(whole(weight.shape) for weight in weights),
+                whole(weight_tiles.shape),
                 pl.BlockSpec((1, 1, owned, side), lambda i, *_: (layer, 0, 0, 0)),
             ],
             out_specs=whole(out),
             scratch_shapes=[pltpu.VMEM((owned, across * 2 * rows, side), jnp.float32)],
         ),
-        compiler_params=pltpu.CompilerParams(vmem_limit_bytes=(12 if layer == 0 else 24) << 20),
-    )(where, counts, incoming, *weights, bias_terms)
+        compiler_params=pltpu.CompilerParams(vmem_limit_bytes=24 << 20),
+    )(where, counts, incoming, weight_tiles, bias_terms)
 
 
 def local(activations, live_blocks, tile_index, tile_count, weight_tiles, bias_terms):
@@ -266,16 +240,15 @@
     for layer in range(layers):
         last = layer == layers - 1
         if layer == 0:
-            scalars, states = (where, heavy, counts_hbm, live_partner), (own, partner)
+            scalars, states = (where, table, heavy, live_partner), (own, partner)
+            cost = pl.CostEstimate(flops=10**11, transcendentals=0, bytes_accessed=64 << 20)
         else:
-            scalars, states = (where, heavy, live_own, live_partner), (state,)
-        outgoing, *weights = pick(
-            layer, layers, owned, groups, table, scalars, states, weight_tiles
-        )
-        weights = weights or [weight_tiles]
+            scalars, states = (where, table, heavy, live_own, live_partner), (state,)
+            cost = None
+        outgoing = pick(layer, layers, owned, groups, scalars, states, cost)
         incoming = lax.all_to_all(outgoing, FETCH_OVER, 0, 0, tiled=True)
         incoming = incoming.reshape(2 * rest, groups, owned + 1, 2, rows, side)
-        result = multiply(layer, last, where, counts, incoming, weights, bias_terms)
+        result = multiply(layer, last, where, counts, incoming, weight_tiles, bias_terms)
         result = result.reshape((4 * rest,) + result.shape[3:])
         returned = lax.all_to_all(result, ROWS_OVER, 0, 0, tiled=True)
         state = returned.reshape((blocks,) + returned.shape[2:])

time: 175 us -> 172 us (0.983)
  Pallas kernels: 17.8 us -> 14.6 us
    pallas_call x4, Pallas kernels: 10.1 us -> 6.9 us  [pick(): pl.pallas_call(functools.partial(pick_kernel, layer, layers, owned, group...]
where the time goes in v8:
time: 172 us; the launch traced here: 171 us
  blocking collectives  143 us (83%)
  Pallas kernels  14.6 us (8%)
  starting transfers between devices  10.5 us (6%)
    all_to_all x4, blocking collectives, local(): incoming = lax.all_to_all(outgoing, FETCH_OVER, 0, 0, tiled=True)  79.8 us
    all_to_all x4, blocking collectives, local(): returned = lax.all_to_all(result, ROWS_OVER, 0, 0, tiled=True)  63.4 us
    pallas_call x4, Pallas kernels, pick(): pl.pallas_call(functools.partial(pick_kernel, layer, layers, owned, group...  6.9 us
    ppermute x1, starting transfers between devices, local(): partner = lax.ppermute(own, ROWS_OVER, partners)  5.08 us
    pallas_call x4, Pallas kernels, multiply(): pl.pallas_call(functools.partial(multiply_kernel, layer, last), out_shape...  4.45 us
    all_to_all x1, starting transfers between devices, local(): heavy = lax.all_to_all(heavy, FETCH_OVER, 0, 0, tiled=True)  3.83 us
  transfers between devices with their start and end apart: 3, of which 1 were waited for; matrix products, arithmetic and copies ran while one was open for 1% of the time, Pallas kernels for 2%

profile of v8, /device:TPU:0, one launch (start us, length us, event | category | flops | bytes accessed | tf_op | source)
XLA Modules:
  0.0 171.4 jit_solution(7692097219840190443)
XLA Ops:
  0.0 5.1 %collective-permute-start.1 = (bf16[128,8,128]{2,1,0:T(8,128)(2,1)}, bf16[128,8,128]{2,1,0:T(8,128)(2,1)S(1)}, u32[]{:S(2)}, u32[]{:S(2)}) collective-permute-start(bf16[128,8,128]{2,1,0:T(8,128)(2,1)} %bitcast.64), channel_id=1, source_target_pairs={{0,24},{4,28},{8,16},{12,20},{16,8},{20,12},{24,0},{28,4},{1,25},{... | collective-permute-start | bytes 786440 | tf_op jit(solution)/shard_map/ppermute | solution.py:225
  5.1 1.3 announce.1
  6.4 3.8 %all-to-all-start = ((s32[16,1,128]{2,1,0:T(1,128)}), s32[16,1,128]{2,1,0:T(1,128)S(1)}, u32[]{:S(2)}, u32[]{:S(2)}) async-start(s32[16,1,128]{2,1,0:T(1,128)} %announce.1), calls=%async_computation | async-start | bytes 16384 | tf_op jit(solution)/shard_map/all_to_all | solution.py:228
  10.3 1.6 collective-permute-start
  11.8 0.9 reshape.56
  12.7 1.9 %mask.1.refs_1_ = bf16[128,8,128]{2,1,0:T(8,128)(2,1)S(1)} custom-call(s32[512]{0:T(512)} %bitcast.55, bf16[128,8,128]{2,1,0:T(8,128)(2,1)} %bitcast.65), custom_call_target="tpu_custom_call" | custom-call | tf_op jit(solution)/shard_map/mask/pallas_call | solution.py:65
  14.6 1.4 collective-permute-done
  16.0 0.0 all-to-all-done
  16.0 0.0 collective-permute-done.1.refs_2_
  16.0 0.0 slice-start
  16.0 0.0 slice-start.1
  16.0 0.0 slice-start.2
  16.1 0.0 slice-start.3
  16.1 1.6 shard_map.64
  17.7 0.0 copy-start
  17.7 0.0 copy-start.1
  17.7 21.2 %all_to_all.45 = bf16[16,17,2,8,128]{4,3,2,1,0:T(8,128)(2,1)S(1)} all-to-all(bf16[16,17,2,8,128]{4,3,2,1,0:T(8,128)(2,1)S(1)} %shard_map.64), channel_id=1, replica_groups=mesh['half'=2,'pair'=2,'rest'=2,'gy'=4] {'pair','rest','gy'}, dimensions={0} | all-to-all | bytes 2228224 | tf_op jit(solution)/shard_map/all_to_all | solution.py:249
  38.8 0.0 slice-done
  38.9 0.0 slice-done.1
  38.9 0.0 slice-done.2
  38.9 0.0 slice-done.3
  38.9 0.0 copy-done
  38.9 0.0 copy-done.1
  38.9 0.0 copy-start.2
  38.9 1.1 shard_map.65
  40.0 17.3 %all_to_all.46 = bf16[8,16,2,8,128]{4,3,2,1,0:T(8,128)(2,1)S(1)} all-to-all(bf16[8,16,2,8,128]{4,3,2,1,0:T(8,128)(2,1)S(1)} %bitcast.34), channel_id=1, replica_groups=mesh['half'=2,'pair'=2,'rest'=2,'gy'=4] {'half','pair','rest'}, dimensions={0} | all-to-all | bytes 1048576 | tf_op jit(solution)/shard_map/all_to_all | solution.py:253
  57.3 0.0 copy-done.2
  57.3 1.8 %shard_map.66 = bf16[16,17,2,8,128]{4,3,2,1,0:T(8,128)(2,1)S(1)} custom-call(s32[1]{0:T(128)} %bitcast.where, s32[4096]{0:T(1024)S(1)} %bitcast.42, s32[16,4]{1,0:T(8,128)S(1)} %bitcast.46, s32[512]{0:T(512)S(1)} %bitcast.56, s32[512]{0:T(512)S(1)} %bitcast.60, bf16[128,2,8,128]{3,2,1,0:T(8,128)(2,1)S(1)} %bitcast.38), custom_call_target="tpu_custom_call" | custom-call | tf_op jit(solution)/shard_map/pallas_call | solution.py:125
  59.1 19.5 %all_to_all.47 = bf16[16,17,2,8,128]{4,3,2,1,0:T(8,128)(2,1)S(1)} all-to-all(bf16[16,17,2,8,128]{4,3,2,1,0:T(8,128)(2,1)S(1)} %shard_map.66), channel_id=1, replica_groups=mesh['half'=2,'pair'=2,'rest'=2,'gy'=4] {'pair','rest','gy'}, dimensions={0} | all-to-all | bytes 2228224 | tf_op jit(solution)/shard_map/all_to_all | solution.py:249
  78.7 1.1 shard_map.67
  79.8 17.2 %all_to_all.48 = bf16[8,16,2,8,128]{4,3,2,1,0:T(8,128)(2,1)S(1)} all-to-all(bf16[8,16,2,8,128]{4,3,2,1,0:T(8,128)(2,1)S(1)} %bitcast.35), channel_id=1, replica_groups=mesh['half'=2,'pair'=2,'rest'=2,'gy'=4] {'half','pair','rest'}, dimensions={0} | all-to-all | bytes 1048576 | tf_op jit(solution)/shard_map/all_to_all | solution.py:253
  97.0 1.8 %shard_map.68 = bf16[16,17,2,8,128]{4,3,2,1,0:T(8,128)(2,1)S(1)} custom-call(s32[1]{0:T(128)} %bitcast.where, s32[4096]{0:T(1024)S(1)} %bitcast.43, s32[16,4]{1,0:T(8,128)S(1)} %bitcast.47, s32[512]{0:T(512)S(1)} %bitcast.57, s32[512]{0:T(512)S(1)} %bitcast.61, bf16[128,2,8,128]{3,2,1,0:T(8,128)(2,1)S(1)} %bitcast.39), custom_call_target="tpu_custom_call" | custom-call | tf_op jit(solution)/shard_map/pallas_call | solution.py:125
  98.8 19.5 %all_to_all.49 = bf16[16,17,2,8,128]{4,3,2,1,0:T(8,128)(2,1)S(1)} all-to-all(bf16[16,17,2,8,128]{4,3,2,1,0:T(8,128)(2,1)S(1)} %shard_map.68), channel_id=1, replica_groups=mesh['half'=2,'pair'=2,'rest'=2,'gy'=4] {'pair','rest','gy'}, dimensions={0} | all-to-all | bytes 2228224 | tf_op jit(solution)/shard_map/all_to_all | solution.py:249
  118.3 1.1 shard_map.69
  119.4 17.2 %all_to_all.50 = bf16[8,16,2,8,128]{4,3,2,1,0:T(8,128)(2,1)S(1)} all-to-all(bf16[8,16,2,8,128]{4,3,2,1,0:T(8,128)(2,1)S(1)} %bitcast.36), channel_id=1, replica_groups=mesh['half'=2,'pair'=2,'rest'=2,'gy'=4] {'half','pair','rest'}, dimensions={0} | all-to-all | bytes 1048576 | tf_op jit(solution)/shard_map/all_to_all | solution.py:253
  136.6 1.8 %shard_map.70 = bf16[16,17,2,8,128]{4,3,2,1,0:T(8,128)(2,1)S(1)} custom-call(s32[1]{0:T(128)} %bitcast.where, s32[4096]{0:T(1024)S(1)} %bitcast.44, s32[16,4]{1,0:T(8,128)S(1)} %bitcast.48, s32[512]{0:T(512)S(1)} %bitcast.58, s32[512]{0:T(512)S(1)} %bitcast.62, bf16[128,2,8,128]{3,2,1,0:T(8,128)(2,1)S(1)} %bitcast.37), custom_call_target="tpu_custom_call" | custom-call | tf_op jit(solution)/shard_map/pallas_call | solution.py:125
  138.4 19.5 %all_to_all.51 = bf16[16,17,2,8,128]{4,3,2,1,0:T(8,128)(2,1)S(1)} all-to-all(bf16[16,17,2,8,128]{4,3,2,1,0:T(8,128)(2,1)S(1)} %shard_map.70), channel_id=1, replica_groups=mesh['half'=2,'pair'=2,'rest'=2,'gy'=4] {'pair','rest','gy'}, dimensions={0} | all-to-all | bytes 2228224 | tf_op jit(solution)/shard_map/all_to_all | solution.py:249
  157.9 1.1 shard_map.71
  159.0 11.6 %all_to_all.52 = bf16[8,16,8,128]{3,2,1,0:T(8,128)(2,1)S(1)} all-to-all(bf16[8,16,8,128]{3,2,1,0:T(8,128)(2,1)S(1)} %bitcast.40), channel_id=1, replica_groups=mesh['half'=2,'pair'=2,'rest'=2,'gy'=4] {'half','pair','rest'}, dimensions={0} | all-to-all | bytes 524288 | tf_op jit(solution)/shard_map/all_to_all | solution.py:253
  170.7 0.7 copy.14
  (2 shorter events, 0.0 us)
Async XLA Ops:
  0.0 16.0 %collective-permute-start.1 = (bf16[128,8,128]{2,1,0:T(8,128)(2,1)}, bf16[128,8,128]{2,1,0:T(8,128)(2,1)S(1)}, u32[]{:S(2)}, u32[]{:S(2)}) collective-permute-start(bf16[128,8,128]{2,1,0:T(8,128)(2,1)} %bitcast.64), channel_id=1, source_target_pairs={{0,24},{4,28},{8,16},{12,20},{16,8},{20,12},{24,0},{28,4},{1,25},{... | collective-permute-start | bytes 786440 | tf_op jit(solution)/shard_map/ppermute | solution.py:225
  6.4 9.6 %all-to-all-start = ((s32[16,1,128]{2,1,0:T(1,128)}), s32[16,1,128]{2,1,0:T(1,128)S(1)}, u32[]{:S(2)}, u32[]{:S(2)}) async-start(s32[16,1,128]{2,1,0:T(1,128)} %announce.1), calls=%async_computation | async-start | bytes 16384 | tf_op jit(solution)/shard_map/all_to_all | solution.py:228
  10.3 5.8 %collective-permute-start = (s32[4,128]{1,0:T(4,128)}, s32[4,128]{1,0:T(4,128)S(1)}, u32[]{:S(2)}, u32[]{:S(2)}) collective-permute-start(s32[4,128]{1,0:T(4,128)} %bitcast.54), channel_id=1, source_target_pairs={{0,24},{4,28},{8,16},{12,20},{16,8},{20,12},{24,0},{28,4},{1,25},{... | collective-permute-start | bytes 6152 | tf_op jit(solution)/shard_map/ppermute | solution.py:231
  16.0 22.8 %slice-start = ((s8[16777216]{0:T(1024)(128)(4,1)}), s8[4194304]{0:T(1024)(128)(4,1)S(1)}, s32[]{:S(2)}) async-start(s8[16777216]{0:T(1024)(128)(4,1)} %bitcast.28), calls=%async_computation.9 | async-start | bytes 8388608
  16.0 22.8 %slice-start.1 = ((s8[16777216]{0:T(1024)(128)(4,1)}), s8[4194304]{0:T(1024)(128)(4,1)S(1)}, s32[]{:S(2)}) async-start(s8[16777216]{0:T(1024)(128)(4,1)} %bitcast.28), calls=%async_computation.10 | async-start | bytes 8388608
  16.0 22.8 %slice-start.2 = ((s8[16777216]{0:T(1024)(128)(4,1)}), s8[4194304]{0:T(1024)(128)(4,1)S(1)}, s32[]{:S(2)}) async-start(s8[16777216]{0:T(1024)(128)(4,1)} %bitcast.28), calls=%async_computation.11 | async-start | bytes 8388608
  16.1 22.8 %slice-start.3 = ((s8[16777216]{0:T(1024)(128)(4,1)}), s8[4194304]{0:T(1024)(128)(4,1)S(1)}, s32[]{:S(2)}) async-start(s8[16777216]{0:T(1024)(128)(4,1)} %bitcast.28), calls=%async_computation.12 | async-start | bytes 8388608
  17.7 21.2 %copy-start = (f32[4,1,16,128]{3,2,1,0:T(8,128)S(1)}, f32[4,1,16,128]{3,2,1,0:T(8,128)}, u32[]{:S(2)}) copy-start(f32[4,1,16,128]{3,2,1,0:T(8,128)} %bias_ref.7) | copy-start | bytes 98308
  17.7 21.2 %copy-start.1 = (s32[4,1,16]{2,1,0:T(1,128)S(1)}, s32[4,1,16]{2,1,0:T(1,128)}, u32[]{:S(2)}) copy-start(s32[4,1,16]{2,1,0:T(1,128)} %param.9) | copy-start | bytes 772
  38.9 18.5 %copy-start.2 = (s32[4,1,128]{2,1,0:T(1,128)S(1)}, s32[4,1,128]{2,1,0:T(1,128)}, u32[]{:S(2)}) copy-start(s32[4,1,128]{2,1,0:T(1,128)} %param.7) | copy-start | bytes 6148

commit v9 on v8

--- a/solution.py
+++ b/solution.py
@@ -73,10 +73,15 @@
     )(live, own)
 
 
-def pick_kernel(layer, layers, owned, groups, where, table, heavy, *refs):
+def pick_kernel(layer, owned, groups, where, heavy, *refs):
     half = where[0]
     batch = 8
-    *live_refs, out_ref, kept_ref = refs
+    *live_refs, table_any, out_ref, kept_ref, table, sem = refs
+    slots = table.shape[0] // 2
+    fetch = pltpu.make_async_copy(
+        table_any.at[pl.ds(2 * layer * slots, 2 * slots)], table, sem
+    )
+    fetch.start()
     blocks = kept_ref.shape[0]
 
     def mask(b, carry):
@@ -100,11 +105,11 @@
     lax.fori_loop(0, blocks // batch, mask, 0)
 
     across = out_ref.shape[0] // groups
-    slots = table.shape[0] // (2 * layers)
+    fetch.wait()
 
     def one_owner(owner, carry):
         for g in range(groups):
-            first = 2 * layer * slots + g * blocks + (half * across + owner) * owned
+            first = g * blocks + (half * across + owner) * owned
             spots = [table[first + k] for k in range(owned)]
             spots.append(table[first + slots + heavy[owner * groups + g, layer]])
             for k, spot in enumerate(spots):
@@ -118,23 +123,27 @@
     return pl.BlockSpec(shape, lambda i, *_: (0,) * len(shape))
 
 
-def pick(layer, layers, owned, groups, scalars, states, cost):
+def pick(layer, layers, owned, groups, scalars, states, table, cost):
     blocks, (rows, side) = states[0].shape[0], states[0].shape[-2:]
-    devices = scalars[2].shape[0]
+    devices = scalars[1].shape[0]
     shape = (devices, owned + 1, 2, rows, side)
     return pl.pallas_call(
-        functools.partial(pick_kernel, layer, layers, owned, groups),
+        functools.partial(pick_kernel, layer, owned, groups),
         out_shape=jax.ShapeDtypeStruct(shape, states[0].dtype),
         grid_spec=pltpu.PrefetchScalarGridSpec(
             num_scalar_prefetch=len(scalars),
             grid=(1,),
-            in_specs=[whole(state.shape) for state in states],
+            in_specs=[whole(state.shape) for state in states] + [pl.BlockSpec(memory_space=pl.ANY)],
             out_specs=whole(shape),
-            scratch_shapes=[pltpu.VMEM((blocks, 2, rows, side), states[0].dtype)],
+            scratch_shapes=[
+                pltpu.VMEM((blocks, 2, rows, side), states[0].dtype),
+                pltpu.SMEM((table.shape[0] // layers,), jnp.int32),
+                pltpu.SemaphoreType.DMA,
+            ],
         ),
         compiler_params=pltpu.CompilerParams(vmem_limit_bytes=6 << 20),
         cost_estimate=cost,
-    )(*scalars, *states)
+    )(*scalars, *states, table)
 
 
 def multiply_kernel(layer, last, where, counts, x_ref, w_ref, bias_ref, out_ref, acc_ref):
@@ -240,12 +249,12 @@
     for layer in range(layers):
         last = layer == layers - 1
         if layer == 0:
-            scalars, states = (where, table, heavy, live_partner), (own, partner)
+            scalars, states = (where, heavy, live_partner), (own, partner)
             cost = pl.CostEstimate(flops=10**11, transcendentals=0, bytes_accessed=64 << 20)
         else:
-            scalars, states = (where, table, heavy, live_own, live_partner), (state,)
+            scalars, states = (where, heavy, live_own, live_partner), (state,)
             cost = None
-        outgoing = pick(layer, layers, owned, groups, scalars, states, cost)
+        outgoing = pick(layer, layers, owned, groups, scalars, states, table, cost)
         incoming = lax.all_to_all(outgoing, FETCH_OVER, 0, 0, tiled=True)
         incoming = incoming.reshape(2 * rest, groups, owned + 1, 2, rows, side)
         result = multiply(layer, last, where, counts, incoming, weight_tiles, bias_terms)

time: 172 us -> 172 us (level)
  no operation moved by 1% of the time
where the time goes in v9:
time: 172 us; the launch traced here: 171 us
  blocking collectives  143 us (83%)
  Pallas kernels  14.3 us (8%)
  starting transfers between devices  10.5 us (6%)
    all_to_all x4, blocking collectives, local(): incoming = lax.all_to_all(outgoing, FETCH_OVER, 0, 0, tiled=True)  79.8 us
    all_to_all x4, blocking collectives, local(): returned = lax.all_to_all(result, ROWS_OVER, 0, 0, tiled=True)  63.4 us
    pallas_call x4, Pallas kernels, pick(): pl.pallas_call(functools.partial(pick_kernel, layer, owned, groups), out_...  6.63 us
    ppermute x1, starting transfers between devices, local(): partner = lax.ppermute(own, ROWS_OVER, partners)  5.08 us
    pallas_call x4, Pallas kernels, multiply(): pl.pallas_call(functools.partial(multiply_kernel, layer, last), out_shape...  4.45 us
    all_to_all x1, starting transfers between devices, local(): heavy = lax.all_to_all(heavy, FETCH_OVER, 0, 0, tiled=True)  3.83 us
  transfers between devices with their start and end apart: 3, of which 1 were waited for; matrix products, arithmetic and copies ran while one was open for 1% of the time, Pallas kernels for 2%

profile of v9, /device:TPU:0, one launch (start us, length us, event | category | flops | bytes accessed | tf_op | source)
XLA Modules:
  0.0 171.1 jit_solution(12986687572386441568)
XLA Ops:
  0.0 5.1 %collective-permute-start.1 = (bf16[128,8,128]{2,1,0:T(8,128)(2,1)}, bf16[128,8,128]{2,1,0:T(8,128)(2,1)S(1)}, u32[]{:S(2)}, u32[]{:S(2)}) collective-permute-start(bf16[128,8,128]{2,1,0:T(8,128)(2,1)} %bitcast.64), channel_id=1, source_target_pairs={{0,24},{4,28},{8,16},{12,20},{16,8},{20,12},{24,0},{28,4},{1,25},{... | collective-permute-start | bytes 786440 | tf_op jit(solution)/shard_map/ppermute | solution.py:234
  5.1 1.3 announce.1
  6.4 3.8 %all-to-all-start = ((s32[16,1,128]{2,1,0:T(1,128)}), s32[16,1,128]{2,1,0:T(1,128)S(1)}, u32[]{:S(2)}, u32[]{:S(2)}) async-start(s32[16,1,128]{2,1,0:T(1,128)} %announce.1), calls=%async_computation | async-start | bytes 16384 | tf_op jit(solution)/shard_map/all_to_all | solution.py:237
  10.3 1.6 collective-permute-start
  11.8 0.9 reshape.58
  12.7 1.9 %mask.1.refs_1_ = bf16[128,8,128]{2,1,0:T(8,128)(2,1)S(1)} custom-call(s32[512]{0:T(512)} %bitcast.55, bf16[128,8,128]{2,1,0:T(8,128)(2,1)} %bitcast.65), custom_call_target="tpu_custom_call" | custom-call | tf_op jit(solution)/shard_map/mask/pallas_call | solution.py:65
  14.6 1.4 collective-permute-done
  16.0 0.0 all-to-all-done
  16.0 0.0 collective-permute-done.1.refs_2_
  16.0 0.0 slice-start
  16.0 0.0 slice-start.1
  16.0 0.0 slice-start.2
  16.1 0.0 slice-start.3
  16.1 1.6 shard_map.64
  17.7 0.0 copy-start
  17.7 0.0 copy-start.1
  17.7 21.2 %all_to_all.45 = bf16[16,17,2,8,128]{4,3,2,1,0:T(8,128)(2,1)S(1)} all-to-all(bf16[16,17,2,8,128]{4,3,2,1,0:T(8,128)(2,1)S(1)} %shard_map.64), channel_id=1, replica_groups=mesh['half'=2,'pair'=2,'rest'=2,'gy'=4] {'pair','rest','gy'}, dimensions={0} | all-to-all | bytes 2228224 | tf_op jit(solution)/shard_map/all_to_all | solution.py:258
  38.9 0.0 slice-done
  38.9 0.0 slice-done.1
  38.9 0.0 slice-done.2
  38.9 0.0 slice-done.3
  38.9 0.0 copy-done
  38.9 0.0 copy-done.1
  38.9 0.0 copy-start.2
  38.9 1.1 shard_map.65
  40.1 17.3 %all_to_all.46 = bf16[8,16,2,8,128]{4,3,2,1,0:T(8,128)(2,1)S(1)} all-to-all(bf16[8,16,2,8,128]{4,3,2,1,0:T(8,128)(2,1)S(1)} %bitcast.34), channel_id=1, replica_groups=mesh['half'=2,'pair'=2,'rest'=2,'gy'=4] {'half','pair','rest'}, dimensions={0} | all-to-all | bytes 1048576 | tf_op jit(solution)/shard_map/all_to_all | solution.py:262
  57.4 0.0 copy-done.2
  57.4 1.7 shard_map.66
  59.1 19.5 %all_to_all.47 = bf16[16,17,2,8,128]{4,3,2,1,0:T(8,128)(2,1)S(1)} all-to-all(bf16[16,17,2,8,128]{4,3,2,1,0:T(8,128)(2,1)S(1)} %shard_map.66), channel_id=1, replica_groups=mesh['half'=2,'pair'=2,'rest'=2,'gy'=4] {'pair','rest','gy'}, dimensions={0} | all-to-all | bytes 2228224 | tf_op jit(solution)/shard_map/all_to_all | solution.py:258
  78.6 1.1 shard_map.67
  79.7 17.2 %all_to_all.48 = bf16[8,16,2,8,128]{4,3,2,1,0:T(8,128)(2,1)S(1)} all-to-all(bf16[8,16,2,8,128]{4,3,2,1,0:T(8,128)(2,1)S(1)} %bitcast.35), channel_id=1, replica_groups=mesh['half'=2,'pair'=2,'rest'=2,'gy'=4] {'half','pair','rest'}, dimensions={0} | all-to-all | bytes 1048576 | tf_op jit(solution)/shard_map/all_to_all | solution.py:262
  96.9 1.7 shard_map.68
  98.6 19.5 %all_to_all.49 = bf16[16,17,2,8,128]{4,3,2,1,0:T(8,128)(2,1)S(1)} all-to-all(bf16[16,17,2,8,128]{4,3,2,1,0:T(8,128)(2,1)S(1)} %shard_map.68), channel_id=1, replica_groups=mesh['half'=2,'pair'=2,'rest'=2,'gy'=4] {'pair','rest','gy'}, dimensions={0} | all-to-all | bytes 2228224 | tf_op jit(solution)/shard_map/all_to_all | solution.py:258
  118.1 1.1 shard_map.69
  119.2 17.2 %all_to_all.50 = bf16[8,16,2,8,128]{4,3,2,1,0:T(8,128)(2,1)S(1)} all-to-all(bf16[8,16,2,8,128]{4,3,2,1,0:T(8,128)(2,1)S(1)} %bitcast.36), channel_id=1, replica_groups=mesh['half'=2,'pair'=2,'rest'=2,'gy'=4] {'half','pair','rest'}, dimensions={0} | all-to-all | bytes 1048576 | tf_op jit(solution)/shard_map/all_to_all | solution.py:262
  136.4 1.7 shard_map.70
  138.1 19.5 %all_to_all.51 = bf16[16,17,2,8,128]{4,3,2,1,0:T(8,128)(2,1)S(1)} all-to-all(bf16[16,17,2,8,128]{4,3,2,1,0:T(8,128)(2,1)S(1)} %shard_map.70), channel_id=1, replica_groups=mesh['half'=2,'pair'=2,'rest'=2,'gy'=4] {'pair','rest','gy'}, dimensions={0} | all-to-all | bytes 2228224 | tf_op jit(solution)/shard_map/all_to_all | solution.py:258
  157.6 1.1 shard_map.71
  158.8 11.6 %all_to_all.52 = bf16[8,16,8,128]{3,2,1,0:T(8,128)(2,1)S(1)} all-to-all(bf16[8,16,8,128]{3,2,1,0:T(8,128)(2,1)S(1)} %bitcast.40), channel_id=1, replica_groups=mesh['half'=2,'pair'=2,'rest'=2,'gy'=4] {'half','pair','rest'}, dimensions={0} | all-to-all | bytes 524288 | tf_op jit(solution)/shard_map/all_to_all | solution.py:262
  170.4 0.7 copy.14
  (2 shorter events, 0.0 us)
Async XLA Ops:
  0.0 16.0 %collective-permute-start.1 = (bf16[128,8,128]{2,1,0:T(8,128)(2,1)}, bf16[128,8,128]{2,1,0:T(8,128)(2,1)S(1)}, u32[]{:S(2)}, u32[]{:S(2)}) collective-permute-start(bf16[128,8,128]{2,1,0:T(8,128)(2,1)} %bitcast.64), channel_id=1, source_target_pairs={{0,24},{4,28},{8,16},{12,20},{16,8},{20,12},{24,0},{28,4},{1,25},{... | collective-permute-start | bytes 786440 | tf_op jit(solution)/shard_map/ppermute | solution.py:234
  6.4 9.6 %all-to-all-start = ((s32[16,1,128]{2,1,0:T(1,128)}), s32[16,1,128]{2,1,0:T(1,128)S(1)}, u32[]{:S(2)}, u32[]{:S(2)}) async-start(s32[16,1,128]{2,1,0:T(1,128)} %announce.1), calls=%async_computation | async-start | bytes 16384 | tf_op jit(solution)/shard_map/all_to_all | solution.py:237
  10.3 5.8 %collective-permute-start = (s32[4,128]{1,0:T(4,128)}, s32[4,128]{1,0:T(4,128)S(1)}, u32[]{:S(2)}, u32[]{:S(2)}) collective-permute-start(s32[4,128]{1,0:T(4,128)} %bitcast.54), channel_id=1, source_target_pairs={{0,24},{4,28},{8,16},{12,20},{16,8},{20,12},{24,0},{28,4},{1,25},{... | collective-permute-start | bytes 6152 | tf_op jit(solution)/shard_map/ppermute | solution.py:240
  16.0 22.9 %slice-start = ((s8[16777216]{0:T(1024)(128)(4,1)}), s8[4194304]{0:T(1024)(128)(4,1)S(1)}, s32[]{:S(2)}) async-start(s8[16777216]{0:T(1024)(128)(4,1)} %bitcast.28), calls=%async_computation.9 | async-start | bytes 8388608
  16.0 22.9 %slice-start.1 = ((s8[16777216]{0:T(1024)(128)(4,1)}), s8[4194304]{0:T(1024)(128)(4,1)S(1)}, s32[]{:S(2)}) async-start(s8[16777216]{0:T(1024)(128)(4,1)} %bitcast.28), calls=%async_computation.10 | async-start | bytes 8388608
  16.0 22.8 %slice-start.2 = ((s8[16777216]{0:T(1024)(128)(4,1)}), s8[4194304]{0:T(1024)(128)(4,1)S(1)}, s32[]{:S(2)}) async-start(s8[16777216]{0:T(1024)(128)(4,1)} %bitcast.28), calls=%async_computation.11 | async-start | bytes 8388608
  16.1 22.8 %slice-start.3 = ((s8[16777216]{0:T(1024)(128)(4,1)}), s8[4194304]{0:T(1024)(128)(4,1)S(1)}, s32[]{:S(2)}) async-start(s8[16777216]{0:T(1024)(128)(4,1)} %bitcast.28), calls=%async_computation.12 | async-start | bytes 8388608
  17.7 21.2 %copy-start = (f32[4,1,16,128]{3,2,1,0:T(8,128)S(1)}, f32[4,1,16,128]{3,2,1,0:T(8,128)}, u32[]{:S(2)}) copy-start(f32[4,1,16,128]{3,2,1,0:T(8,128)} %bias_ref.7) | copy-start | bytes 98308
  17.7 21.2 %copy-start.1 = (s32[4,1,16]{2,1,0:T(1,128)S(1)}, s32[4,1,16]{2,1,0:T(1,128)}, u32[]{:S(2)}) copy-start(s32[4,1,16]{2,1,0:T(1,128)} %param.9) | copy-start | bytes 772
  38.9 18.5 %copy-start.2 = (s32[4,1,128]{2,1,0:T(1,128)S(1)}, s32[4,1,128]{2,1,0:T(1,128)}, u32[]{:S(2)}) copy-start(s32[4,1,128]{2,1,0:T(1,128)} %param.7) | copy-start | bytes 6148

commit v10 on v9

--- a/solution.py
+++ b/solution.py
@@ -13,7 +13,7 @@
 
 
 def masked(alive, tile):
-    return jnp.where(alive > 0, tile, jnp.zeros_like(tile))
+    return tile * jnp.full(tile.shape, alive.astype(jnp.float32)).astype(tile.dtype)
 
 
 def announce_kernel(layers, groups, counts, heavy_ref):
@@ -47,7 +47,7 @@
 
 
 def mask_kernel(live, rows_ref, own_ref):
-    batch = 8
+    batch = 32
 
     def mask(b, carry):
         first = b * batch
@@ -75,7 +75,7 @@
 
 def pick_kernel(layer, owned, groups, where, heavy, *refs):
     half = where[0]
-    batch = 8
+    batch = 32
     *live_refs, table_any, out_ref, kept_ref, table, sem = refs
     slots = table.shape[0] // 2
     fetch = pltpu.make_async_copy(

time: 172 us -> 172 us (level)
  no operation moved by 1% of the time
where the time goes in v10:
time: 172 us; the launch traced here: 171 us
  blocking collectives  143 us (83%)
  Pallas kernels  14.2 us (8%)
  starting transfers between devices  10.5 us (6%)
    all_to_all x4, blocking collectives, local(): incoming = lax.all_to_all(outgoing, FETCH_OVER, 0, 0, tiled=True)  79.8 us
    all_to_all x4, blocking collectives, local(): returned = lax.all_to_all(result, ROWS_OVER, 0, 0, tiled=True)  63.4 us
    pallas_call x4, Pallas kernels, pick(): pl.pallas_call(functools.partial(pick_kernel, layer, owned, groups), out_...  6.63 us
    ppermute x1, starting transfers between devices, local(): partner = lax.ppermute(own, ROWS_OVER, partners)  5.08 us
    pallas_call x4, Pallas kernels, multiply(): pl.pallas_call(functools.partial(multiply_kernel, layer, last), out_shape...  4.45 us
    all_to_all x1, starting transfers between devices, local(): heavy = lax.all_to_all(heavy, FETCH_OVER, 0, 0, tiled=True)  3.83 us
  transfers between devices with their start and end apart: 3, of which 1 were waited for; matrix products, arithmetic and copies ran while one was open for 1% of the time, Pallas kernels for 2%

profile of v10, /device:TPU:0, one launch (start us, length us, event | category | flops | bytes accessed | tf_op | source)
XLA Modules:
  0.0 171.1 jit_solution(7914686362702753208)
XLA Ops:
  0.0 5.1 %collective-permute-start.1 = (bf16[128,8,128]{2,1,0:T(8,128)(2,1)}, bf16[128,8,128]{2,1,0:T(8,128)(2,1)S(1)}, u32[]{:S(2)}, u32[]{:S(2)}) collective-permute-start(bf16[128,8,128]{2,1,0:T(8,128)(2,1)} %bitcast.64), channel_id=1, source_target_pairs={{0,24},{4,28},{8,16},{12,20},{16,8},{20,12},{24,0},{28,4},{1,25},{... | collective-permute-start | bytes 786440 | tf_op jit(solution)/shard_map/ppermute | solution.py:234
  5.1 1.3 announce.1
  6.4 3.8 %all-to-all-start = ((s32[16,1,128]{2,1,0:T(1,128)}), s32[16,1,128]{2,1,0:T(1,128)S(1)}, u32[]{:S(2)}, u32[]{:S(2)}) async-start(s32[16,1,128]{2,1,0:T(1,128)} %announce.1), calls=%async_computation | async-start | bytes 16384 | tf_op jit(solution)/shard_map/all_to_all | solution.py:237
  10.3 1.6 collective-permute-start
  11.8 0.9 reshape.58
  12.7 1.8 %mask.1.refs_1_ = bf16[128,8,128]{2,1,0:T(8,128)(2,1)S(1)} custom-call(s32[512]{0:T(512)} %bitcast.55, bf16[128,8,128]{2,1,0:T(8,128)(2,1)} %bitcast.65), custom_call_target="tpu_custom_call" | custom-call | tf_op jit(solution)/shard_map/mask/pallas_call | solution.py:65
  14.5 1.5 collective-permute-done
  16.0 0.0 all-to-all-done
  16.0 0.0 collective-permute-done.1.refs_2_
  16.0 0.0 slice-start
  16.0 0.0 slice-start.1
  16.0 0.0 slice-start.2
  16.1 0.0 slice-start.3
  16.1 1.6 shard_map.64
  17.7 0.0 copy-start
  17.7 0.0 copy-start.1
  17.7 21.2 %all_to_all.45 = bf16[16,17,2,8,128]{4,3,2,1,0:T(8,128)(2,1)S(1)} all-to-all(bf16[16,17,2,8,128]{4,3,2,1,0:T(8,128)(2,1)S(1)} %shard_map.64), channel_id=1, replica_groups=mesh['half'=2,'pair'=2,'rest'=2,'gy'=4] {'pair','rest','gy'}, dimensions={0} | all-to-all | bytes 2228224 | tf_op jit(solution)/shard_map/all_to_all | solution.py:258
  38.9 0.0 slice-done
  38.9 0.0 slice-done.1
  38.9 0.0 slice-done.2
  38.9 0.0 slice-done.3
  38.9 0.0 copy-done
  38.9 0.0 copy-done.1
  38.9 0.0 copy-start.2
  38.9 1.1 shard_map.65
  40.1 17.3 %all_to_all.46 = bf16[8,16,2,8,128]{4,3,2,1,0:T(8,128)(2,1)S(1)} all-to-all(bf16[8,16,2,8,128]{4,3,2,1,0:T(8,128)(2,1)S(1)} %bitcast.34), channel_id=1, replica_groups=mesh['half'=2,'pair'=2,'rest'=2,'gy'=4] {'half','pair','rest'}, dimensions={0} | all-to-all | bytes 1048576 | tf_op jit(solution)/shard_map/all_to_all | solution.py:262
  57.4 0.0 copy-done.2
  57.4 1.7 shard_map.66
  59.1 19.5 %all_to_all.47 = bf16[16,17,2,8,128]{4,3,2,1,0:T(8,128)(2,1)S(1)} all-to-all(bf16[16,17,2,8,128]{4,3,2,1,0:T(8,128)(2,1)S(1)} %shard_map.66), channel_id=1, replica_groups=mesh['half'=2,'pair'=2,'rest'=2,'gy'=4] {'pair','rest','gy'}, dimensions={0} | all-to-all | bytes 2228224 | tf_op jit(solution)/shard_map/all_to_all | solution.py:258
  78.6 1.1 shard_map.67
  79.7 17.2 %all_to_all.48 = bf16[8,16,2,8,128]{4,3,2,1,0:T(8,128)(2,1)S(1)} all-to-all(bf16[8,16,2,8,128]{4,3,2,1,0:T(8,128)(2,1)S(1)} %bitcast.35), channel_id=1, replica_groups=mesh['half'=2,'pair'=2,'rest'=2,'gy'=4] {'half','pair','rest'}, dimensions={0} | all-to-all | bytes 1048576 | tf_op jit(solution)/shard_map/all_to_all | solution.py:262
  96.9 1.7 shard_map.68
  98.6 19.5 %all_to_all.49 = bf16[16,17,2,8,128]{4,3,2,1,0:T(8,128)(2,1)S(1)} all-to-all(bf16[16,17,2,8,128]{4,3,2,1,0:T(8,128)(2,1)S(1)} %shard_map.68), channel_id=1, replica_groups=mesh['half'=2,'pair'=2,'rest'=2,'gy'=4] {'pair','rest','gy'}, dimensions={0} | all-to-all | bytes 2228224 | tf_op jit(solution)/shard_map/all_to_all | solution.py:258
  118.1 1.1 shard_map.69
  119.2 17.2 %all_to_all.50 = bf16[8,16,2,8,128]{4,3,2,1,0:T(8,128)(2,1)S(1)} all-to-all(bf16[8,16,2,8,128]{4,3,2,1,0:T(8,128)(2,1)S(1)} %bitcast.36), channel_id=1, replica_groups=mesh['half'=2,'pair'=2,'rest'=2,'gy'=4] {'half','pair','rest'}, dimensions={0} | all-to-all | bytes 1048576 | tf_op jit(solution)/shard_map/all_to_all | solution.py:262
  136.4 1.7 shard_map.70
  138.1 19.5 %all_to_all.51 = bf16[16,17,2,8,128]{4,3,2,1,0:T(8,128)(2,1)S(1)} all-to-all(bf16[16,17,2,8,128]{4,3,2,1,0:T(8,128)(2,1)S(1)} %shard_map.70), channel_id=1, replica_groups=mesh['half'=2,'pair'=2,'rest'=2,'gy'=4] {'pair','rest','gy'}, dimensions={0} | all-to-all | bytes 2228224 | tf_op jit(solution)/shard_map/all_to_all | solution.py:258
  157.6 1.1 shard_map.71
  158.8 11.6 %all_to_all.52 = bf16[8,16,8,128]{3,2,1,0:T(8,128)(2,1)S(1)} all-to-all(bf16[8,16,8,128]{3,2,1,0:T(8,128)(2,1)S(1)} %bitcast.40), channel_id=1, replica_groups=mesh['half'=2,'pair'=2,'rest'=2,'gy'=4] {'half','pair','rest'}, dimensions={0} | all-to-all | bytes 524288 | tf_op jit(solution)/shard_map/all_to_all | solution.py:262
  170.4 0.7 copy.14
  (2 shorter events, 0.0 us)
Async XLA Ops:
  0.0 16.0 %collective-permute-start.1 = (bf16[128,8,128]{2,1,0:T(8,128)(2,1)}, bf16[128,8,128]{2,1,0:T(8,128)(2,1)S(1)}, u32[]{:S(2)}, u32[]{:S(2)}) collective-permute-start(bf16[128,8,128]{2,1,0:T(8,128)(2,1)} %bitcast.64), channel_id=1, source_target_pairs={{0,24},{4,28},{8,16},{12,20},{16,8},{20,12},{24,0},{28,4},{1,25},{... | collective-permute-start | bytes 786440 | tf_op jit(solution)/shard_map/ppermute | solution.py:234
  6.4 9.6 %all-to-all-start = ((s32[16,1,128]{2,1,0:T(1,128)}), s32[16,1,128]{2,1,0:T(1,128)S(1)}, u32[]{:S(2)}, u32[]{:S(2)}) async-start(s32[16,1,128]{2,1,0:T(1,128)} %announce.1), calls=%async_computation | async-start | bytes 16384 | tf_op jit(solution)/shard_map/all_to_all | solution.py:237
  10.3 5.8 %collective-permute-start = (s32[4,128]{1,0:T(4,128)}, s32[4,128]{1,0:T(4,128)S(1)}, u32[]{:S(2)}, u32[]{:S(2)}) collective-permute-start(s32[4,128]{1,0:T(4,128)} %bitcast.54), channel_id=1, source_target_pairs={{0,24},{4,28},{8,16},{12,20},{16,8},{20,12},{24,0},{28,4},{1,25},{... | collective-permute-start | bytes 6152 | tf_op jit(solution)/shard_map/ppermute | solution.py:240
  16.0 22.9 %slice-start = ((s8[16777216]{0:T(1024)(128)(4,1)}), s8[4194304]{0:T(1024)(128)(4,1)S(1)}, s32[]{:S(2)}) async-start(s8[16777216]{0:T(1024)(128)(4,1)} %bitcast.28), calls=%async_computation.9 | async-start | bytes 8388608
  16.0 22.9 %slice-start.1 = ((s8[16777216]{0:T(1024)(128)(4,1)}), s8[4194304]{0:T(1024)(128)(4,1)S(1)}, s32[]{:S(2)}) async-start(s8[16777216]{0:T(1024)(128)(4,1)} %bitcast.28), calls=%async_computation.10 | async-start | bytes 8388608
  16.0 22.8 %slice-start.2 = ((s8[16777216]{0:T(1024)(128)(4,1)}), s8[4194304]{0:T(1024)(128)(4,1)S(1)}, s32[]{:S(2)}) async-start(s8[16777216]{0:T(1024)(128)(4,1)} %bitcast.28), calls=%async_computation.11 | async-start | bytes 8388608
  16.1 22.8 %slice-start.3 = ((s8[16777216]{0:T(1024)(128)(4,1)}), s8[4194304]{0:T(1024)(128)(4,1)S(1)}, s32[]{:S(2)}) async-start(s8[16777216]{0:T(1024)(128)(4,1)} %bitcast.28), calls=%async_computation.12 | async-start | bytes 8388608
  17.7 21.2 %copy-start = (f32[4,1,16,128]{3,2,1,0:T(8,128)S(1)}, f32[4,1,16,128]{3,2,1,0:T(8,128)}, u32[]{:S(2)}) copy-start(f32[4,1,16,128]{3,2,1,0:T(8,128)} %bias_ref.7) | copy-start | bytes 98308
  17.7 21.2 %copy-start.1 = (s32[4,1,16]{2,1,0:T(1,128)S(1)}, s32[4,1,16]{2,1,0:T(1,128)}, u32[]{:S(2)}) copy-start(s32[4,1,16]{2,1,0:T(1,128)} %param.9) | copy-start | bytes 772
  38.9 18.5 %copy-start.2 = (s32[4,1,128]{2,1,0:T(1,128)S(1)}, s32[4,1,128]{2,1,0:T(1,128)}, u32[]{:S(2)}) copy-start(s32[4,1,128]{2,1,0:T(1,128)} %param.7) | copy-start | bytes 6148
